TPU v7x, 256 devices: a whole 4x4x8 slice. The times are simulated.
256 devices in a mesh: dom: 32 (over y_lo, z, core), repl: 8 (over y_hi, x).
Axes of the slice: x: 4, y: 4 (y_hi: 2, y_lo: 2; y = y_hi * 2 + y_lo), z: 8, core: 2. Of those that a mesh axis runs over, the one named last changes fastest.
Arguments:
- features: float32 [131072, 256], P(('dom', 'repl')), may hold values from -6 to 6
- weight: bfloat16 [256, 256], replicated, may hold values from -0.375 to 0.375
- bias_vector: float32 [256], replicated, may hold values from -0.5 to 0.5
- cotangent: bfloat16 [131072, 256], P(('dom', 'repl')), may hold values from -6 to 6
- near_tiles: bfloat16 [4096, 128, 128], P(('dom', 'repl')), may hold values from -0.1875 to 0.1875
- near_offsets: int32 [256, 33], P(('dom', 'repl')), may hold values from 0 to 16, as said below
- near_cols: int32 [256, 16], P(('dom', 'repl')), may hold values from 0 to 3, as said below
- far_tiles: bfloat16 [256, 32, 1, 128, 128], P(('dom', 'repl')), may hold values from -0.1875 to 0.1875
- far_rows: int32 [256, 32, 1], P(('dom', 'repl')), may hold values from -1 to 31, as said below
- far_cols: int32 [256, 32, 1], P(('dom', 'repl')), may hold values from 0 to 3
Outputs:
- hidden: bfloat16 [131072, 256], P(('dom', 'repl'))
- grad_features: float32 [131072, 256], P(('dom', 'repl'))
- weight_grad: float32 [256, 256], replicated
Inputs may be any that keep to these rules, and one draw needn't show every extreme that they name: `near_offsets`: each row is non-decreasing, begins with 0 and ends with 16. `near_cols`: within one tile row of one device the near tiles' columns differ and rise. `far_rows`: -1 marks an empty slot. A device's slots for the groups whose index of dom lies at most 2 steps from its own around the cycle are never empty.
All inputs are finite; a program needn't handle non-finite values.
Results may differ from a plain program's by a relative error of at most 0.0075.
Values may be sent and summed in bfloat16 or wider, within the bound.
No kernel may reach another device: no remote copies, remote signals or barrier semaphores. Data moves between devices by JAX's collectives and lax.ppermute only.
A program may use at most 128 MiB of HBM per device.

v0:
```python
import math

import jax
import jax.numpy as jnp
from jax import lax
from jax.sharding import PartitionSpec as P


def membership_flags(index, extent, dtype):
    return (index[..., None] == jnp.arange(extent, dtype=jnp.int32)).astype(dtype)


def slot_rows(offsets, slot_count):
    slots = jnp.arange(slot_count, dtype=jnp.int32)
    return jnp.sum((offsets[1:, None] <= slots[None, :]).astype(jnp.int32), axis=0)


def precise_total_sum(form, hot, values):
    return jnp.einsum(form, hot, values, precision=lax.Precision.HIGHEST)


def select(form, hot, values):
    return jnp.einsum(form, hot, values, preferred_element_type=jnp.float32).astype(jnp.bfloat16)


def tile_product(form, tiles, values):
    return jnp.einsum(form, tiles, values, preferred_element_type=jnp.float32)


def activation_grad(pre_values, upstream):
    sigma = jax.nn.sigmoid(pre_values)
    return (upstream.astype(jnp.float32) * sigma * (1.0 + pre_values * (1.0 - sigma))).astype(
        jnp.bfloat16
    )


def on_device(
    features,
    weight,
    bias_vector,
    cotangent,
    near_tiles,
    near_offsets,
    near_cols,
    far_tiles,
    far_rows,
    far_cols,
):
    rows_dev, feat_width = features.shape
    tile_size = near_tiles.shape[1]
    blocks_per_processor = rows_dev // tile_size
    dom_count = lax.axis_size("dom")
    repl_count = lax.axis_size("repl")
    blocks_dom = blocks_per_processor * repl_count
    near_count = near_tiles.shape[0]
    far_block = far_tiles[0]
    far_row_ids = far_rows[0]
    far_col_ids = far_cols[0]
    near_row_ids = slot_rows(near_offsets[0], near_count)
    nearby_column_index = near_cols[0]
    reduced = features.astype(jnp.bfloat16)
    local_block_list = reduced.reshape(blocks_per_processor, tile_size, feat_width)
    nearby_input_rows = select(
        "el,lxh->exh",
        membership_flags(nearby_column_index, blocks_per_processor, jnp.bfloat16),
        local_block_list,
    )
    near_prod = tile_product("qab,qbf->qaf", near_tiles, nearby_input_rows)
    partial_sum = precise_total_sum(
        "qr,qaf->raf", membership_flags(near_row_ids, blocks_dom, jnp.float32), near_prod
    )
    shard_rows = lax.all_gather(reduced, "dom", axis=0, tiled=True)
    range_count = shard_rows.shape[0] // rows_dev
    tiles = far_block
    row_ids = far_row_ids
    col_ids = far_col_ids
    source = shard_rows.reshape(range_count, blocks_per_processor, tile_size, feat_width)
    inputs = select(
        "kqc,kcbf->kqbf", membership_flags(col_ids, blocks_per_processor, jnp.bfloat16), source
    )
    far_prod = tile_product("kqab,kqbf->kqaf", tiles, inputs)
    partial_sum = partial_sum + precise_total_sum(
        "kqr,kqaf->raf", membership_flags(row_ids, blocks_dom, jnp.float32), far_prod
    )
    group_partial = partial_sum.reshape(blocks_dom * tile_size, feat_width)
    summed = lax.psum_scatter(group_partial, "repl", scatter_dimension=0, tiled=True).astype(
        jnp.bfloat16
    )
    pre_act = jnp.dot(summed, weight, preferred_element_type=jnp.float32) + bias_vector
    hidden = jax.nn.silu(pre_act).astype(jnp.bfloat16)
    grad_pre = activation_grad(pre_act, cotangent)
    weight_term = lax.dot_general(
        summed, grad_pre, (((0,), (0,)), ((), ())), preferred_element_type=jnp.float32
    )
    grad_rows = lax.dot_general(
        grad_pre, weight, (((1,), (1,)), ((), ())), preferred_element_type=jnp.float32
    ).astype(jnp.bfloat16)
    group_grad = lax.all_gather(grad_rows, "repl", axis=0, tiled=True)
    node_total = rows_dev * dom_count * repl_count
    weight_grad = lax.psum(weight_term, ("dom", "repl")) * (1.0 / math.sqrt(node_total))
    cluster_block_list = group_grad.reshape(blocks_dom, tile_size, feat_width)
    near_grads = select(
        "om,mgh->ogh", membership_flags(near_row_ids, blocks_dom, jnp.bfloat16), cluster_block_list
    )
    nearby_backward_pass = tile_product("ltp,ltk->lpk", near_tiles, near_grads)
    local_contribution = precise_total_sum(
        "ml,mrx->lrx",
        membership_flags(nearby_column_index, blocks_per_processor, jnp.float32),
        nearby_backward_pass,
    )
    row_count = rows_dev * lax.axis_size("dom")
    tiles = far_block
    row_ids = far_row_ids
    col_ids = far_col_ids
    far_grads = select(
        "kqr,rbf->kqbf", membership_flags(row_ids, blocks_dom, jnp.bfloat16), cluster_block_list
    )
    terms = tile_product("kqab,kqaf->kqbf", tiles, far_grads)
    placed = precise_total_sum(
        "kqc,kqbf->kcbf", membership_flags(col_ids, blocks_per_processor, jnp.float32), terms
    )
    far_grad = lax.psum_scatter(
        placed.reshape(row_count, feat_width).astype(jnp.bfloat16),
        "dom",
        scatter_dimension=0,
        tiled=True,
    ).astype(jnp.float32)
    grad_features = far_grad + local_contribution.reshape(rows_dev, feat_width)
    return (hidden, grad_features, weight_grad)


def solution(mesh):
    placed = (
        P(("dom", "repl"), None),
        P(),
        P(),
        P(("dom", "repl"), None),
        P(("dom", "repl"), None, None),
        P(("dom", "repl"), None),
        P(("dom", "repl"), None),
        P(("dom", "repl"), None, None, None, None),
        P(("dom", "repl"), None, None),
        P(("dom", "repl"), None, None),
    )
    return jax.shard_map(
        on_device,
        mesh=mesh,
        in_specs=placed,
        out_specs=(P(("dom", "repl"), None), P(("dom", "repl"), None), P()),
        check_vma=False,
    )
```

profile of v0, /device:TPU:2, one launch (start us, length us, event | category | flops | bytes accessed | tf_op | source)
XLA Modules:
  0.0 674.9 jit_solution(15560080894403100846)
XLA Ops:
  7.2 0.0 copy-start
  7.2 0.0 copy-start.2
  7.2 0.0 all-gather.3.cloned.1.call-start
  7.2 1.9 convert_element_type.53
  9.1 0.0 all-gather.3.cloned.1.call-update
  9.2 0.0 reduce-scatter.3.cloned.1.call-start
  9.2 1.5 convolution_convert_fusion.1
  10.7 0.0 copy-done.2
  10.7 1.9 convolution_bitcast_fusion.3
  12.6 0.0 copy-start.8
  12.6 2.3 copy.19
  14.9 0.0 copy-done.11
  14.9 0.1 slice_bitcast_fusion
  15.0 0.1 convert_reduce_fusion
  15.1 0.0 copy-done.8
  15.1 0.1 fusion.18
  15.2 3.6 fusion.28
  18.7 66.3 %all-gather.3.cloned.1.call-done = bf16[16384,256]{1,0:T(8,128)(2,1)} async-done(((bf16[512,256]{1,0:T(8,128)(2,1)}), bf16[16384,256]{1,0:T(8,128)(2,1)}) %all-gather.3.cloned.1.call-update) | async-done | bytes 8388624 | tf_op jit(solution)/shard_map/all_gather | solution.py:72
  85.0 11.8 %fusion = bf16[32,1,128,256]{3,1,2,0:T(2,128)(2,1)} fusion(bf16[32,4,128,256]{3,2,1,0:T(8,128)(2,1)} %bitcast.65, pred[32,4,1,1]{1,0,2,3:T(32,128)(4,1)S(1)} %get-tuple-element.6), kind=kOutput, calls=%fused_computation.1 | convolution fusion | flops 8388608 | bytes 10485888 | tf_op jit(solution)/shard_map/kqc,kcbf->kqbf/dot_general | solution.py:23
  96.8 8.6 %copy.31 = bf16[32,1,128,256]{2,3,0,1:T(8,128)(2,1)S(1)} copy(bf16[32,1,128,256]{3,1,2,0:T(2,128)(2,1)} %fusion) | data formatting | bytes 4194304 | tf_op jit(solution)/shard_map/kqc,kcbf->kqbf/dot_general | solution.py:23
  105.4 0.0 copy-done
  105.4 2.7 convolution_bitcast_fusion.1
  108.1 0.0 copy-start.6
  108.1 5.5 copy.20
  113.6 0.0 copy-done.6
  113.6 5.7 convolution_add_fusion
  119.3 4.4 copy.21
  123.7 0.0 copy-start.5
  123.7 0.0 copy-start.9
  123.7 0.0 copy-start.10
  123.7 0.0 reduce-scatter.3.cloned.1.call-update
  123.7 0.0 all-gather.5.cloned.1.call-start
  123.8 89.6 %reduce-scatter.3.cloned.1.call-done = f32[512,256]{1,0:T(8,128)} async-done(((f32[4096,256]{1,0:T(8,128)}), f32[512,256]{1,0:T(8,128)}) %reduce-scatter.3.cloned.1.call-update) | async-done | bytes 524304 | tf_op jit(solution)/shard_map/reduce_scatter | solution.py:86
  213.4 0.0 copy-done.5
  213.4 0.0 copy-done.9
  213.4 0.0 copy-done.10
  213.4 0.0 copy-start.4
  213.4 2.2 multiply_convert_fusion.1
  215.7 1.0 convolution_convert_fusion.2
  216.6 0.0 all-gather.5.cloned.1.call-update
  216.7 0.2 all-reduce.2.cloned.1.call-start
  216.9 0.0 copy-done.4
  216.9 1.0 fusion.14
  217.9 0.0 all-reduce.2.cloned.1.call-update
  217.9 0.0 reduce-scatter.5.cloned.1.call-start
  218.0 57.9 %all-gather.5.cloned.1.call-done = bf16[4096,256]{1,0:T(8,128)(2,1)} async-done(((bf16[512,256]{1,0:T(8,128)(2,1)}), bf16[4096,256]{1,0:T(8,128)(2,1)}) %all-gather.5.cloned.1.call-update) | async-done | bytes 2097168 | tf_op jit(solution)/shard_map/all_gather | solution.py:98
  275.8 2.9 convolution_convert_fusion
  278.8 3.7 convolution_bitcast_fusion
  282.5 5.6 copy.24
  288.1 8.7 %multiply_convert_fusion = bf16[32,4,128,256]{3,2,1,0:T(8,128)(2,1)} fusion(f32[32,128,256]{2,1,0:T(8,128)} %copy.24, f32[32,4]{1,0:T(8,128)S(1)} %get-tuple-element.5), kind=kLoop, calls=%fused_computation | loop fusion | flops 8388608 | bytes 12583424 | tf_op jit(solution)/shard_map/convert_element_type | solution.py:123
  296.8 0.0 reduce-scatter.5.cloned.1.call-update
  296.8 238.4 %all-reduce.2.cloned.1.call-done = f32[256,256]{1,0:T(8,128)} async-done(((f32[256,256]{1,0:T(8,128)}), f32[256,256]{1,0:T(8,128)}) %all-reduce.2.cloned.1.call-update) | async-done | bytes 262160 | tf_op jit(solution)/shard_map/psum | solution.py:100
  535.2 1.7 broadcast_multiply_fusion
  536.9 0.0 copy-done.1
  537.0 1.2 fusion.6
  538.2 0.0 copy-done.3
  538.2 0.5 convolution_bitcast_fusion.2
  538.7 0.0 copy-start.7
  538.7 2.0 copy.27
  540.8 0.0 copy-done.7
  540.8 2.4 fusion.33
  543.2 0.1 copy.28
  543.3 123.3 %reduce-scatter.5.cloned.1.call-done = bf16[512,256]{1,0:T(8,128)(2,1)} async-done(((bf16[16384,256]{1,0:T(8,128)(2,1)}), bf16[512,256]{1,0:T(8,128)(2,1)}) %reduce-scatter.5.cloned.1.call-update) | async-done | bytes 262160 | tf_op jit(solution)/shard_map/reduce_scatter | solution.py:122
  666.6 1.8 bitcast_add_fusion
  (3 shorter events, 0.0 us)
Async XLA Ops:
  7.2 98.3 %copy-start = (bf16[1,32,1,128,128]{4,3,2,1,0:T(8,128)(2,1)S(1)}, bf16[1,32,1,128,128]{4,3,2,1,0:T(8,128)(2,1)}, u32[]{:S(2)}) copy-start(bf16[1,32,1,128,128]{4,3,2,1,0:T(8,128)(2,1)} %param.17) | copy-start | bytes 3145732
  7.2 3.5 copy-start.2
  7.2 77.8 %all-gather.3.cloned.1.call-start = ((), (), s32[]{:S(2)}) async-start(), calls=%async_computation.2 | async-start | bytes 8650752 | tf_op jit(solution)/shard_map/all_gather | solution.py:72
  9.2 204.3 %reduce-scatter.3.cloned.1.call-start = ((), (), s32[]{:S(2)}) async-start(), calls=%async_computation.3 | async-start | bytes 4718592 | tf_op jit(solution)/shard_map/reduce_scatter | solution.py:86
  12.6 2.3 copy-start.11
  12.6 2.5 copy-start.8
  108.1 5.5 copy-start.6
  123.7 89.7 %copy-start.5 = (bf16[256,256]{1,0:T(8,128)(2,1)S(1)}, bf16[256,256]{1,0:T(8,128)(2,1)}, u32[]{:S(2)}) copy-start(bf16[256,256]{1,0:T(8,128)(2,1)} %param.11) | copy-start | bytes 393220
  123.7 89.7 %copy-start.9 = (bf16[512,256]{1,0:T(8,128)(2,1)S(1)}, bf16[512,256]{1,0:T(8,128)(2,1)}, u32[]{:S(2)}) copy-start(bf16[512,256]{1,0:T(8,128)(2,1)} %param.13) | copy-start | bytes 786436
  123.7 89.7 %copy-start.10 = (f32[256]{0:T(256)S(1)}, f32[256]{0:T(256)}, u32[]{:S(2)}) copy-start(f32[256]{0:T(256)} %param.12) | copy-start | bytes 3076
  123.7 152.1 %all-gather.5.cloned.1.call-start = ((), (), s32[]{:S(2)}) async-start(), calls=%async_computation.4 | async-start | bytes 2359296 | tf_op jit(solution)/shard_map/all_gather | solution.py:98
  213.4 3.5 copy-start.4
  216.7 318.5 %all-reduce.2.cloned.1.call-start = ((), (), s32[]{:S(2)}) async-start(), calls=%async_computation.6 | async-start | bytes 524288 | tf_op jit(solution)/shard_map/psum | solution.py:100
  217.9 448.7 %reduce-scatter.5.cloned.1.call-start = ((), (), s32[]{:S(2)}) async-start(), calls=%async_computation.5 | async-start | bytes 8650752 | tf_op jit(solution)/shard_map/reduce_scatter | solution.py:122
  296.8 240.1 %copy-start.1 = (bf16[4096,256]{1,0:T(8,128)(2,1)S(1)}, bf16[4096,256]{1,0:T(8,128)(2,1)}, u32[]{:S(2)}) copy-start(bf16[4096,256]{1,0:T(8,128)(2,1)} %all-gather.5.cloned.1.call-done) | copy-start | bytes 6291460
  535.2 3.0 copy-start.3
  538.7 2.0 copy-start.7
Sparse Core Ops, SparseCore 0:
  10.4 74.5 all-gather.2
  123.9 89.5 reduce-scatter.2
  216.8 59.0 all-gather.4
  281.7 253.4 all-reduce.1
  537.6 128.9 reduce-scatter.4
where the time goes:
time: 676 us; the launch traced here: 675 us
  waiting for transfers between devices  576 us (85%)
  matrix products  42.2 us (6%)
  local copies, waits for them, and re-layouts  28.6 us (4%)
  other arithmetic  14.4 us (2%)
  between operations  13.9 us (2%)
    psum x1, waiting for transfers between devices, on_device(): lax.psum(weight_term, ('dom', 'repl')) * (1.0 / math.sqrt(node_total))  238 us
    reduce_scatter x1, waiting for transfers between devices, on_device(): lax.psum_scatter(placed.reshape(row_count, feat_width).astype(jnp.bfloat1...  123 us
    reduce_scatter x1, waiting for transfers between devices, on_device(): lax.psum_scatter(group_partial, 'repl', scatter_dimension=0, tiled=True)  89.6 us
    all_gather x1, waiting for transfers between devices, on_device(): shard_rows = lax.all_gather(reduced, 'dom', axis=0, tiled=True)  66.3 us
    all_gather x1, waiting for transfers between devices, on_device(): group_grad = lax.all_gather(grad_rows, 'repl', axis=0, tiled=True)  57.9 us
    dot_general x4, matrix products, select(): jnp.einsum(form, hot, values, preferred_element_type=jnp.float32)  17.5 us
    dot_general x4, local copies, waits for them, and re-layouts, tile_product(): return jnp.einsum(form, tiles, values, preferred_element_type=jnp.float32)  15.4 us
  transfers between devices with their start and end apart: 5, of which 5 were waited for; matrix products, arithmetic and copies ran while one was open for 6% of the time, Pallas kernels for 0%

commit v1 on v0

v1 whole, which is shorter than its diff:
```python
import math

import jax
import jax.numpy as jnp
from jax import lax
from jax.experimental import pallas as pl
from jax.experimental.pallas import tpu as pltpu
from jax.sharding import PartitionSpec as P

BF16 = jnp.bfloat16
F32 = jnp.float32
STEP = 8


def slot_rows(offsets, slot_count):
    slots = jnp.arange(slot_count, dtype=jnp.int32)
    return jnp.sum((offsets[1:, None] <= slots[None, :]).astype(jnp.int32), axis=0)


def smem():
    return pl.BlockSpec(memory_space=pltpu.SMEM)


def whole(shape):
    return pl.BlockSpec(shape, lambda i: (0,) * len(shape))


def stepped(shape):
    return pl.BlockSpec(shape, lambda i: (i,) + (0,) * (len(shape) - 1))


def params(mib=40):
    return pltpu.CompilerParams(
        dimension_semantics=("arbitrary",), vmem_limit_bytes=mib * 1024 * 1024
    )


def transposed_dot(left, right):
    return lax.dot_general(left, right, (((0,), (0,)), ((), ())), preferred_element_type=F32)


def pick_blocks(wanted, features, dom_count, tile):
    rows, width = features.shape

    def kernel(wanted_ref, feat_ref, out_ref, red_ref):
        step = pl.program_id(0)

        @pl.when(step == 0)
        def _():
            red_ref[...] = feat_ref[...].astype(BF16)

        for j in range(STEP):
            at = pl.multiple_of(wanted_ref[step * STEP + j] * tile, tile)
            out_ref[j] = red_ref[pl.ds(at, tile), :]

    return pl.pallas_call(
        kernel,
        grid=(dom_count // STEP,),
        in_specs=[smem(), whole((rows, width))],
        out_specs=[stepped((STEP, tile, width)), whole((rows, width))],
        out_shape=[
            jax.ShapeDtypeStruct((dom_count, tile, width), BF16),
            jax.ShapeDtypeStruct((rows, width), BF16),
        ],
        compiler_params=params(),
        name="pick_blocks",
    )(wanted, features)


def aggregate(far_rows, near_rows, near_cols, arrived, far_tiles, near_tiles, reduced, blocks_dom):
    dom_count, tile, width = arrived.shape
    near_count = near_tiles.shape[0]
    steps = dom_count // STEP

    def kernel(frow_ref, nrow_ref, ncol_ref, in_ref, far_ref, near_ref, red_ref, out_ref, acc_ref):
        step = pl.program_id(0)

        def add(row, value):
            at = pl.ds(pl.multiple_of(row * tile, tile), tile)
            acc_ref[at, :] += value

        @pl.when(step == 0)
        def _():
            acc_ref[...] = jnp.zeros_like(acc_ref)
            for q in range(near_count):
                src = pl.ds(pl.multiple_of(ncol_ref[q] * tile, tile), tile)
                add(
                    nrow_ref[q],
                    jnp.dot(near_ref[q], red_ref[src, :], preferred_element_type=F32),
                )

        for j in range(STEP):
            row = frow_ref[step * STEP + j]
            row = jnp.where(row < 0, blocks_dom, row)
            add(row, jnp.dot(far_ref[j], in_ref[j], preferred_element_type=F32))

        @pl.when(step == steps - 1)
        def _():
            out_ref[...] = acc_ref[: blocks_dom * tile, :].astype(BF16)

    return pl.pallas_call(
        kernel,
        grid=(steps,),
        in_specs=[
            smem(),
            smem(),
            smem(),
            stepped((STEP, tile, width)),
            stepped((STEP, tile, tile)),
            whole((near_count, tile, tile)),
            whole(reduced.shape),
        ],
        out_specs=whole((blocks_dom * tile, width)),
        out_shape=jax.ShapeDtypeStruct((blocks_dom * tile, width), BF16),
        scratch_shapes=[pltpu.VMEM(((blocks_dom + 1) * tile, width), F32)],
        compiler_params=params(),
        name="aggregate",
    )(far_rows, near_rows, near_cols, arrived, far_tiles, near_tiles, reduced)


def dense_stage(parts, weight, bias, cotangent):
    peers, rows, width = parts.shape
    chunk = 256

    def kernel(parts_ref, w_ref, b_ref, ct_ref, hid_ref, grads_ref, wt_ref):
        step = pl.program_id(0)
        total = parts_ref[0].astype(F32)
        for j in range(1, peers):
            total = total + parts_ref[j].astype(F32)
        summed = total.astype(BF16)
        w = w_ref[...]
        pre = jnp.dot(summed, w, preferred_element_type=F32) + b_ref[...]
        sigma = jax.nn.sigmoid(pre)
        hid_ref[...] = (pre * sigma).astype(BF16)
        grad_pre = (ct_ref[...].astype(F32) * sigma * (1.0 + pre * (1.0 - sigma))).astype(BF16)
        grad_rows = lax.dot_general(
            grad_pre, w, (((1,), (1,)), ((), ())), preferred_element_type=F32
        ).astype(BF16)
        for j in range(peers):
            grads_ref[j] = grad_rows
        term = transposed_dot(summed, grad_pre)

        @pl.when(step == 0)
        def _():
            wt_ref[...] = term

        @pl.when(step != 0)
        def _():
            wt_ref[...] += term

    return pl.pallas_call(
        kernel,
        grid=(rows // chunk,),
        in_specs=[
            pl.BlockSpec((peers, chunk, width), lambda i: (0, i, 0)),
            whole(weight.shape),
            whole((1, width)),
            stepped((chunk, width)),
        ],
        out_specs=[
            stepped((chunk, width)),
            pl.BlockSpec((peers, chunk, width), lambda i: (0, i, 0)),
            whole((width, width)),
        ],
        out_shape=[
            jax.ShapeDtypeStruct((rows, width), BF16),
            jax.ShapeDtypeStruct((peers, rows, width), BF16),
            jax.ShapeDtypeStruct((width, width), F32),
        ],
        compiler_params=params(),
        name="dense_stage",
    )(parts, weight, bias, cotangent)


def far_terms(far_rows, group_grad, far_tiles, tile):
    dom_count = far_tiles.shape[0]
    width = group_grad.shape[1]

    def kernel(frow_ref, grad_ref, far_ref, out_ref):
        step = pl.program_id(0)
        for j in range(STEP):
            row = frow_ref[step * STEP + j]
            at = pl.ds(pl.multiple_of(jnp.maximum(row, 0) * tile, tile), tile)
            term = transposed_dot(far_ref[j], grad_ref[at, :])
            out_ref[j] = jnp.where(row >= 0, term, 0.0).astype(BF16)

    return pl.pallas_call(
        kernel,
        grid=(dom_count // STEP,),
        in_specs=[smem(), whole(group_grad.shape), stepped((STEP, tile, tile))],
        out_specs=stepped((STEP, tile, width)),
        out_shape=jax.ShapeDtypeStruct((dom_count, tile, width), BF16),
        compiler_params=params(),
        name="far_terms",
    )(far_rows, group_grad, far_tiles)


def near_terms(near_rows, near_cols, group_grad, near_tiles, rows_dev):
    near_count, tile, _ = near_tiles.shape
    width = group_grad.shape[1]

    def kernel(nrow_ref, ncol_ref, grad_ref, near_ref, out_ref):
        out_ref[...] = jnp.zeros_like(out_ref)
        for q in range(near_count):
            src = pl.ds(pl.multiple_of(nrow_ref[q] * tile, tile), tile)
            dst = pl.ds(pl.multiple_of(ncol_ref[q] * tile, tile), tile)
            out_ref[dst, :] += transposed_dot(near_ref[q], grad_ref[src, :])

    return pl.pallas_call(
        kernel,
        grid=(1,),
        in_specs=[smem(), smem(), whole(group_grad.shape), whole(near_tiles.shape)],
        out_specs=whole((rows_dev, width)),
        out_shape=jax.ShapeDtypeStruct((rows_dev, width), F32),
        compiler_params=params(),
        name="near_terms",
    )(near_rows, near_cols, group_grad, near_tiles)


def place_terms(wanted, arrived, local):
    dom_count, tile, width = arrived.shape

    def kernel(wanted_ref, in_ref, local_ref, out_ref):
        step = pl.program_id(0)

        @pl.when(step == 0)
        def _():
            out_ref[...] = local_ref[...]

        for j in range(STEP):
            at = pl.ds(pl.multiple_of(wanted_ref[step * STEP + j] * tile, tile), tile)
            out_ref[at, :] += in_ref[j].astype(F32)

    return pl.pallas_call(
        kernel,
        grid=(dom_count // STEP,),
        in_specs=[smem(), stepped((STEP, tile, width)), whole(local.shape)],
        out_specs=whole(local.shape),
        out_shape=jax.ShapeDtypeStruct(local.shape, F32),
        compiler_params=params(),
        name="place_terms",
    )(wanted, arrived, local)


def exchange(values, axes):
    return lax.all_to_all(values, axes, 0, 0, tiled=True)


def on_device(
    features,
    weight,
    bias_vector,
    cotangent,
    near_tiles,
    near_offsets,
    near_cols,
    far_tiles,
    far_rows,
    far_cols,
):
    rows_dev, width = features.shape
    tile = near_tiles.shape[1]
    dom_count = lax.axis_size("dom")
    repl_count = lax.axis_size("repl")
    blocks_dom = rows_dev // tile * repl_count
    tiles = far_tiles.reshape(dom_count, tile, tile)
    frow = far_rows.reshape(dom_count)
    fcol = far_cols.reshape(dom_count)
    ncol = near_cols[0]
    nrow = slot_rows(near_offsets[0], near_tiles.shape[0])

    wanted = exchange(jnp.broadcast_to(fcol[:, None], (dom_count, 128)), "dom")[:, 0]
    blocks, reduced = pick_blocks(wanted, features, dom_count, tile)
    arrived = exchange(blocks, "dom")
    partial = aggregate(frow, nrow, ncol, arrived, tiles, near_tiles, reduced, blocks_dom)
    parts = exchange(partial.reshape(repl_count, rows_dev, width), "repl")
    hidden, grads, weight_term = dense_stage(parts, weight, bias_vector.reshape(1, width), cotangent)

    group_grad = exchange(grads, "repl").reshape(blocks_dom * tile, width)
    terms = far_terms(frow, group_grad, tiles, tile)
    far_back = exchange(terms, "dom")

    device_count = dom_count * repl_count
    node_total = rows_dev * device_count
    per_device = width // device_count
    gathered = exchange(weight_term, ("dom", "repl")).reshape(device_count, per_device * width)
    total = jnp.sum(gathered, axis=0, keepdims=True) * (1.0 / math.sqrt(node_total))
    spread = jnp.broadcast_to(total, (device_count, per_device * width))
    weight_grad = exchange(spread, ("dom", "repl")).reshape(width, width)

    local = near_terms(nrow, ncol, group_grad, near_tiles, rows_dev)
    grad_features = place_terms(wanted, far_back, local)
    return (hidden, grad_features, weight_grad)


def solution(mesh):
    placed = (
        P(("dom", "repl"), None),
        P(),
        P(),
        P(("dom", "repl"), None),
        P(("dom", "repl"), None, None),
        P(("dom", "repl"), None),
        P(("dom", "repl"), None),
        P(("dom", "repl"), None, None, None, None),
        P(("dom", "repl"), None, None),
        P(("dom", "repl"), None, None),
    )
    return jax.shard_map(
        on_device,
        mesh=mesh,
        in_specs=placed,
        out_specs=(P(("dom", "repl"), None), P(("dom", "repl"), None), P()),
        check_vma=False,
    )
```

time: 676 us -> 262 us (0.39)
  waiting for transfers between devices: 576 us -> 137 us
  blocking collectives: 0 us -> 73.7 us
  matrix products: 42.2 us -> 0 us
  starting transfers between devices: 0.39 us -> 25.2 us
  local copies, waits for them, and re-layouts: 28.6 us -> 10.7 us
  other arithmetic: 14.4 us -> 0.41 us
  between operations: 13.9 us -> 0.79 us
  Pallas kernels: 0 us -> 11.6 us
    psum x1 -> x0, waiting for transfers between devices: 238 us -> none  [on_device(): lax.psum(weight_term, ('dom', 'repl')) * (1.0 / math.sqrt(node_total))]
    reduce_scatter x2 -> x0, waiting for transfers between devices: 213 us -> none  [the longest x1 123 us: on_device(): lax.psum_scatter(placed.reshape(row_count, feat_width).astype(jnp.bfloat1...]
    all_to_all x0 -> x4, waiting for transfers between devices: none -> 137 us  [exchange(): return lax.all_to_all(values, axes, 0, 0, tiled=True)]
    all_gather x2 -> x0, waiting for transfers between devices: 124 us -> none  [the longest x1 66.3 us: on_device(): shard_rows = lax.all_gather(reduced, 'dom', axis=0, tiled=True)]
    all_to_all x0 -> x3, blocking collectives: none -> 73.7 us  [exchange(): return lax.all_to_all(values, axes, 0, 0, tiled=True)]
    dot_general x14 -> x0, matrix products: 42.2 us -> none  [the longest x4 17.5 us: select(): jnp.einsum(form, hot, values, preferred_element_type=jnp.float32)]
    all_to_all x0 -> x4, starting transfers between devices: none -> 25.2 us  [exchange(): return lax.all_to_all(values, axes, 0, 0, tiled=True)]
    dot_general x6 -> x0, local copies, waits for them, and re-layouts: 24.1 us -> none  [the longest x4 15.4 us: tile_product(): return jnp.einsum(form, tiles, values, preferred_element_type=jnp.float32)]
  transfers between devices with their start and end apart: 5 -> 4, of which waited for: 5 -> 4; matrix products, arithmetic and copies ran while one was open for 6% -> 0% of each run, Pallas kernels for 0% -> 1%
where the time goes in v1:
time: 262 us; the launch traced here: 259 us
  waiting for transfers between devices  137 us (52%)
  blocking collectives  73.7 us (28%)
  starting transfers between devices  25.2 us (10%)
  Pallas kernels  11.6 us (4%)
  local copies, waits for them, and re-layouts  10.7 us (4%)
    all_to_all x4, waiting for transfers between devices, exchange(): return lax.all_to_all(values, axes, 0, 0, tiled=True)  137 us
    all_to_all x3, blocking collectives, exchange(): return lax.all_to_all(values, axes, 0, 0, tiled=True)  73.7 us
    all_to_all x4, starting transfers between devices, exchange(): return lax.all_to_all(values, axes, 0, 0, tiled=True)  25.2 us
    unnamed x31, local copies, waits for them, and re-layouts  8.64 us
  transfers between devices with their start and end apart: 4, of which 4 were waited for; matrix products, arithmetic and copies ran while one was open for 0% of the time, Pallas kernels for 1%

profile of v1, /device:TPU:2, one launch (start us, length us, event | category | flops | bytes accessed | tf_op | source)
XLA Modules:
  0.0 259.1 jit_solution(4097439655720512678)
XLA Ops:
  0.6 0.7 broadcast_in_dim.7
  1.4 18.1 %all_to_all.47 = s32[32,1,128]{2,1,0:T(1,128)S(1)} all-to-all(s32[32,1,128]{2,1,0:T(1,128)S(1)} %broadcast_in_dim.7), channel_id=1, replica_groups=mesh['dom'=32,'repl'=8] {'dom'}, dimensions={0} | all-to-all | bytes 32768 | tf_op jit(solution)/shard_map/all_to_all | solution.py:246
  19.5 0.1 slice_reduce_fusion.wanted_ref
  19.6 0.0 copy-start.8
  19.6 1.0 copy-done.8
  20.6 0.8 pick_blocks.1
  21.5 0.0 copy-start.3
  21.5 1.3 copy-done.3
  22.8 0.0 copy-start.14
  22.8 0.0 copy-start.1
  22.8 0.0 copy-start.11
  22.8 0.0 copy-start.12
  22.8 4.2 %all-to-all-start.1 = ((bf16[32,128,256]{2,1,0:T(8,128)(2,1)}), bf16[32,128,256]{2,1,0:T(8,128)(2,1)S(1)}, u32[]{:S(2)}, u32[]{:S(2)}) async-start(bf16[32,128,256]{2,1,0:T(8,128)(2,1)} %copy-done.3), calls=%async_computation.1 | async-start | bytes 4194304 | tf_op jit(solution)/shard_map/all_to_all | solution.py:246
  27.0 0.0 copy-done.14
  27.0 0.1 slice_bitcast_fusion
  27.0 0.1 convert_reduce_fusion.nrow_ref
  27.2 50.2 %all-to-all-done.1.in_ref = bf16[32,128,256]{2,1,0:T(8,128)(2,1)S(1)} async-done(((bf16[32,128,256]{2,1,0:T(8,128)(2,1)}), bf16[32,128,256]{2,1,0:T(8,128)(2,1)S(1)}, u32[]{:S(2)}, u32[]{:S(2)}) %all-to-all-start.1) | async-done | bytes 2097184 | tf_op jit(solution)/shard_map/all_to_all | solution.py:246
  77.3 0.0 copy-done.1
  77.3 0.0 copy-done.11
  77.3 0.0 copy-done.12
  77.3 0.0 copy-start.6
  77.3 1.0 copy-done.6
  78.4 2.7 %aggregate.1 = bf16[4096,256]{1,0:T(8,128)(2,1)S(1)} custom-call(s32[32]{0:T(128)S(1)} %bitcast.22, s32[16]{0:T(128)S(1)} %convert_reduce_fusion.nrow_ref, s32[16]{0:T(128)S(1)} %bitcast.20, bf16[32,128,256]{2,1,0:T(8,128)(2,1)S(1)} %all-to-all-done.1.in_ref, bf16[32,128,128]{2,1,0:T(8,128)(2,1)S(1)} %bitcast.17, bf16[16,128,128]{2,1,0:T(8,128)(2,1)S(1)} %copy-done.6, ...), custom_call_target="tpu_custom_call" | custom-call | tf_op jit(solution)/shard_map/aggregate/pallas_call | solution.py:101
  81.1 0.0 copy-start.9
  81.1 0.0 copy-start.10
  81.1 0.0 copy-start.13
  81.1 33.7 %all_to_all.48.parts_ref = bf16[8,512,256]{2,1,0:T(8,128)(2,1)S(1)} all-to-all(bf16[8,512,256]{2,1,0:T(8,128)(2,1)S(1)} %bitcast.16), channel_id=1, replica_groups=mesh['dom'=32,'repl'=8] {'repl'}, dimensions={0} | all-to-all | bytes 4194304 | tf_op jit(solution)/shard_map/all_to_all | solution.py:246
  114.8 0.0 copy-done.9
  114.8 0.0 copy-done.10
  114.8 0.0 copy-done.13
  114.8 1.8 dense_stage.1
  116.6 0.0 copy-start.2
  116.6 1.3 copy-done.2
  118.0 0.3 copy.15
  118.2 21.9 %all_to_all.49 = f32[256,1,256]{2,1,0:T(1,128)S(1)} all-to-all(f32[256,1,256]{2,1,0:T(1,128)S(1)} %copy.15), channel_id=1, replica_groups=mesh['dom'=32,'repl'=8] {'dom','repl'}, dimensions={0} | all-to-all | bytes 524288 | tf_op jit(solution)/shard_map/all_to_all | solution.py:246
  140.1 5.0 %all-to-all-start.3 = ((bf16[8,512,256]{2,1,0:T(8,128)(2,1)}), bf16[8,512,256]{2,1,0:T(8,128)(2,1)S(1)}, u32[]{:S(2)}, u32[]{:S(2)}) async-start(bf16[8,512,256]{2,1,0:T(8,128)(2,1)} %copy-done.2), calls=%async_computation.3 | async-start | bytes 4194304 | tf_op jit(solution)/shard_map/all_to_all | solution.py:246
  145.1 0.3 reduce_sum.19
  145.4 27.2 %all-to-all-done.3 = bf16[8,512,256]{2,1,0:T(8,128)(2,1)S(1)} async-done(((bf16[8,512,256]{2,1,0:T(8,128)(2,1)}), bf16[8,512,256]{2,1,0:T(8,128)(2,1)S(1)}, u32[]{:S(2)}, u32[]{:S(2)}) %all-to-all-start.3) | async-done | bytes 2097184 | tf_op jit(solution)/shard_map/all_to_all | solution.py:246
  172.6 0.8 broadcast_in_dim.8
  173.4 11.3 %all-to-all-start.6 = ((f32[256,1,256]{2,1,0:T(1,128)}), f32[256,1,256]{2,1,0:T(1,128)S(1)}, u32[]{:S(2)}, u32[]{:S(2)}) async-start(f32[256,1,256]{2,1,0:T(1,128)} %broadcast_in_dim.8), calls=%async_computation.6 | async-start | bytes 524288 | tf_op jit(solution)/shard_map/all_to_all | solution.py:246
  184.8 1.9 far_terms.1
  186.7 0.0 copy-start
  186.7 1.3 copy-done
  188.1 0.0 copy-start.7
  188.1 11.6 %all-to-all-done.6 = f32[256,1,256]{2,1,0:T(1,128)S(1)} async-done(((f32[256,1,256]{2,1,0:T(1,128)}), f32[256,1,256]{2,1,0:T(1,128)S(1)}, u32[]{:S(2)}, u32[]{:S(2)}) %all-to-all-start.6) | async-done | bytes 262176 | tf_op jit(solution)/shard_map/all_to_all | solution.py:246
  199.6 4.8 %all-to-all-start.4 = ((bf16[32,128,256]{2,1,0:T(8,128)(2,1)}), bf16[32,128,256]{2,1,0:T(8,128)(2,1)}, u32[]{:S(2)}, u32[]{:S(2)}) async-start(bf16[32,128,256]{2,1,0:T(8,128)(2,1)} %copy-done), calls=%async_computation.4 | async-start | bytes 4194304 | tf_op jit(solution)/shard_map/all_to_all | solution.py:246
  204.4 0.7 copy.18
  205.1 0.0 copy-done.7
  205.1 1.0 near_terms.1.local_ref
  206.2 0.0 copy-start.4
  206.2 0.8 copy-done.4
  207.0 47.8 %all-to-all-done.4.in_ref = bf16[32,128,256]{2,1,0:T(8,128)(2,1)} async-done(((bf16[32,128,256]{2,1,0:T(8,128)(2,1)}), bf16[32,128,256]{2,1,0:T(8,128)(2,1)}, u32[]{:S(2)}, u32[]{:S(2)}) %all-to-all-start.4) | async-done | bytes 2097184 | tf_op jit(solution)/shard_map/all_to_all | solution.py:246
  254.7 0.0 copy-start.5
  254.7 1.0 copy-done.5
  255.8 3.3 %place_terms.1 = f32[512,256]{1,0:T(8,128)} custom-call(s32[32]{0:T(128)S(1)} %slice_reduce_fusion.wanted_ref, bf16[32,128,256]{2,1,0:T(8,128)(2,1)} %all-to-all-done.4.in_ref, f32[512,256]{1,0:T(8,128)S(1)} %copy-done.5), custom_call_target="tpu_custom_call" | custom-call | tf_op jit(solution)/shard_map/place_terms/pallas_call | solution.py:234
  (1 shorter events, 0.0 us)
Async XLA Ops:
  19.6 1.0 copy-start.8
  21.5 1.3 copy-start.3
  22.8 4.2 %copy-start.14 = (s32[1,33]{1,0:T(1,128)S(1)}, s32[1,33]{1,0:T(1,128)}, u32[]{:S(2)}) copy-start(s32[1,33]{1,0:T(1,128)} %param.15) | copy-start | bytes 400
  22.8 54.5 %copy-start.1 = (bf16[1,32,1,128,128]{4,3,2,1,0:T(8,128)(2,1)S(1)}, bf16[1,32,1,128,128]{4,3,2,1,0:T(8,128)(2,1)}, u32[]{:S(2)}) copy-start(bf16[1,32,1,128,128]{4,3,2,1,0:T(8,128)(2,1)} %param.17) | copy-start | bytes 3145732
  22.8 54.5 %copy-start.11 = (s32[1,16]{1,0:T(1,128)S(1)}, s32[1,16]{1,0:T(1,128)}, u32[]{:S(2)}) copy-start(s32[1,16]{1,0:T(1,128)} %param.16) | copy-start | bytes 196
  22.8 54.5 %copy-start.12 = (s32[1,32,1]{1,2,0:T(1,128)S(1)}, s32[1,32,1]{1,2,0:T(1,128)}, u32[]{:S(2)}) copy-start(s32[1,32,1]{1,2,0:T(1,128)} %param.18) | copy-start | bytes 388
  22.8 54.5 %all-to-all-start.1 = ((bf16[32,128,256]{2,1,0:T(8,128)(2,1)}), bf16[32,128,256]{2,1,0:T(8,128)(2,1)S(1)}, u32[]{:S(2)}, u32[]{:S(2)}) async-start(bf16[32,128,256]{2,1,0:T(8,128)(2,1)} %copy-done.3), calls=%async_computation.1 | async-start | bytes 4194304 | tf_op jit(solution)/shard_map/all_to_all | solution.py:246
  77.3 1.0 copy-start.6
  81.1 33.7 %copy-start.9 = (bf16[512,256]{1,0:T(8,128)(2,1)S(1)}, bf16[512,256]{1,0:T(8,128)(2,1)}, u32[]{:S(2)}) copy-start(bf16[512,256]{1,0:T(8,128)(2,1)} %ct_ref.1) | copy-start | bytes 786436
  81.1 33.7 %copy-start.10 = (bf16[256,256]{1,0:T(8,128)(2,1)S(1)}, bf16[256,256]{1,0:T(8,128)(2,1)}, u32[]{:S(2)}) copy-start(bf16[256,256]{1,0:T(8,128)(2,1)} %w_ref.1) | copy-start | bytes 393220
  81.1 33.7 %copy-start.13 = (f32[256]{0:T(256)S(1)}, f32[256]{0:T(256)}, u32[]{:S(2)}) copy-start(f32[256]{0:T(256)} %param.12) | copy-start | bytes 3076
  116.6 1.3 copy-start.2
  140.1 32.5 %all-to-all-start.3 = ((bf16[8,512,256]{2,1,0:T(8,128)(2,1)}), bf16[8,512,256]{2,1,0:T(8,128)(2,1)S(1)}, u32[]{:S(2)}, u32[]{:S(2)}) async-start(bf16[8,512,256]{2,1,0:T(8,128)(2,1)} %copy-done.2), calls=%async_computation.3 | async-start | bytes 4194304 | tf_op jit(solution)/shard_map/all_to_all | solution.py:246
  173.4 26.2 %all-to-all-start.6 = ((f32[256,1,256]{2,1,0:T(1,128)}), f32[256,1,256]{2,1,0:T(1,128)S(1)}, u32[]{:S(2)}, u32[]{:S(2)}) async-start(f32[256,1,256]{2,1,0:T(1,128)} %broadcast_in_dim.8), calls=%async_computation.6 | async-start | bytes 524288 | tf_op jit(solution)/shard_map/all_to_all | solution.py:246
  186.7 1.3 copy-start
  188.1 17.1 %copy-start.7 = (bf16[16,128,128]{2,1,0:T(8,128)(2,1)S(1)}, bf16[16,128,128]{2,1,0:T(8,128)(2,1)}, u32[]{:S(2)}) copy-start(bf16[16,128,128]{2,1,0:T(8,128)(2,1)} %near_ref.3) | copy-start | bytes 1572868
  199.6 55.1 %all-to-all-start.4 = ((bf16[32,128,256]{2,1,0:T(8,128)(2,1)}), bf16[32,128,256]{2,1,0:T(8,128)(2,1)}, u32[]{:S(2)}, u32[]{:S(2)}) async-start(bf16[32,128,256]{2,1,0:T(8,128)(2,1)} %copy-done), calls=%async_computation.4 | async-start | bytes 4194304 | tf_op jit(solution)/shard_map/all_to_all | solution.py:246
  206.2 0.8 copy-start.4
  254.7 1.0 copy-start.5

commit v2 on v1

v2 whole, which is shorter than its diff:
```python
import math

import jax
import jax.numpy as jnp
from jax import lax
from jax.experimental import pallas as pl
from jax.experimental.pallas import tpu as pltpu
from jax.sharding import PartitionSpec as P


BF16 = jnp.bfloat16
F32 = jnp.float32
STEP = 8


def slot_rows(offsets, slot_count):
    slots = jnp.arange(slot_count, dtype=jnp.int32)
    return jnp.sum((offsets[1:, None] <= slots[None, :]).astype(jnp.int32), axis=0)


def smem():
    return pl.BlockSpec(memory_space=pltpu.SMEM)


def whole(shape):
    return pl.BlockSpec(shape, lambda i: (0,) * len(shape))


def stepped(shape):
    return pl.BlockSpec(shape, lambda i: (i,) + (0,) * (len(shape) - 1))


def params(mib=40):
    return pltpu.CompilerParams(
        dimension_semantics=("arbitrary",), vmem_limit_bytes=mib * 1024 * 1024
    )


def transposed_dot(left, right):
    return lax.dot_general(left, right, (((0,), (0,)), ((), ())), preferred_element_type=F32)


def hbm():
    return pl.BlockSpec(memory_space=pltpu.HBM)


def in_hbm(values):
    return pltpu.with_memory_space_constraint(values, pltpu.HBM)


def pick_blocks(wanted, reduced, dom_count, tile):
    width = reduced.shape[1]

    def kernel(wanted_ref, red_ref, out_ref, sem):
        copies = []
        for d in range(dom_count):
            at = pl.multiple_of(wanted_ref[d] * tile, tile)
            copy = pltpu.make_async_copy(red_ref.at[pl.ds(at, tile), :], out_ref.at[d], sem.at[d])
            copy.start()
            copies.append(copy)
        for copy in copies:
            copy.wait()

    return pl.pallas_call(
        kernel,
        grid=(1,),
        in_specs=[smem(), whole(reduced.shape)],
        out_specs=hbm(),
        out_shape=pltpu.HBM((dom_count, tile, width), BF16),
        scratch_shapes=[pltpu.SemaphoreType.DMA((dom_count,))],
        compiler_params=params(),
        name="pick_blocks",
    )(wanted, reduced)


def aggregate(far_rows, near_rows, near_cols, arrived, far_tiles, near_tiles, reduced, blocks_dom):
    dom_count, tile, width = arrived.shape
    near_count = near_tiles.shape[0]
    steps = dom_count // STEP

    def kernel(
        frow_ref, nrow_ref, ncol_ref, in_ref, far_ref, near_hbm, red_ref, out_ref, acc_ref, near_ref, sem
    ):
        step = pl.program_id(0)
        fetch = pltpu.make_async_copy(near_hbm, near_ref, sem)

        def add(row, value):
            at = pl.ds(pl.multiple_of(row * tile, tile), tile)
            acc_ref[at, :] += value

        @pl.when(step == 0)
        def _():
            fetch.start()
            acc_ref[...] = jnp.zeros_like(acc_ref)

        for j in range(STEP):
            row = frow_ref[step * STEP + j]
            row = jnp.where(row < 0, blocks_dom, row)
            add(row, jnp.dot(far_ref[j], in_ref[j], preferred_element_type=F32))

        @pl.when(step == steps - 1)
        def _():
            fetch.wait()
            for q in range(near_count):
                src = pl.ds(pl.multiple_of(ncol_ref[q] * tile, tile), tile)
                add(
                    nrow_ref[q],
                    jnp.dot(near_ref[q], red_ref[src, :], preferred_element_type=F32),
                )
            out_ref[...] = acc_ref[: blocks_dom * tile, :].astype(BF16)

    return pl.pallas_call(
        kernel,
        grid=(steps,),
        in_specs=[
            smem(),
            smem(),
            smem(),
            stepped((STEP, tile, width)),
            stepped((STEP, tile, tile)),
            hbm(),
            whole(reduced.shape),
        ],
        out_specs=whole((blocks_dom * tile, width)),
        out_shape=jax.ShapeDtypeStruct((blocks_dom * tile, width), BF16),
        scratch_shapes=[
            pltpu.VMEM(((blocks_dom + 1) * tile, width), F32),
            pltpu.VMEM(near_tiles.shape, BF16),
            pltpu.SemaphoreType.DMA,
        ],
        compiler_params=params(),
        name="aggregate",
    )(far_rows, near_rows, near_cols, arrived, far_tiles, in_hbm(near_tiles), reduced)


def dense_stage(parts, weight, bias, cotangent):
    peers, rows, width = parts.shape
    chunk = 256

    def kernel(parts_ref, w_ref, b_ref, ct_ref, hid_ref, grads_ref, wt_ref, rows_ref, sem):
        step = pl.program_id(0)
        last = rows // chunk - 1
        total = parts_ref[0].astype(F32)
        for j in range(1, peers):
            total = total + parts_ref[j].astype(F32)
        summed = total.astype(BF16)
        w = w_ref[...]
        pre = jnp.dot(summed, w, preferred_element_type=F32) + b_ref[...]
        sigma = jax.nn.sigmoid(pre)
        hid_ref[...] = (pre * sigma).astype(BF16)
        grad_pre = (ct_ref[...].astype(F32) * sigma * (1.0 + pre * (1.0 - sigma))).astype(BF16)
        grad_rows = lax.dot_general(
            grad_pre, w, (((1,), (1,)), ((), ())), preferred_element_type=F32
        ).astype(BF16)
        at = pl.ds(pl.multiple_of(step * chunk, chunk), chunk)
        rows_ref[at, :] = grad_rows
        copies = [
            pltpu.make_async_copy(rows_ref.at[at, :], grads_ref.at[j, at, :], sem.at[step, j])
            for j in range(peers)
        ]
        for copy in copies:
            copy.start()
        term = transposed_dot(summed, grad_pre)

        @pl.when(step == 0)
        def _():
            wt_ref[...] = term

        @pl.when(step != 0)
        def _():
            wt_ref[...] += term

        @pl.when(step == last)
        def _():
            for i in range(last + 1):
                part = pl.ds(i * chunk, chunk)
                for j in range(peers):
                    pltpu.make_async_copy(
                        rows_ref.at[part, :], grads_ref.at[j, part, :], sem.at[i, j]
                    ).wait()

    return pl.pallas_call(
        kernel,
        grid=(rows // chunk,),
        in_specs=[
            pl.BlockSpec((peers, chunk, width), lambda i: (0, i, 0)),
            whole(weight.shape),
            whole((1, width)),
            stepped((chunk, width)),
        ],
        out_specs=[
            stepped((chunk, width)),
            hbm(),
            whole((width, width)),
        ],
        out_shape=[
            jax.ShapeDtypeStruct((rows, width), BF16),
            pltpu.HBM((peers, rows, width), BF16),
            jax.ShapeDtypeStruct((width, width), F32),
        ],
        scratch_shapes=[
            pltpu.VMEM((rows, width), BF16),
            pltpu.SemaphoreType.DMA((rows // chunk, peers)),
        ],
        compiler_params=params(),
        name="dense_stage",
    )(parts, weight, bias, cotangent)


def far_terms(far_rows, group_grad, far_tiles, tile):
    dom_count = far_tiles.shape[0]
    width = group_grad.shape[1]

    def kernel(frow_ref, grad_ref, far_ref, out_ref, terms_ref, sem):
        copies = []
        for k in range(dom_count):
            row = frow_ref[k]
            at = pl.ds(pl.multiple_of(jnp.maximum(row, 0) * tile, tile), tile)
            term = transposed_dot(far_ref[k], grad_ref[at, :])
            terms_ref[k] = jnp.where(row >= 0, term, 0.0).astype(BF16)
            copy = pltpu.make_async_copy(terms_ref.at[k], out_ref.at[k], sem.at[k])
            copy.start()
            copies.append(copy)
        for copy in copies:
            copy.wait()

    return pl.pallas_call(
        kernel,
        grid=(1,),
        in_specs=[smem(), whole(group_grad.shape), whole(far_tiles.shape)],
        out_specs=hbm(),
        out_shape=pltpu.HBM((dom_count, tile, width), BF16),
        scratch_shapes=[
            pltpu.VMEM((dom_count, tile, width), BF16),
            pltpu.SemaphoreType.DMA((dom_count,)),
        ],
        compiler_params=params(),
        name="far_terms",
    )(far_rows, group_grad, far_tiles)


def near_terms(near_rows, near_cols, group_grad, near_tiles, rows_dev):
    near_count, tile, _ = near_tiles.shape
    width = group_grad.shape[1]

    def kernel(nrow_ref, ncol_ref, grad_ref, near_ref, out_ref):
        out_ref[...] = jnp.zeros_like(out_ref)
        for q in range(near_count):
            src = pl.ds(pl.multiple_of(nrow_ref[q] * tile, tile), tile)
            dst = pl.ds(pl.multiple_of(ncol_ref[q] * tile, tile), tile)
            out_ref[dst, :] += transposed_dot(near_ref[q], grad_ref[src, :])

    return pl.pallas_call(
        kernel,
        grid=(1,),
        in_specs=[smem(), smem(), whole(group_grad.shape), whole(near_tiles.shape)],
        out_specs=whole((rows_dev, width)),
        out_shape=pltpu.HBM((rows_dev, width), F32),
        compiler_params=params(),
        name="near_terms",
    )(near_rows, near_cols, group_grad, near_tiles)


def place_terms(wanted, arrived, local):
    dom_count, tile, width = arrived.shape
    steps = dom_count // STEP

    def kernel(wanted_ref, in_ref, local_hbm, out_ref, local_ref, sem):
        step = pl.program_id(0)
        fetch = pltpu.make_async_copy(local_hbm, local_ref, sem)

        @pl.when(step == 0)
        def _():
            fetch.start()
            out_ref[...] = jnp.zeros_like(out_ref)

        for j in range(STEP):
            at = pl.ds(pl.multiple_of(wanted_ref[step * STEP + j] * tile, tile), tile)
            out_ref[at, :] += in_ref[j].astype(F32)

        @pl.when(step == steps - 1)
        def _():
            fetch.wait()
            out_ref[...] += local_ref[...]

    return pl.pallas_call(
        kernel,
        grid=(steps,),
        in_specs=[smem(), stepped((STEP, tile, width)), hbm()],
        out_specs=whole(local.shape),
        out_shape=jax.ShapeDtypeStruct(local.shape, F32),
        scratch_shapes=[pltpu.VMEM(local.shape, F32), pltpu.SemaphoreType.DMA],
        compiler_params=params(),
        name="place_terms",
    )(wanted, in_hbm(arrived), in_hbm(local))


def swap(values, axis, count, bit):
    return lax.ppermute(values, axis, [(i, i ^ bit) for i in range(count)])


def total_over_all(values, scale, dom_count, repl_count):
    place = lax.axis_index("repl")
    bits = []
    bit = repl_count // 2
    while bit:
        bits.append(bit)
        bit //= 2
    for bit in bits:
        half = values.shape[0] // 2
        mine = (place // bit) % 2
        kept = lax.dynamic_slice_in_dim(values, mine * half, half, 0)
        sent = lax.dynamic_slice_in_dim(values, (1 - mine) * half, half, 0)
        values = kept + swap(sent, "repl", repl_count, bit)
    bit = 1
    while bit < dom_count:
        values = values + swap(values, "dom", dom_count, bit)
        bit *= 2
    values = values * scale
    for bit in reversed(bits):
        other = swap(values, "repl", repl_count, bit)
        mine = (place // bit) % 2
        first = jnp.where(mine == 0, values, other)
        second = jnp.where(mine == 0, other, values)
        values = jnp.concatenate([first, second], axis=0)
    return values


def exchange(values, axes):
    return lax.all_to_all(values, axes, 0, 0, tiled=True)


def on_device(
    features,
    weight,
    bias_vector,
    cotangent,
    near_tiles,
    near_offsets,
    near_cols,
    far_tiles,
    far_rows,
    far_cols,
):
    rows_dev, width = features.shape
    tile = near_tiles.shape[1]
    dom_count = lax.axis_size("dom")
    repl_count = lax.axis_size("repl")
    blocks_dom = rows_dev // tile * repl_count
    tiles = far_tiles.reshape(dom_count, tile, tile)
    frow = far_rows.reshape(dom_count)
    fcol = far_cols.reshape(dom_count)
    ncol = near_cols[0]
    nrow = slot_rows(near_offsets[0], near_tiles.shape[0])

    wanted = exchange(jnp.broadcast_to(fcol[:, None], (dom_count, 128)), "dom")[:, 0]
    reduced = features.astype(BF16)
    blocks = pick_blocks(wanted, reduced, dom_count, tile)
    arrived = exchange(blocks, "dom")
    partial = aggregate(frow, nrow, ncol, arrived, tiles, near_tiles, reduced, blocks_dom)
    parts = exchange(partial.reshape(repl_count, rows_dev, width), "repl")
    hidden, grads, weight_term = dense_stage(parts, weight, bias_vector.reshape(1, width), cotangent)

    group_grad = exchange(grads, "repl").reshape(blocks_dom * tile, width)
    terms = far_terms(frow, group_grad, tiles, tile)
    far_back = exchange(terms, "dom")

    node_total = rows_dev * dom_count * repl_count
    weight_grad = total_over_all(weight_term, 1.0 / math.sqrt(node_total), dom_count, repl_count)

    local = near_terms(nrow, ncol, group_grad, near_tiles, rows_dev)
    grad_features = place_terms(wanted, far_back, local)
    return (hidden, grad_features, weight_grad)


def solution(mesh):
    placed = (
        P(("dom", "repl"), None),
        P(),
        P(),
        P(("dom", "repl"), None),
        P(("dom", "repl"), None, None),
        P(("dom", "repl"), None),
        P(("dom", "repl"), None),
        P(("dom", "repl"), None, None, None, None),
        P(("dom", "repl"), None, None),
        P(("dom", "repl"), None, None),
    )
    return jax.shard_map(
        on_device,
        mesh=mesh,
        in_specs=placed,
        out_specs=(P(("dom", "repl"), None), P(("dom", "repl"), None), P()),
        check_vma=False,
    )
```

time: 262 us -> 244 us (0.931)
  waiting for transfers between devices: 137 us -> 117 us
  starting transfers between devices: 25.2 us -> 40.6 us
  blocking collectives: 73.7 us -> 64.5 us
  local copies, waits for them, and re-layouts: 10.7 us -> 1.63 us
  Pallas kernels: 11.6 us -> 15.3 us
    all_to_all x4 -> x3, waiting for transfers between devices: 137 us -> 57.4 us  [exchange(): return lax.all_to_all(values, axes, 0, 0, tiled=True)]
    ppermute x0 -> x11, waiting for transfers between devices: none -> 59.8 us  [swap(): return lax.ppermute(values, axis, [(i, i ^ bit) for i in range(count)])]
    ppermute x0 -> x11, starting transfers between devices: none -> 21.1 us  [swap(): return lax.ppermute(values, axis, [(i, i ^ bit) for i in range(count)])]
    all_to_all x3 -> x2, blocking collectives: 73.7 us -> 64.5 us  [exchange(): return lax.all_to_all(values, axes, 0, 0, tiled=True)]
    unnamed x31 -> x16, local copies, waits for them, and re-layouts: 8.64 us -> 0.05 us
    all_to_all x4 -> x3, starting transfers between devices: 25.2 us -> 19.5 us  [exchange(): return lax.all_to_all(values, axes, 0, 0, tiled=True)]
  transfers between devices with their start and end apart: 4 -> 14, of which waited for: 4 -> 13; matrix products, arithmetic and copies ran while one was open for 0% -> 1% of each run, Pallas kernels for 1% -> 1%
where the time goes in v2:
time: 244 us; the launch traced here: 242 us
  waiting for transfers between devices  117 us (48%)
  blocking collectives  64.5 us (26%)
  starting transfers between devices  40.6 us (17%)
  Pallas kernels  15.3 us (6%)
    all_to_all x2, blocking collectives, exchange(): return lax.all_to_all(values, axes, 0, 0, tiled=True)  64.5 us
    ppermute x11, waiting for transfers between devices, swap(): return lax.ppermute(values, axis, [(i, i ^ bit) for i in range(count)])  59.8 us
    all_to_all x3, waiting for transfers between devices, exchange(): return lax.all_to_all(values, axes, 0, 0, tiled=True)  57.4 us
    ppermute x11, starting transfers between devices, swap(): return lax.ppermute(values, axis, [(i, i ^ bit) for i in range(count)])  21.1 us
    all_to_all x3, starting transfers between devices, exchange(): return lax.all_to_all(values, axes, 0, 0, tiled=True)  19.5 us
  transfers between devices with their start and end apart: 14, of which 13 were waited for; matrix products, arithmetic and copies ran while one was open for 1% of the time, Pallas kernels for 1%

profile of v2, /device:TPU:2, one launch (start us, length us, event | category | flops | bytes accessed | tf_op | source)
XLA Modules:
  0.0 242.2 jit_solution(17447715532119635950)
XLA Ops:
  0.6 1.4 broadcast_in_dim.10
  2.0 9.9 %all-to-all-start = ((s32[32,1,128]{2,1,0:T(1,128)}), s32[32,1,128]{2,1,0:T(1,128)S(1)}, u32[]{:S(2)}, u32[]{:S(2)}) async-start(s32[32,1,128]{2,1,0:T(1,128)} %broadcast_in_dim.10), calls=%async_computation | async-start | bytes 32768 | tf_op jit(solution)/shard_map/all_to_all | solution.py:330
  11.9 1.1 convert_element_type.7.red_ref
  12.9 7.3 %all-to-all-done = s32[32,1,128]{2,1,0:T(1,128)S(1)} async-done(((s32[32,1,128]{2,1,0:T(1,128)}), s32[32,1,128]{2,1,0:T(1,128)S(1)}, u32[]{:S(2)}, u32[]{:S(2)}) %all-to-all-start) | async-done | bytes 16416 | tf_op jit(solution)/shard_map/all_to_all | solution.py:330
  20.2 0.1 slice_reduce_fusion.wanted_ref
  20.3 2.2 pick_blocks.1
  22.5 0.0 copy-start.7
  22.5 0.0 copy-start
  22.5 0.0 copy-start.4
  22.5 0.0 copy-start.5
  22.5 4.2 %all-to-all-start.1 = ((bf16[32,128,256]{2,1,0:T(8,128)(2,1)}), bf16[32,128,256]{2,1,0:T(8,128)(2,1)S(1)}, u32[]{:S(2)}, u32[]{:S(2)}) async-start(bf16[32,128,256]{2,1,0:T(8,128)(2,1)} %pick_blocks.1), calls=%async_computation.1 | async-start | bytes 4194304 | tf_op jit(solution)/shard_map/all_to_all | solution.py:330
  26.7 0.0 copy-done.7
  26.7 0.1 slice_bitcast_fusion
  26.8 0.1 convert_reduce_fusion.nrow_ref
  26.9 50.2 %all-to-all-done.1.in_ref = bf16[32,128,256]{2,1,0:T(8,128)(2,1)S(1)} async-done(((bf16[32,128,256]{2,1,0:T(8,128)(2,1)}), bf16[32,128,256]{2,1,0:T(8,128)(2,1)S(1)}, u32[]{:S(2)}, u32[]{:S(2)}) %all-to-all-start.1) | async-done | bytes 2097184 | tf_op jit(solution)/shard_map/all_to_all | solution.py:330
  77.1 0.0 copy-done
  77.1 0.0 copy-done.4
  77.1 0.0 copy-done.5
  77.1 2.8 %aggregate.1 = bf16[4096,256]{1,0:T(8,128)(2,1)S(1)} custom-call(s32[32]{0:T(128)S(1)} %bitcast.17, s32[16]{0:T(128)S(1)} %convert_reduce_fusion.nrow_ref, s32[16]{0:T(128)S(1)} %bitcast.15, bf16[32,128,256]{2,1,0:T(8,128)(2,1)S(1)} %all-to-all-done.1.in_ref, bf16[32,128,128]{2,1,0:T(8,128)(2,1)S(1)} %bitcast.13, bf16[16,128,128]{2,1,0:T(8,128)(2,1)} %near_ref.1, ...), custom_call_target="tpu_custom_call" | custom-call | tf_op jit(solution)/shard_map/aggregate/pallas_call | solution.py:112
  79.8 0.0 copy-start.2
  79.8 0.0 copy-start.3
  79.9 0.0 copy-start.6
  79.9 33.7 %all_to_all.29.parts_ref = bf16[8,512,256]{2,1,0:T(8,128)(2,1)S(1)} all-to-all(bf16[8,512,256]{2,1,0:T(8,128)(2,1)S(1)} %bitcast.12), channel_id=1, replica_groups=mesh['dom'=32,'repl'=8] {'repl'}, dimensions={0} | all-to-all | bytes 4194304 | tf_op jit(solution)/shard_map/all_to_all | solution.py:330
  113.6 0.0 copy-done.2
  113.6 0.0 copy-done.3
  113.6 0.0 copy-done.6
  113.6 2.8 %dense_stage.1 = (bf16[512,256]{1,0:T(8,128)(2,1)}, bf16[8,512,256]{2,1,0:T(8,128)(2,1)}, f32[256,256]{1,0:T(8,128)S(1)}) custom-call(bf16[8,512,256]{2,1,0:T(8,128)(2,1)S(1)} %all_to_all.29.parts_ref, bf16[256,256]{1,0:T(8,128)(2,1)S(1)} %copy-done.3, f32[1,256]{1,0:T(1,128)S(1)} %bitcast.19, bf16[512,256]{1,0:T(8,128)(2,1)S(1)} %copy-done.2), custom_call_target="tpu_custom_call" | custom-call | tf_op jit(solution)/shard_map/dense_stage/pallas_call | solution.py:182
  116.4 30.8 %all_to_all.30 = bf16[8,512,256]{2,1,0:T(8,128)(2,1)S(1)} all-to-all(bf16[8,512,256]{2,1,0:T(8,128)(2,1)} %get-tuple-element.7), channel_id=1, replica_groups=mesh['dom'=32,'repl'=8] {'repl'}, dimensions={0} | all-to-all | bytes 4194304 | tf_op jit(solution)/shard_map/all_to_all | solution.py:330
  147.2 2.4 far_terms.1
  149.6 5.5 %all-to-all-start.4 = ((bf16[32,128,256]{2,1,0:T(8,128)(2,1)}), bf16[32,128,256]{2,1,0:T(8,128)(2,1)}, u32[]{:S(2)}, u32[]{:S(2)}) async-start(bf16[32,128,256]{2,1,0:T(8,128)(2,1)} %far_terms.1), calls=%async_computation.4 | async-start | bytes 4194304 | tf_op jit(solution)/shard_map/all_to_all | solution.py:330
  155.1 0.0 copy-start.1
  155.1 1.2 collective-permute-start
  156.4 8.9 %collective-permute-done = f32[128,256]{1,0:T(8,128)S(1)} collective-permute-done((f32[128,256]{1,0:T(8,128)S(1)}, f32[128,256]{1,0:T(8,128)S(1)}, u32[]{:S(2)}, u32[]{:S(2)}) %collective-permute-start) | collective-permute-done | bytes 131104 | tf_op jit(solution)/shard_map/ppermute | solution.py:299
  165.3 1.6 collective-permute-start.1
  166.9 4.3 %collective-permute-done.1 = f32[64,256]{1,0:T(8,128)S(1)} collective-permute-done((f32[64,256]{1,0:T(8,128)S(1)}, f32[64,256]{1,0:T(8,128)S(1)}, u32[]{:S(2)}, u32[]{:S(2)}) %collective-permute-start.1) | collective-permute-done | bytes 65568 | tf_op jit(solution)/shard_map/ppermute | solution.py:299
  171.2 1.3 collective-permute-start.2
  172.5 2.7 %collective-permute-done.2 = f32[32,256]{1,0:T(8,128)S(1)} collective-permute-done((f32[32,256]{1,0:T(8,128)S(1)}, f32[32,256]{1,0:T(8,128)S(1)}, u32[]{:S(2)}, u32[]{:S(2)}) %collective-permute-start.2) | collective-permute-done | bytes 32800 | tf_op jit(solution)/shard_map/ppermute | solution.py:299
  175.2 0.0 collective-permute-start.3
  175.2 1.2 collective-permute-done.3
  176.4 3.8 %collective-permute-start.4 = (f32[32,256]{1,0:T(8,128)S(1)}, f32[32,256]{1,0:T(8,128)S(1)}, u32[]{:S(2)}, u32[]{:S(2)}) collective-permute-start(f32[32,256]{1,0:T(8,128)S(1)} %add.70), channel_id=1, source_target_pairs={{0,16},{8,24},{16,0},{24,8},{32,48},{40,56},{48,32},{56,40},{64,80... | collective-permute-start | bytes 98312 | tf_op jit(solution)/shard_map/ppermute | solution.py:299
  180.2 22.9 %collective-permute-done.4 = f32[32,256]{1,0:T(8,128)S(1)} collective-permute-done((f32[32,256]{1,0:T(8,128)S(1)}, f32[32,256]{1,0:T(8,128)S(1)}, u32[]{:S(2)}, u32[]{:S(2)}) %collective-permute-start.4) | collective-permute-done | bytes 32800 | tf_op jit(solution)/shard_map/ppermute | solution.py:299
  203.1 1.7 collective-permute-start.5
  204.8 3.2 %collective-permute-done.5 = f32[32,256]{1,0:T(8,128)S(1)} collective-permute-done((f32[32,256]{1,0:T(8,128)S(1)}, f32[32,256]{1,0:T(8,128)S(1)}, u32[]{:S(2)}, u32[]{:S(2)}) %collective-permute-start.5) | collective-permute-done | bytes 32800 | tf_op jit(solution)/shard_map/ppermute | solution.py:299
  208.0 4.8 %collective-permute-start.6 = (f32[32,256]{1,0:T(8,128)S(1)}, f32[32,256]{1,0:T(8,128)S(1)}, u32[]{:S(2)}, u32[]{:S(2)}) collective-permute-start(f32[32,256]{1,0:T(8,128)S(1)} %add.72), channel_id=1, source_target_pairs={{0,64},{8,72},{16,80},{24,88},{32,96},{40,104},{48,112},{56,120},{... | collective-permute-start | bytes 98312 | tf_op jit(solution)/shard_map/ppermute | solution.py:299
  212.7 3.1 %collective-permute-done.6 = f32[32,256]{1,0:T(8,128)S(1)} collective-permute-done((f32[32,256]{1,0:T(8,128)S(1)}, f32[32,256]{1,0:T(8,128)S(1)}, u32[]{:S(2)}, u32[]{:S(2)}) %collective-permute-start.6) | collective-permute-done | bytes 32800 | tf_op jit(solution)/shard_map/ppermute | solution.py:299
  215.8 2.1 collective-permute-start.7
  217.9 1.9 collective-permute-done.7
  219.8 1.4 collective-permute-start.8
  221.2 2.5 %collective-permute-done.8 = f32[32,256]{1,0:T(8,128)S(1)} collective-permute-done((f32[32,256]{1,0:T(8,128)S(1)}, f32[32,256]{1,0:T(8,128)S(1)}, u32[]{:S(2)}, u32[]{:S(2)}) %collective-permute-start.8) | collective-permute-done | bytes 32800 | tf_op jit(solution)/shard_map/ppermute | solution.py:299
  223.7 1.5 collective-permute-start.9
  225.3 4.3 %collective-permute-done.9 = f32[64,256]{1,0:T(8,128)S(1)} collective-permute-done((f32[64,256]{1,0:T(8,128)S(1)}, f32[64,256]{1,0:T(8,128)S(1)}, u32[]{:S(2)}, u32[]{:S(2)}) %collective-permute-start.9) | collective-permute-done | bytes 65568 | tf_op jit(solution)/shard_map/ppermute | solution.py:299
  229.6 1.7 collective-permute-start.10
  231.4 4.8 %collective-permute-done.10 = f32[128,256]{1,0:T(8,128)S(1)} collective-permute-done((f32[128,256]{1,0:T(8,128)S(1)}, f32[128,256]{1,0:T(8,128)S(1)}, u32[]{:S(2)}, u32[]{:S(2)}) %collective-permute-start.10) | collective-permute-done | bytes 131104 | tf_op jit(solution)/shard_map/ppermute | solution.py:299
  236.2 0.7 pad_maximum_fusion
  236.9 0.0 copy-done.1
  236.9 1.8 near_terms.1.local_hbm
  238.8 0.0 all-to-all-done.4.in_ref
  238.8 3.4 %place_terms.1 = f32[512,256]{1,0:T(8,128)} custom-call(s32[32]{0:T(128)S(1)} %slice_reduce_fusion.wanted_ref, bf16[32,128,256]{2,1,0:T(8,128)(2,1)} %all-to-all-done.4.in_ref, f32[512,256]{1,0:T(8,128)} %near_terms.1.local_hbm), custom_call_target="tpu_custom_call" | custom-call | tf_op jit(solution)/shard_map/place_terms/pallas_call | solution.py:286
  (16 shorter events, 0.2 us)
Async XLA Ops:
  2.0 18.2 %all-to-all-start = ((s32[32,1,128]{2,1,0:T(1,128)}), s32[32,1,128]{2,1,0:T(1,128)S(1)}, u32[]{:S(2)}, u32[]{:S(2)}) async-start(s32[32,1,128]{2,1,0:T(1,128)} %broadcast_in_dim.10), calls=%async_computation | async-start | bytes 32768 | tf_op jit(solution)/shard_map/all_to_all | solution.py:330
  22.5 4.2 %copy-start.7 = (s32[1,33]{1,0:T(1,128)S(1)}, s32[1,33]{1,0:T(1,128)}, u32[]{:S(2)}) copy-start(s32[1,33]{1,0:T(1,128)} %param.15) | copy-start | bytes 400
  22.5 54.6 %copy-start = (bf16[1,32,1,128,128]{4,3,2,1,0:T(8,128)(2,1)S(1)}, bf16[1,32,1,128,128]{4,3,2,1,0:T(8,128)(2,1)}, u32[]{:S(2)}) copy-start(bf16[1,32,1,128,128]{4,3,2,1,0:T(8,128)(2,1)} %param.17) | copy-start | bytes 3145732
  22.5 54.5 %copy-start.4 = (s32[1,16]{1,0:T(1,128)S(1)}, s32[1,16]{1,0:T(1,128)}, u32[]{:S(2)}) copy-start(s32[1,16]{1,0:T(1,128)} %param.16) | copy-start | bytes 196
  22.5 54.5 %copy-start.5 = (s32[1,32,1]{1,2,0:T(1,128)S(1)}, s32[1,32,1]{1,2,0:T(1,128)}, u32[]{:S(2)}) copy-start(s32[1,32,1]{1,2,0:T(1,128)} %param.18) | copy-start | bytes 388
  22.5 54.5 %all-to-all-start.1 = ((bf16[32,128,256]{2,1,0:T(8,128)(2,1)}), bf16[32,128,256]{2,1,0:T(8,128)(2,1)S(1)}, u32[]{:S(2)}, u32[]{:S(2)}) async-start(bf16[32,128,256]{2,1,0:T(8,128)(2,1)} %pick_blocks.1), calls=%async_computation.1 | async-start | bytes 4194304 | tf_op jit(solution)/shard_map/all_to_all | solution.py:330
  79.8 33.7 %copy-start.2 = (bf16[512,256]{1,0:T(8,128)(2,1)S(1)}, bf16[512,256]{1,0:T(8,128)(2,1)}, u32[]{:S(2)}) copy-start(bf16[512,256]{1,0:T(8,128)(2,1)} %ct_ref.1) | copy-start | bytes 786436
  79.8 33.7 %copy-start.3 = (bf16[256,256]{1,0:T(8,128)(2,1)S(1)}, bf16[256,256]{1,0:T(8,128)(2,1)}, u32[]{:S(2)}) copy-start(bf16[256,256]{1,0:T(8,128)(2,1)} %w_ref.1) | copy-start | bytes 393220
  79.9 33.7 %copy-start.6 = (f32[256]{0:T(256)S(1)}, f32[256]{0:T(256)}, u32[]{:S(2)}) copy-start(f32[256]{0:T(256)} %param.12) | copy-start | bytes 3076
  149.6 89.2 %all-to-all-start.4 = ((bf16[32,128,256]{2,1,0:T(8,128)(2,1)}), bf16[32,128,256]{2,1,0:T(8,128)(2,1)}, u32[]{:S(2)}, u32[]{:S(2)}) async-start(bf16[32,128,256]{2,1,0:T(8,128)(2,1)} %far_terms.1), calls=%async_computation.4 | async-start | bytes 4194304 | tf_op jit(solution)/shard_map/all_to_all | solution.py:330
  155.1 81.9 %copy-start.1 = (bf16[16,128,128]{2,1,0:T(8,128)(2,1)S(1)}, bf16[16,128,128]{2,1,0:T(8,128)(2,1)}, u32[]{:S(2)}) copy-start(bf16[16,128,128]{2,1,0:T(8,128)(2,1)} %near_ref.1) | copy-start | bytes 1572868
  155.1 10.1 %collective-permute-start = (f32[128,256]{1,0:T(8,128)S(1)}, f32[128,256]{1,0:T(8,128)S(1)}, u32[]{:S(2)}, u32[]{:S(2)}) collective-permute-start(f32[128,256]{1,0:T(8,128)S(1)} %constant_dynamic-slice_fusion.2), channel_id=1, source_target_pairs={{0,4},{1,5},{2,6},{3,7},{4,0},{5,1},{6,2},{7,3},{8,12},{9,13},{10,... | collective-permute-start | bytes 393224 | tf_op jit(solution)/shard_map/ppermute | solution.py:299
  165.3 5.9 %collective-permute-start.1 = (f32[64,256]{1,0:T(8,128)S(1)}, f32[64,256]{1,0:T(8,128)S(1)}, u32[]{:S(2)}, u32[]{:S(2)}) collective-permute-start(f32[64,256]{1,0:T(8,128)S(1)} %constant_dynamic-slice_fusion.1), channel_id=1, source_target_pairs={{0,2},{1,3},{2,0},{3,1},{4,6},{5,7},{6,4},{7,5},{8,10},{9,11},{10,... | collective-permute-start | bytes 196616 | tf_op jit(solution)/shard_map/ppermute | solution.py:299
  171.2 4.0 %collective-permute-start.2 = (f32[32,256]{1,0:T(8,128)S(1)}, f32[32,256]{1,0:T(8,128)S(1)}, u32[]{:S(2)}, u32[]{:S(2)}) collective-permute-start(f32[32,256]{1,0:T(8,128)S(1)} %constant_dynamic-slice_fusion), channel_id=1, source_target_pairs={{0,1},{1,0},{2,3},{3,2},{4,5},{5,4},{6,7},{7,6},{8,9},{9,8},{10,11... | collective-permute-start | bytes 98312 | tf_op jit(solution)/shard_map/ppermute | solution.py:299
  175.2 1.2 collective-permute-start.3
  176.4 26.7 %collective-permute-start.4 = (f32[32,256]{1,0:T(8,128)S(1)}, f32[32,256]{1,0:T(8,128)S(1)}, u32[]{:S(2)}, u32[]{:S(2)}) collective-permute-start(f32[32,256]{1,0:T(8,128)S(1)} %add.70), channel_id=1, source_target_pairs={{0,16},{8,24},{16,0},{24,8},{32,48},{40,56},{48,32},{56,40},{64,80... | collective-permute-start | bytes 98312 | tf_op jit(solution)/shard_map/ppermute | solution.py:299
  203.1 4.8 %collective-permute-start.5 = (f32[32,256]{1,0:T(8,128)S(1)}, f32[32,256]{1,0:T(8,128)S(1)}, u32[]{:S(2)}, u32[]{:S(2)}) collective-permute-start(f32[32,256]{1,0:T(8,128)S(1)} %add.71), channel_id=1, source_target_pairs={{0,32},{8,40},{16,48},{24,56},{32,0},{40,8},{48,16},{56,24},{64,96... | collective-permute-start | bytes 98312 | tf_op jit(solution)/shard_map/ppermute | solution.py:299
  208.0 7.8 %collective-permute-start.6 = (f32[32,256]{1,0:T(8,128)S(1)}, f32[32,256]{1,0:T(8,128)S(1)}, u32[]{:S(2)}, u32[]{:S(2)}) collective-permute-start(f32[32,256]{1,0:T(8,128)S(1)} %add.72), channel_id=1, source_target_pairs={{0,64},{8,72},{16,80},{24,88},{32,96},{40,104},{48,112},{56,120},{... | collective-permute-start | bytes 98312 | tf_op jit(solution)/shard_map/ppermute | solution.py:299
  215.8 4.0 %collective-permute-start.7 = (f32[32,256]{1,0:T(8,128)S(1)}, f32[32,256]{1,0:T(8,128)S(1)}, u32[]{:S(2)}, u32[]{:S(2)}) collective-permute-start(f32[32,256]{1,0:T(8,128)S(1)} %add.73), channel_id=1, source_target_pairs={{0,128},{8,136},{16,144},{24,152},{32,160},{40,168},{48,176},{56,1... | collective-permute-start | bytes 98312 | tf_op jit(solution)/shard_map/ppermute | solution.py:299
  219.8 3.9 %collective-permute-start.8 = (f32[32,256]{1,0:T(8,128)S(1)}, f32[32,256]{1,0:T(8,128)S(1)}, u32[]{:S(2)}, u32[]{:S(2)}) collective-permute-start(f32[32,256]{1,0:T(8,128)S(1)} %add_multiply_fusion), channel_id=1, source_target_pairs={{0,1},{1,0},{2,3},{3,2},{4,5},{5,4},{6,7},{7,6},{8,9},{9,8},{10,11... | collective-permute-start | bytes 98312 | tf_op jit(solution)/shard_map/ppermute | solution.py:299
  223.7 5.9 %collective-permute-start.9 = (f32[64,256]{1,0:T(8,128)S(1)}, f32[64,256]{1,0:T(8,128)S(1)}, u32[]{:S(2)}, u32[]{:S(2)}) collective-permute-start(f32[64,256]{1,0:T(8,128)S(1)} %pad_maximum_fusion.2), channel_id=1, source_target_pairs={{0,2},{1,3},{2,0},{3,1},{4,6},{5,7},{6,4},{7,5},{8,10},{9,11},{10,... | collective-permute-start | bytes 196616 | tf_op jit(solution)/shard_map/ppermute | solution.py:299
  229.6 6.6 %collective-permute-start.10 = (f32[128,256]{1,0:T(8,128)S(1)}, f32[128,256]{1,0:T(8,128)S(1)}, u32[]{:S(2)}, u32[]{:S(2)}) collective-permute-start(f32[128,256]{1,0:T(8,128)S(1)} %pad_maximum_fusion.1), channel_id=1, source_target_pairs={{0,4},{1,5},{2,6},{3,7},{4,0},{5,1},{6,2},{7,3},{8,12},{9,13},{10,... | collective-permute-start | bytes 393224 | tf_op jit(solution)/shard_map/ppermute | solution.py:299

commit v3 on v2

--- a/solution.py
+++ b/solution.py
@@ -10,7 +10,6 @@
 
 BF16 = jnp.bfloat16
 F32 = jnp.float32
-STEP = 8
 
 
 def slot_rows(offsets, slot_count):
@@ -48,89 +47,120 @@
     return pltpu.with_memory_space_constraint(values, pltpu.HBM)
 
 
-def pick_blocks(wanted, reduced, dom_count, tile):
-    width = reduced.shape[1]
-
-    def kernel(wanted_ref, red_ref, out_ref, sem):
+STAGES = ((0, -1, 1), (-2, 2), (-3, 3), (4,))
+
+
+def anywhere():
+    return pl.BlockSpec(memory_space=pl.ANY)
+
+
+def pick_blocks(place, peer_cols, sources, offsets, z_count, tile):
+    width = sources[0].shape[1]
+    count = len(offsets)
+    peers = peer_cols.shape[0]
+
+    def kernel(place_ref, cols_ref, *refs):
+        src, out, sem = refs[:count], refs[count:-1], refs[-1]
+        rest, z, core = place_ref[0], place_ref[1], place_ref[2]
         copies = []
-        for d in range(dom_count):
-            at = pl.multiple_of(wanted_ref[d] * tile, tile)
-            copy = pltpu.make_async_copy(red_ref.at[pl.ds(at, tile), :], out_ref.at[d], sem.at[d])
+        for q in range(peers):
+            for n, offset in enumerate(offsets):
+                k = rest + lax.rem(z + offset + z_count, z_count) * 2 + core
+                at = pl.multiple_of(cols_ref[q, k] * tile, tile)
+                copy = pltpu.make_async_copy(
+                    src[n].at[pl.ds(at, tile), :], out[q].at[n], sem.at[q, n]
+                )
+                copy.start()
+                copies.append(copy)
+        for copy in copies:
+            copy.wait()
+
+    return pl.pallas_call(
+        kernel,
+        grid=(1,),
+        in_specs=[smem(), smem()] + [anywhere()] * count,
+        out_specs=[anywhere()] * peers,
+        out_shape=[jax.ShapeDtypeStruct((count, tile, width), BF16)] * peers,
+        scratch_shapes=[pltpu.SemaphoreType.DMA((peers, count))],
+        compiler_params=params(),
+        name="pick_blocks",
+    )(place, peer_cols, *sources)
+
+
+def aggregate(
+    place, far_rows, far_cols, near_rows, near_cols, lane, handed, far_tiles, near_tiles, blocks_dom
+):
+    tile = near_tiles.shape[1]
+    width = lane[0].shape[1]
+    near_count = near_tiles.shape[0]
+    slots = [(t, n, offset) for t, stage in enumerate(STAGES) for n, offset in enumerate(stage)]
+    z_count = len(slots)
+    y_stride = 2 * z_count
+    rows_out = blocks_dom * tile
+    piece = rows_out // 8
+
+    def kernel(place_ref, frow_ref, fcol_ref, nrow_ref, ncol_ref, *refs):
+        lane_refs = refs[:z_count]
+        hand_refs = refs[z_count : z_count + 3 * len(STAGES)]
+        far_ref, near_hbm, out_ref, acc_ref, near_ref, done_ref, sem, out_sem = refs[
+            z_count + 3 * len(STAGES) :
+        ]
+        fetch = pltpu.make_async_copy(near_hbm, near_ref, sem)
+        fetch.start()
+        acc_ref[...] = jnp.zeros_like(acc_ref)
+        rest, z, core = place_ref[0], place_ref[1], place_ref[2]
+
+        def add(row, value):
+            at = pl.ds(pl.multiple_of(row * tile, tile), tile)
+            acc_ref[at, :] += value
+
+        for m, (t, n, offset) in enumerate(slots):
+            for q in range(4):
+                line = y_stride - rest if q >= 2 else rest
+                side = 1 - core if q % 2 else core
+                k = line + lax.rem(z + offset + z_count, z_count) * 2 + side
+                if q == 0:
+                    at = pl.ds(pl.multiple_of(fcol_ref[k] * tile, tile), tile)
+                    block = lane_refs[m][at, :]
+                else:
+                    block = hand_refs[3 * t + q - 1][n]
+                row = frow_ref[k]
+                row = jnp.where(row < 0, blocks_dom, row)
+                add(row, jnp.dot(far_ref[k], block, preferred_element_type=F32))
+        fetch.wait()
+        for q in range(near_count):
+            at = pl.ds(pl.multiple_of(ncol_ref[q] * tile, tile), tile)
+            add(
+                nrow_ref[q],
+                jnp.dot(near_ref[q], lane_refs[0][at, :], preferred_element_type=F32),
+            )
+        copies = []
+        for n in range(8):
+            at = pl.ds(n * piece, piece)
+            done_ref[at, :] = acc_ref[at, :].astype(BF16)
+            copy = pltpu.make_async_copy(done_ref.at[at, :], out_ref.at[at, :], out_sem.at[n])
             copy.start()
             copies.append(copy)
         for copy in copies:
             copy.wait()
 
+    arrays = [*lane, *handed, far_tiles]
     return pl.pallas_call(
         kernel,
         grid=(1,),
-        in_specs=[smem(), whole(reduced.shape)],
+        in_specs=[smem()] * 5 + [whole(a.shape) for a in arrays] + [hbm()],
         out_specs=hbm(),
-        out_shape=pltpu.HBM((dom_count, tile, width), BF16),
-        scratch_shapes=[pltpu.SemaphoreType.DMA((dom_count,))],
-        compiler_params=params(),
-        name="pick_blocks",
-    )(wanted, reduced)
-
-
-def aggregate(far_rows, near_rows, near_cols, arrived, far_tiles, near_tiles, reduced, blocks_dom):
-    dom_count, tile, width = arrived.shape
-    near_count = near_tiles.shape[0]
-    steps = dom_count // STEP
-
-    def kernel(
-        frow_ref, nrow_ref, ncol_ref, in_ref, far_ref, near_hbm, red_ref, out_ref, acc_ref, near_ref, sem
-    ):
-        step = pl.program_id(0)
-        fetch = pltpu.make_async_copy(near_hbm, near_ref, sem)
-
-        def add(row, value):
-            at = pl.ds(pl.multiple_of(row * tile, tile), tile)
-            acc_ref[at, :] += value
-
-        @pl.when(step == 0)
-        def _():
-            fetch.start()
-            acc_ref[...] = jnp.zeros_like(acc_ref)
-
-        for j in range(STEP):
-            row = frow_ref[step * STEP + j]
-            row = jnp.where(row < 0, blocks_dom, row)
-            add(row, jnp.dot(far_ref[j], in_ref[j], preferred_element_type=F32))
-
-        @pl.when(step == steps - 1)
-        def _():
-            fetch.wait()
-            for q in range(near_count):
-                src = pl.ds(pl.multiple_of(ncol_ref[q] * tile, tile), tile)
-                add(
-                    nrow_ref[q],
-                    jnp.dot(near_ref[q], red_ref[src, :], preferred_element_type=F32),
-                )
-            out_ref[...] = acc_ref[: blocks_dom * tile, :].astype(BF16)
-
-    return pl.pallas_call(
-        kernel,
-        grid=(steps,),
-        in_specs=[
-            smem(),
-            smem(),
-            smem(),
-            stepped((STEP, tile, width)),
-            stepped((STEP, tile, tile)),
-            hbm(),
-            whole(reduced.shape),
-        ],
-        out_specs=whole((blocks_dom * tile, width)),
-        out_shape=jax.ShapeDtypeStruct((blocks_dom * tile, width), BF16),
+        out_shape=pltpu.HBM((rows_out, width), BF16),
         scratch_shapes=[
             pltpu.VMEM(((blocks_dom + 1) * tile, width), F32),
             pltpu.VMEM(near_tiles.shape, BF16),
+            pltpu.VMEM((rows_out, width), BF16),
             pltpu.SemaphoreType.DMA,
+            pltpu.SemaphoreType.DMA((8,)),
         ],
         compiler_params=params(),
         name="aggregate",
-    )(far_rows, near_rows, near_cols, arrived, far_tiles, in_hbm(near_tiles), reduced)
+    )(place, far_rows, far_cols, near_rows, near_cols, *arrays, in_hbm(near_tiles))
 
 
 def dense_stage(parts, weight, bias, cotangent):
@@ -261,69 +291,73 @@
     )(near_rows, near_cols, group_grad, near_tiles)
 
 
-def place_terms(wanted, arrived, local):
-    dom_count, tile, width = arrived.shape
-    steps = dom_count // STEP
-
-    def kernel(wanted_ref, in_ref, local_hbm, out_ref, local_ref, sem):
-        step = pl.program_id(0)
+def place_terms(me, group_cols, masks, arrived, local):
+    dom_count, tile, _ = arrived.shape
+
+    def kernel(me_ref, cols_ref, in_hbm_ref, local_hbm, out_ref, in_ref, local_ref, sem, in_sem):
         fetch = pltpu.make_async_copy(local_hbm, local_ref, sem)
-
-        @pl.when(step == 0)
-        def _():
-            fetch.start()
-            out_ref[...] = jnp.zeros_like(out_ref)
-
-        for j in range(STEP):
-            at = pl.ds(pl.multiple_of(wanted_ref[step * STEP + j] * tile, tile), tile)
-            out_ref[at, :] += in_ref[j].astype(F32)
-
-        @pl.when(step == steps - 1)
-        def _():
-            fetch.wait()
-            out_ref[...] += local_ref[...]
-
-    return pl.pallas_call(
-        kernel,
-        grid=(steps,),
-        in_specs=[smem(), stepped((STEP, tile, width)), hbm()],
+        fetch.start()
+        here = me_ref[0]
+        copies = []
+        for n, mask in enumerate(masks):
+            d = lax.bitwise_xor(here, mask)
+            copy = pltpu.make_async_copy(in_hbm_ref.at[d], in_ref.at[n], in_sem.at[n])
+            copy.start()
+            copies.append(copy)
+        out_ref[...] = jnp.zeros_like(out_ref)
+        for n in range(dom_count):
+            copies[n].wait()
+            at = pl.ds(pl.multiple_of(cols_ref[n, here] * tile, tile), tile)
+            out_ref[at, :] += in_ref[n].astype(F32)
+        fetch.wait()
+        out_ref[...] += local_ref[...]
+
+    return pl.pallas_call(
+        kernel,
+        grid=(1,),
+        in_specs=[smem(), smem(), hbm(), hbm()],
         out_specs=whole(local.shape),
         out_shape=jax.ShapeDtypeStruct(local.shape, F32),
-        scratch_shapes=[pltpu.VMEM(local.shape, F32), pltpu.SemaphoreType.DMA],
+        scratch_shapes=[
+            pltpu.VMEM(arrived.shape, BF16),
+            pltpu.VMEM(local.shape, F32),
+            pltpu.SemaphoreType.DMA,
+            pltpu.SemaphoreType.DMA((dom_count,)),
+        ],
         compiler_params=params(),
         name="place_terms",
-    )(wanted, in_hbm(arrived), in_hbm(local))
+    )(me, group_cols, in_hbm(arrived), in_hbm(local))
 
 
 def swap(values, axis, count, bit):
     return lax.ppermute(values, axis, [(i, i ^ bit) for i in range(count)])
 
 
+def meet(values, axis, count, bit):
+    rounded = lax.reduce_precision(values, 8, 7)
+    return rounded + swap(rounded.astype(BF16), axis, count, bit).astype(F32)
+
+
 def total_over_all(values, scale, dom_count, repl_count):
-    place = lax.axis_index("repl")
-    bits = []
-    bit = repl_count // 2
-    while bit:
-        bits.append(bit)
-        bit //= 2
-    for bit in bits:
-        half = values.shape[0] // 2
-        mine = (place // bit) % 2
-        kept = lax.dynamic_slice_in_dim(values, mine * half, half, 0)
-        sent = lax.dynamic_slice_in_dim(values, (1 - mine) * half, half, 0)
-        values = kept + swap(sent, "repl", repl_count, bit)
+    core = lax.axis_index("dom") % 2
+    half = values.shape[0] // 2
+    kept = lax.dynamic_slice_in_dim(values, core * half, half, 0)
+    sent = lax.dynamic_slice_in_dim(values, (1 - core) * half, half, 0)
+    values = kept + swap(sent, "dom", dom_count, 1)
+    bit = 2
+    while bit < dom_count // 2:
+        values = meet(values, "dom", dom_count, bit)
+        bit *= 2
     bit = 1
-    while bit < dom_count:
-        values = values + swap(values, "dom", dom_count, bit)
+    while bit < repl_count // 2:
+        values = meet(values, "repl", repl_count, bit)
         bit *= 2
-    values = values * scale
-    for bit in reversed(bits):
-        other = swap(values, "repl", repl_count, bit)
-        mine = (place // bit) % 2
-        first = jnp.where(mine == 0, values, other)
-        second = jnp.where(mine == 0, other, values)
-        values = jnp.concatenate([first, second], axis=0)
-    return values
+    values = meet(values, "dom", dom_count, dom_count // 2)
+    values = meet(values, "repl", repl_count, repl_count // 2) * scale
+    other = swap(values, "dom", dom_count, 1)
+    first = jnp.where(core == 0, values, other)
+    second = jnp.where(core == 0, other, values)
+    return jnp.concatenate([first, second], axis=0)
 
 
 def exchange(values, axes):
@@ -353,11 +387,54 @@
     ncol = near_cols[0]
     nrow = slot_rows(near_offsets[0], near_tiles.shape[0])
 
-    wanted = exchange(jnp.broadcast_to(fcol[:, None], (dom_count, 128)), "dom")[:, 0]
     reduced = features.astype(BF16)
-    blocks = pick_blocks(wanted, reduced, dom_count, tile)
-    arrived = exchange(blocks, "dom")
-    partial = aggregate(frow, nrow, ncol, arrived, tiles, near_tiles, reduced, blocks_dom)
+    z_count = dom_count // 4
+    here = lax.axis_index("dom")
+    place = jnp.stack([here // (2 * z_count) * (2 * z_count), here // 2 % z_count, here % 2])
+
+    def along_z(values, shift):
+        pairs = [
+            (i, i // (2 * z_count) * (2 * z_count) + (i // 2 + shift) % z_count * 2 + i % 2)
+            for i in range(dom_count)
+        ]
+        return lax.ppermute(values, "dom", pairs)
+
+    up = [along_z(reduced, 1)]
+    down = [along_z(reduced, -1)]
+    masks = (1, dom_count // 2, dom_count // 2 + 1)
+    row = jnp.broadcast_to(fcol[None, :], (8, dom_count))
+    rows = [swap(row, "dom", dom_count, m)[0] for m in masks]
+    peer_cols = jnp.stack(rows)
+    for _ in range(2):
+        up.append(along_z(up[-1], 1))
+        down.append(along_z(down[-1], -1))
+    half = rows_dev // 2
+    across = [along_z(up[-1][:half], 1), along_z(down[-1][half:], -1)]
+    across = jnp.concatenate(across, axis=0)
+    lane = (reduced, up[0], down[0], up[1], down[1], up[2], down[2], across)
+
+    def hand_out(first, offsets):
+        picked = pick_blocks(
+            place, peer_cols, lane[first : first + len(offsets)], offsets, z_count, tile
+        )
+        return [swap(blocks, "dom", dom_count, m) for blocks, m in zip(picked, masks)]
+
+    handed = []
+    first = 0
+    for stage in STAGES:
+        handed += hand_out(first, stage)
+        first += len(stage)
+    partial = aggregate(
+        place, frow, fcol, nrow, ncol, lane, handed, tiles, near_tiles, blocks_dom
+    )
+    known = [0, *masks]
+    group_cols = jnp.concatenate([fcol[None, :], peer_cols], axis=0)
+    bit = 2
+    while bit < dom_count // 2:
+        other = swap(group_cols, "dom", dom_count, bit)
+        group_cols = jnp.concatenate([group_cols, other], axis=0)
+        known += [m + bit for m in known]
+        bit *= 2
     parts = exchange(partial.reshape(repl_count, rows_dev, width), "repl")
     hidden, grads, weight_term = dense_stage(parts, weight, bias_vector.reshape(1, width), cotangent)
 
@@ -369,7 +446,7 @@
     weight_grad = total_over_all(weight_term, 1.0 / math.sqrt(node_total), dom_count, repl_count)
 
     local = near_terms(nrow, ncol, group_grad, near_tiles, rows_dev)
-    grad_features = place_terms(wanted, far_back, local)
+    grad_features = place_terms(here.reshape(1), group_cols, known, far_back, local)
     return (hidden, grad_features, weight_grad)
 
 

time: 244 us -> 244 us (level)
  waiting for transfers between devices: 117 us -> 100 us
  starting transfers between devices: 40.6 us -> 50.5 us
  Pallas kernels: 15.3 us -> 19.8 us
  blocking collectives: 64.5 us -> 67.5 us
    all_to_all x3 -> x1, waiting for transfers between devices: 57.4 us -> 0.01 us  [exchange(): return lax.all_to_all(values, axes, 0, 0, tiled=True)]
    ppermute x11 -> x27, waiting for transfers between devices: 59.8 us -> 88.2 us  [swap(): return lax.ppermute(values, axis, [(i, i ^ bit) for i in range(count)])]
    ppermute x0 -> x8, starting transfers between devices: none -> 15.4 us  [along_z(): return lax.ppermute(values, 'dom', pairs)]
    all_to_all x3 -> x1, starting transfers between devices: 19.5 us -> 4.77 us  [exchange(): return lax.all_to_all(values, axes, 0, 0, tiled=True)]
    ppermute x0 -> x8, waiting for transfers between devices: none -> 12.2 us  [along_z(): return lax.ppermute(values, 'dom', pairs)]
    ppermute x11 -> x27, starting transfers between devices: 21.1 us -> 30.3 us  [swap(): return lax.ppermute(values, axis, [(i, i ^ bit) for i in range(count)])]
    pallas_call x3 -> x6, Pallas kernels: 8.35 us -> 12.8 us  [the longest x4 4.71 us: pick_blocks(): pl.pallas_call(kernel, grid=(1,), in_specs=[smem(), smem()] + [anywhere()...]
    all_to_all x2, blocking collectives: 64.5 us -> 67.5 us  [exchange(): return lax.all_to_all(values, axes, 0, 0, tiled=True)]
  transfers between devices with their start and end apart: 14 -> 36, of which waited for: 13 -> 22; matrix products, arithmetic and copies ran while one was open for 1% -> 1% of each run, Pallas kernels for 1% -> 3%
where the time goes in v3:
time: 244 us; the launch traced here: 243 us
  waiting for transfers between devices  100 us (41%)
  blocking collectives  67.5 us (28%)
  starting transfers between devices  50.5 us (21%)
  Pallas kernels  19.8 us (8%)
    ppermute x27, waiting for transfers between devices, swap(): return lax.ppermute(values, axis, [(i, i ^ bit) for i in range(count)])  88.2 us
    all_to_all x2, blocking collectives, exchange(): return lax.all_to_all(values, axes, 0, 0, tiled=True)  67.5 us
    ppermute x27, starting transfers between devices, swap(): return lax.ppermute(values, axis, [(i, i ^ bit) for i in range(count)])  30.3 us
    ppermute x8, starting transfers between devices, along_z(): return lax.ppermute(values, 'dom', pairs)  15.4 us
    ppermute x8, waiting for transfers between devices, along_z(): return lax.ppermute(values, 'dom', pairs)  12.2 us
  transfers between devices with their start and end apart: 36, of which 22 were waited for; matrix products, arithmetic and copies ran while one was open for 1% of the time, Pallas kernels for 3%

profile of v3, /device:TPU:2, one launch (start us, length us, event | category | flops | bytes accessed | tf_op | source)
XLA Modules:
  0.0 242.5 jit_solution(3771732170700966847)
XLA Ops:
  0.7 1.2 convert_element_type.49.refs_0_
  1.8 5.9 %collective-permute-start.1 = (bf16[512,256]{1,0:T(8,128)(2,1)S(1)}, bf16[512,256]{1,0:T(8,128)(2,1)S(1)}, u32[]{:S(2)}, u32[]{:S(2)}) collective-permute-start(bf16[512,256]{1,0:T(8,128)(2,1)S(1)} %convert_element_type.49.refs_0_), channel_id=1, source_target_pairs={{0,112},{8,120},{16,0},{24,8},{32,16},{40,24},{48,32},{56,40},{64,... | collective-permute-start | bytes 786440 | tf_op jit(solution)/shard_map/ppermute | solution.py:400
  7.8 5.6 %collective-permute-done.1.refs_2_ = bf16[512,256]{1,0:T(8,128)(2,1)S(1)} collective-permute-done((bf16[512,256]{1,0:T(8,128)(2,1)S(1)}, bf16[512,256]{1,0:T(8,128)(2,1)S(1)}, u32[]{:S(2)}, u32[]{:S(2)}) %collective-permute-start.1) | collective-permute-done | bytes 262176 | tf_op jit(solution)/shard_map/ppermute | solution.py:400
  13.3 3.7 %collective-permute-start.3 = (bf16[512,256]{1,0:T(8,128)(2,1)S(1)}, bf16[512,256]{1,0:T(8,128)(2,1)S(1)}, u32[]{:S(2)}, u32[]{:S(2)}) collective-permute-start(bf16[512,256]{1,0:T(8,128)(2,1)S(1)} %collective-permute-done.1.refs_2_), channel_id=1, source_target_pairs={{0,112},{8,120},{16,0},{24,8},{32,16},{40,24},{48,32},{56,40},{64,... | collective-permute-start | bytes 786440 | tf_op jit(solution)/shard_map/ppermute | solution.py:400
  17.0 0.7 broadcast_in_dim.2
  17.7 1.6 collective-permute-start.9
  19.3 0.3 collective-permute-start.8
  19.6 1.1 collective-permute-done.10
  20.7 0.6 collective-permute-done.9
  21.3 0.4 collective-permute-done.3.refs_1_.refs_4_
  21.7 3.7 %collective-permute-start.5 = (bf16[512,256]{1,0:T(8,128)(2,1)S(1)}, bf16[512,256]{1,0:T(8,128)(2,1)S(1)}, u32[]{:S(2)}, u32[]{:S(2)}) collective-permute-start(bf16[512,256]{1,0:T(8,128)(2,1)S(1)} %collective-permute-done.3.refs_1_.refs_4_), channel_id=1, source_target_pairs={{0,112},{8,120},{16,0},{24,8},{32,16},{40,24},{48,32},{56,40},{64,... | collective-permute-start | bytes 786440 | tf_op jit(solution)/shard_map/ppermute | solution.py:400
  25.5 1.5 pick_blocks.4
  27.0 1.7 collective-permute-start.12
  28.7 0.2 collective-permute-start.13
  28.9 1.2 pick_blocks.5
  30.1 1.1 collective-permute-done.5.refs_1_.refs_6_
  31.2 3.4 %collective-permute-done.4.refs_0_.refs_5_ = bf16[512,256]{1,0:T(8,128)(2,1)S(1)} collective-permute-done((bf16[512,256]{1,0:T(8,128)(2,1)S(1)}, bf16[512,256]{1,0:T(8,128)(2,1)S(1)}, u32[]{:S(2)}, u32[]{:S(2)}) %collective-permute-start.4) | collective-permute-done | bytes 262176 | tf_op jit(solution)/shard_map/ppermute | solution.py:400
  34.6 0.4 collective-permute-start.7
  35.0 1.7 collective-permute-start.6
  36.8 1.2 pick_blocks.6
  38.0 0.5 collective-permute-start.15
  38.5 1.7 collective-permute-start.16
  40.3 1.7 collective-permute-done.6
  42.0 0.7 collective-permute-start.18
  42.7 1.4 collective-permute-start.19
  44.1 0.9 pick_blocks.7
  45.0 0.4 collective-permute-start.20
  45.4 0.6 collective-permute-start.21
  45.9 1.4 collective-permute-start.22
  47.5 1.5 collective-permute-done.18.refs_15_
  49.0 2.0 collective-permute-done.19.refs_16_
  50.9 2.3 collective-permute-done.21.refs_18_
  53.2 0.6 collective-permute-done.22.refs_19_
  53.8 4.3 %aggregate.1 = bf16[4096,256]{1,0:T(8,128)(2,1)} custom-call(s32[3]{0:T(128)S(1)} %pad_add_fusion.2.place_ref, s32[32]{0:T(128)S(1)} %bitcast.26, s32[32]{0:T(128)S(1)} %bitcast.19, s32[16]{0:T(128)S(1)} %convert_reduce_fusion.nrow_ref, s32[16]{0:T(128)S(1)} %bitcast.24, bf16[512,256]{1,0:T(8,128)(2,1)S(1)} %convert_element_type.49.refs_0_, ...), custom_call_target="tpu_custom_call" | custom-call | tf_op jit(solution)/shard_map/aggregate/pallas_call | solution.py:148
  58.2 35.1 %all_to_all.15.parts_ref = bf16[8,512,256]{2,1,0:T(8,128)(2,1)S(1)} all-to-all(bf16[8,512,256]{2,1,0:T(8,128)(2,1)} %bitcast.29), channel_id=1, replica_groups=mesh['dom'=32,'repl'=8] {'repl'}, dimensions={0} | all-to-all | bytes 4194304 | tf_op jit(solution)/shard_map/all_to_all | solution.py:364
  93.3 2.8 %dense_stage.1 = (bf16[512,256]{1,0:T(8,128)(2,1)}, bf16[8,512,256]{2,1,0:T(8,128)(2,1)}, f32[256,256]{1,0:T(8,128)S(1)}) custom-call(bf16[8,512,256]{2,1,0:T(8,128)(2,1)S(1)} %all_to_all.15.parts_ref, bf16[256,256]{1,0:T(8,128)(2,1)S(1)} %copy-done.3, f32[1,256]{1,0:T(1,128)S(1)} %bitcast.28, bf16[512,256]{1,0:T(8,128)(2,1)S(1)} %copy-done.2), custom_call_target="tpu_custom_call" | custom-call | tf_op jit(solution)/shard_map/dense_stage/pallas_call | solution.py:212
  96.1 32.4 %all_to_all.16 = bf16[8,512,256]{2,1,0:T(8,128)(2,1)S(1)} all-to-all(bf16[8,512,256]{2,1,0:T(8,128)(2,1)} %get-tuple-element.31), channel_id=1, replica_groups=mesh['dom'=32,'repl'=8] {'repl'}, dimensions={0} | all-to-all | bytes 4194304 | tf_op jit(solution)/shard_map/all_to_all | solution.py:364
  128.5 2.4 far_terms.1
  130.9 4.8 %all-to-all-start.2 = ((bf16[32,128,256]{2,1,0:T(8,128)(2,1)}), bf16[32,128,256]{2,1,0:T(8,128)(2,1)}, u32[]{:S(2)}, u32[]{:S(2)}) async-start(bf16[32,128,256]{2,1,0:T(8,128)(2,1)} %far_terms.1), calls=%async_computation.2 | async-start | bytes 4194304 | tf_op jit(solution)/shard_map/all_to_all | solution.py:364
  135.7 0.2 collective-permute-start.26
  135.9 1.3 collective-permute-done.26
  137.2 1.7 collective-permute-start.27
  138.9 45.8 %collective-permute-done.27 = bf16[128,256]{1,0:T(8,128)(2,1)S(1)} collective-permute-done((bf16[128,256]{1,0:T(8,128)(2,1)S(1)}, bf16[128,256]{1,0:T(8,128)(2,1)S(1)}, u32[]{:S(2)}, u32[]{:S(2)}) %collective-permute-start.27) | collective-permute-done | bytes 65568 | tf_op jit(solution)/shard_map/ppermute | solution.py:333
  184.7 1.3 collective-permute-start.28
  185.9 4.6 %collective-permute-done.28 = bf16[128,256]{1,0:T(8,128)(2,1)S(1)} collective-permute-done((bf16[128,256]{1,0:T(8,128)(2,1)S(1)}, bf16[128,256]{1,0:T(8,128)(2,1)S(1)}, u32[]{:S(2)}, u32[]{:S(2)}) %collective-permute-start.28) | collective-permute-done | bytes 65568 | tf_op jit(solution)/shard_map/ppermute | solution.py:333
  190.6 4.2 %collective-permute-start.29 = (bf16[128,256]{1,0:T(8,128)(2,1)S(1)}, bf16[128,256]{1,0:T(8,128)(2,1)S(1)}, u32[]{:S(2)}, u32[]{:S(2)}) collective-permute-start(bf16[128,256]{1,0:T(8,128)(2,1)S(1)} %fusion.4), channel_id=1, source_target_pairs={{0,64},{8,72},{16,80},{24,88},{32,96},{40,104},{48,112},{56,120},{... | collective-permute-start | bytes 196616 | tf_op jit(solution)/shard_map/ppermute | solution.py:333
  194.8 4.0 %collective-permute-done.29 = bf16[128,256]{1,0:T(8,128)(2,1)S(1)} collective-permute-done((bf16[128,256]{1,0:T(8,128)(2,1)S(1)}, bf16[128,256]{1,0:T(8,128)(2,1)S(1)}, u32[]{:S(2)}, u32[]{:S(2)}) %collective-permute-start.29) | collective-permute-done | bytes 65568 | tf_op jit(solution)/shard_map/ppermute | solution.py:333
  198.9 1.0 collective-permute-start.30
  199.9 3.6 %collective-permute-done.30 = bf16[128,256]{1,0:T(8,128)(2,1)S(1)} collective-permute-done((bf16[128,256]{1,0:T(8,128)(2,1)S(1)}, bf16[128,256]{1,0:T(8,128)(2,1)S(1)}, u32[]{:S(2)}, u32[]{:S(2)}) %collective-permute-start.30) | collective-permute-done | bytes 65568 | tf_op jit(solution)/shard_map/ppermute | solution.py:333
  203.6 1.4 collective-permute-start.31
  205.0 4.5 %collective-permute-done.31 = bf16[128,256]{1,0:T(8,128)(2,1)S(1)} collective-permute-done((bf16[128,256]{1,0:T(8,128)(2,1)S(1)}, bf16[128,256]{1,0:T(8,128)(2,1)S(1)}, u32[]{:S(2)}, u32[]{:S(2)}) %collective-permute-start.31) | collective-permute-done | bytes 65568 | tf_op jit(solution)/shard_map/ppermute | solution.py:333
  209.5 2.0 collective-permute-start.32
  211.5 2.3 collective-permute-done.32
  213.8 1.5 collective-permute-start.33
  215.4 4.3 %collective-permute-done.33 = bf16[128,256]{1,0:T(8,128)(2,1)S(1)} collective-permute-done((bf16[128,256]{1,0:T(8,128)(2,1)S(1)}, bf16[128,256]{1,0:T(8,128)(2,1)S(1)}, u32[]{:S(2)}, u32[]{:S(2)}) %collective-permute-start.33) | collective-permute-done | bytes 65568 | tf_op jit(solution)/shard_map/ppermute | solution.py:333
  219.9 0.8 collective-permute-start.23
  220.6 3.1 %collective-permute-done.23 = s32[4,32]{1,0:T(4,128)S(1)} collective-permute-done((s32[4,32]{1,0:T(4,128)S(1)}, s32[4,32]{1,0:T(4,128)S(1)}, u32[]{:S(2)}, u32[]{:S(2)}) %collective-permute-start.23) | collective-permute-done | bytes 544 | tf_op jit(solution)/shard_map/ppermute | solution.py:333
  223.8 1.2 collective-permute-start.24
  225.0 3.4 %collective-permute-done.24 = s32[8,32]{1,0:T(8,128)S(1)} collective-permute-done((s32[8,32]{1,0:T(8,128)S(1)}, s32[8,32]{1,0:T(8,128)S(1)}, u32[]{:S(2)}, u32[]{:S(2)}) %collective-permute-start.24) | collective-permute-done | bytes 1056 | tf_op jit(solution)/shard_map/ppermute | solution.py:333
  228.4 4.4 %collective-permute-start.25 = (s32[16,32]{1,0:T(8,128)S(1)}, s32[16,32]{1,0:T(8,128)S(1)}, u32[]{:S(2)}, u32[]{:S(2)}) collective-permute-start(s32[16,32]{1,0:T(8,128)S(1)} %concatenate.25), channel_id=1, source_target_pairs={{0,64},{8,72},{16,80},{24,88},{32,96},{40,104},{48,112},{56,120},{... | collective-permute-start | bytes 6152 | tf_op jit(solution)/shard_map/ppermute | solution.py:333
  232.8 3.3 %collective-permute-done.25 = s32[16,32]{1,0:T(8,128)S(1)} collective-permute-done((s32[16,32]{1,0:T(8,128)S(1)}, s32[16,32]{1,0:T(8,128)S(1)}, u32[]{:S(2)}, u32[]{:S(2)}) %collective-permute-start.25) | collective-permute-done | bytes 2080 | tf_op jit(solution)/shard_map/ppermute | solution.py:333
  236.1 0.7 pad_maximum_fusion
  236.8 1.8 near_terms.1.local_hbm
  238.6 3.7 %place_terms.1 = f32[512,256]{1,0:T(8,128)} custom-call(s32[1]{0:T(128)} %bitcast.10.me_ref, s32[32,32]{1,0:T(8,128)S(1)} %concatenate.26.cols_ref, bf16[32,128,256]{2,1,0:T(8,128)(2,1)} %all-to-all-done.2.in_hbm_ref, f32[512,256]{1,0:T(8,128)} %near_terms.1.local_hbm), custom_call_target="tpu_custom_call" | custom-call | tf_op jit(solution)/shard_map/place_terms/pallas_call | solution.py:315
  (65 shorter events, 1.0 us)
Async XLA Ops:
  0.6 53.1 %copy-start.4 = (s32[1,32,1]{1,2,0:T(1,128)S(1)}, s32[1,32,1]{1,2,0:T(1,128)}, u32[]{:S(2)}) copy-start(s32[1,32,1]{1,2,0:T(1,128)} %param.19) | copy-start | bytes 388
  0.6 36.1 %copy-start.8 = (s32[1,33]{1,0:T(1,128)S(1)}, s32[1,33]{1,0:T(1,128)}, u32[]{:S(2)}) copy-start(s32[1,33]{1,0:T(1,128)} %param.15) | copy-start | bytes 400
  0.7 53.1 %copy-start.6 = (s32[1,32,1]{1,2,0:T(1,128)S(1)}, s32[1,32,1]{1,2,0:T(1,128)}, u32[]{:S(2)}) copy-start(s32[1,32,1]{1,2,0:T(1,128)} %param.18) | copy-start | bytes 388
  0.7 53.1 %copy-start = (bf16[1,32,1,128,128]{4,3,2,1,0:T(8,128)(2,1)S(1)}, bf16[1,32,1,128,128]{4,3,2,1,0:T(8,128)(2,1)}, u32[]{:S(2)}) copy-start(bf16[1,32,1,128,128]{4,3,2,1,0:T(8,128)(2,1)} %param.17) | copy-start | bytes 3145732
  0.7 53.1 %copy-start.5 = (s32[1,16]{1,0:T(1,128)S(1)}, s32[1,16]{1,0:T(1,128)}, u32[]{:S(2)}) copy-start(s32[1,16]{1,0:T(1,128)} %param.16) | copy-start | bytes 196
  1.8 11.5 %collective-permute-start.1 = (bf16[512,256]{1,0:T(8,128)(2,1)S(1)}, bf16[512,256]{1,0:T(8,128)(2,1)S(1)}, u32[]{:S(2)}, u32[]{:S(2)}) collective-permute-start(bf16[512,256]{1,0:T(8,128)(2,1)S(1)} %convert_element_type.49.refs_0_), channel_id=1, source_target_pairs={{0,112},{8,120},{16,0},{24,8},{32,16},{40,24},{48,32},{56,40},{64,... | collective-permute-start | bytes 786440 | tf_op jit(solution)/shard_map/ppermute | solution.py:400
  7.8 9.3 %collective-permute-start = (bf16[512,256]{1,0:T(8,128)(2,1)S(1)}, bf16[512,256]{1,0:T(8,128)(2,1)S(1)}, u32[]{:S(2)}, u32[]{:S(2)}) collective-permute-start(bf16[512,256]{1,0:T(8,128)(2,1)S(1)} %convert_element_type.49.refs_0_), channel_id=1, source_target_pairs={{0,16},{8,24},{16,32},{24,40},{32,48},{40,56},{48,64},{56,72},{64,... | collective-permute-start | bytes 786440 | tf_op jit(solution)/shard_map/ppermute | solution.py:400
  13.3 8.4 %collective-permute-start.3 = (bf16[512,256]{1,0:T(8,128)(2,1)S(1)}, bf16[512,256]{1,0:T(8,128)(2,1)S(1)}, u32[]{:S(2)}, u32[]{:S(2)}) collective-permute-start(bf16[512,256]{1,0:T(8,128)(2,1)S(1)} %collective-permute-done.1.refs_2_), channel_id=1, source_target_pairs={{0,112},{8,120},{16,0},{24,8},{32,16},{40,24},{48,32},{56,40},{64,... | collective-permute-start | bytes 786440 | tf_op jit(solution)/shard_map/ppermute | solution.py:400
  17.0 8.4 %collective-permute-start.2 = (bf16[512,256]{1,0:T(8,128)(2,1)S(1)}, bf16[512,256]{1,0:T(8,128)(2,1)S(1)}, u32[]{:S(2)}, u32[]{:S(2)}) collective-permute-start(bf16[512,256]{1,0:T(8,128)(2,1)S(1)} %collective-permute-done.refs_1_), channel_id=1, source_target_pairs={{0,16},{8,24},{16,32},{24,40},{32,48},{40,56},{48,64},{56,72},{64,... | collective-permute-start | bytes 786440 | tf_op jit(solution)/shard_map/ppermute | solution.py:400
  17.7 3.0 %collective-permute-start.10 = (s32[8,32]{1,0:T(8,128)S(1)}, s32[8,32]{1,0:T(8,128)S(1)}, u32[]{:S(2)}, u32[]{:S(2)}) collective-permute-start(s32[8,32]{1,0:T(8,128)S(1)} %broadcast_in_dim.2), channel_id=1, source_target_pairs={{0,136},{8,128},{16,152},{24,144},{32,168},{40,160},{48,184},{56,1... | collective-permute-start | bytes 3080 | tf_op jit(solution)/shard_map/ppermute | solution.py:333
  17.7 3.6 %collective-permute-start.9 = (s32[8,32]{1,0:T(8,128)S(1)}, s32[8,32]{1,0:T(8,128)S(1)}, u32[]{:S(2)}, u32[]{:S(2)}) collective-permute-start(s32[8,32]{1,0:T(8,128)S(1)} %broadcast_in_dim.2), channel_id=1, source_target_pairs={{0,128},{8,136},{16,144},{24,152},{32,160},{40,168},{48,176},{56,1... | collective-permute-start | bytes 3080 | tf_op jit(solution)/shard_map/ppermute | solution.py:333
  19.3 2.0 collective-permute-start.8
  21.7 9.5 %collective-permute-start.5 = (bf16[512,256]{1,0:T(8,128)(2,1)S(1)}, bf16[512,256]{1,0:T(8,128)(2,1)S(1)}, u32[]{:S(2)}, u32[]{:S(2)}) collective-permute-start(bf16[512,256]{1,0:T(8,128)(2,1)S(1)} %collective-permute-done.3.refs_1_.refs_4_), channel_id=1, source_target_pairs={{0,112},{8,120},{16,0},{24,8},{32,16},{40,24},{48,32},{56,40},{64,... | collective-permute-start | bytes 786440 | tf_op jit(solution)/shard_map/ppermute | solution.py:400
  25.4 9.2 %collective-permute-start.4 = (bf16[512,256]{1,0:T(8,128)(2,1)S(1)}, bf16[512,256]{1,0:T(8,128)(2,1)S(1)}, u32[]{:S(2)}, u32[]{:S(2)}) collective-permute-start(bf16[512,256]{1,0:T(8,128)(2,1)S(1)} %collective-permute-done.2.refs_0_.refs_3_), channel_id=1, source_target_pairs={{0,16},{8,24},{16,32},{24,40},{32,48},{40,56},{48,64},{56,72},{64,... | collective-permute-start | bytes 786440 | tf_op jit(solution)/shard_map/ppermute | solution.py:400
  26.9 8.1 %collective-permute-start.11 = (bf16[3,128,256]{2,1,0:T(8,128)(2,1)S(1)}, bf16[3,128,256]{2,1,0:T(8,128)(2,1)S(1)}, u32[]{:S(2)}, u32[]{:S(2)}) collective-permute-start(bf16[3,128,256]{2,1,0:T(8,128)(2,1)S(1)} %get-tuple-element.18), channel_id=1, source_target_pairs={{0,8},{8,0},{16,24},{24,16},{32,40},{40,32},{48,56},{56,48},{64,72... | collective-permute-start | bytes 589832 | tf_op jit(solution)/shard_map/ppermute | solution.py:333
  27.0 11.0 %collective-permute-start.12 = (bf16[3,128,256]{2,1,0:T(8,128)(2,1)S(1)}, bf16[3,128,256]{2,1,0:T(8,128)(2,1)S(1)}, u32[]{:S(2)}, u32[]{:S(2)}) collective-permute-start(bf16[3,128,256]{2,1,0:T(8,128)(2,1)S(1)} %get-tuple-element.19), channel_id=1, source_target_pairs={{0,128},{8,136},{16,144},{24,152},{32,160},{40,168},{48,176},{56,1... | collective-permute-start | bytes 589832 | tf_op jit(solution)/shard_map/ppermute | solution.py:333
  28.7 9.8 %collective-permute-start.13 = (bf16[3,128,256]{2,1,0:T(8,128)(2,1)S(1)}, bf16[3,128,256]{2,1,0:T(8,128)(2,1)S(1)}, u32[]{:S(2)}, u32[]{:S(2)}) collective-permute-start(bf16[3,128,256]{2,1,0:T(8,128)(2,1)S(1)} %get-tuple-element.20), channel_id=1, source_target_pairs={{0,136},{8,128},{16,152},{24,144},{32,168},{40,160},{48,184},{56,1... | collective-permute-start | bytes 589832 | tf_op jit(solution)/shard_map/ppermute | solution.py:333
  31.2 10.8 %collective-permute-start.14 = (bf16[2,128,256]{2,1,0:T(8,128)(2,1)S(1)}, bf16[2,128,256]{2,1,0:T(8,128)(2,1)S(1)}, u32[]{:S(2)}, u32[]{:S(2)}) collective-permute-start(bf16[2,128,256]{2,1,0:T(8,128)(2,1)S(1)} %get-tuple-element.21), channel_id=1, source_target_pairs={{0,8},{8,0},{16,24},{24,16},{32,40},{40,32},{48,56},{56,48},{64,72... | collective-permute-start | bytes 393224 | tf_op jit(solution)/shard_map/ppermute | solution.py:333
  34.6 8.1 %collective-permute-start.7 = (bf16[256,256]{1,0:T(8,128)(2,1)S(1)}, bf16[256,256]{1,0:T(8,128)(2,1)S(1)}, u32[]{:S(2)}, u32[]{:S(2)}) collective-permute-start(bf16[256,256]{1,0:T(8,128)(2,1)S(1)} %slice.26), channel_id=1, source_target_pairs={{0,112},{8,120},{16,0},{24,8},{32,16},{40,24},{48,32},{56,40},{64,... | collective-permute-start | bytes 393224 | tf_op jit(solution)/shard_map/ppermute | solution.py:400
  35.0 6.9 %collective-permute-start.6 = (bf16[256,256]{1,0:T(8,128)(2,1)S(1)}, bf16[256,256]{1,0:T(8,128)(2,1)S(1)}, u32[]{:S(2)}, u32[]{:S(2)}) collective-permute-start(bf16[256,256]{1,0:T(8,128)(2,1)S(1)} %slice.25), channel_id=1, source_target_pairs={{0,16},{8,24},{16,32},{24,40},{32,48},{40,56},{48,64},{56,72},{64,... | collective-permute-start | bytes 393224 | tf_op jit(solution)/shard_map/ppermute | solution.py:400
  38.0 7.0 %collective-permute-start.15 = (bf16[2,128,256]{2,1,0:T(8,128)(2,1)S(1)}, bf16[2,128,256]{2,1,0:T(8,128)(2,1)S(1)}, u32[]{:S(2)}, u32[]{:S(2)}) collective-permute-start(bf16[2,128,256]{2,1,0:T(8,128)(2,1)S(1)} %get-tuple-element.22), channel_id=1, source_target_pairs={{0,128},{8,136},{16,144},{24,152},{32,160},{40,168},{48,176},{56,1... | collective-permute-start | bytes 393224 | tf_op jit(solution)/shard_map/ppermute | solution.py:333
  38.5 6.8 %collective-permute-start.16 = (bf16[2,128,256]{2,1,0:T(8,128)(2,1)S(1)}, bf16[2,128,256]{2,1,0:T(8,128)(2,1)S(1)}, u32[]{:S(2)}, u32[]{:S(2)}) collective-permute-start(bf16[2,128,256]{2,1,0:T(8,128)(2,1)S(1)} %get-tuple-element.23), channel_id=1, source_target_pairs={{0,136},{8,128},{16,152},{24,144},{32,168},{40,160},{48,184},{56,1... | collective-permute-start | bytes 393224 | tf_op jit(solution)/shard_map/ppermute | solution.py:333
  41.9 4.0 %collective-permute-start.17 = (bf16[2,128,256]{2,1,0:T(8,128)(2,1)S(1)}, bf16[2,128,256]{2,1,0:T(8,128)(2,1)S(1)}, u32[]{:S(2)}, u32[]{:S(2)}) collective-permute-start(bf16[2,128,256]{2,1,0:T(8,128)(2,1)S(1)} %get-tuple-element.24), channel_id=1, source_target_pairs={{0,8},{8,0},{16,24},{24,16},{32,40},{40,32},{48,56},{56,48},{64,72... | collective-permute-start | bytes 393224 | tf_op jit(solution)/shard_map/ppermute | solution.py:333
  42.0 7.0 %collective-permute-start.18 = (bf16[2,128,256]{2,1,0:T(8,128)(2,1)S(1)}, bf16[2,128,256]{2,1,0:T(8,128)(2,1)S(1)}, u32[]{:S(2)}, u32[]{:S(2)}) collective-permute-start(bf16[2,128,256]{2,1,0:T(8,128)(2,1)S(1)} %get-tuple-element.25), channel_id=1, source_target_pairs={{0,128},{8,136},{16,144},{24,152},{32,160},{40,168},{48,176},{56,1... | collective-permute-start | bytes 393224 | tf_op jit(solution)/shard_map/ppermute | solution.py:333
  42.7 8.3 %collective-permute-start.19 = (bf16[2,128,256]{2,1,0:T(8,128)(2,1)S(1)}, bf16[2,128,256]{2,1,0:T(8,128)(2,1)S(1)}, u32[]{:S(2)}, u32[]{:S(2)}) collective-permute-start(bf16[2,128,256]{2,1,0:T(8,128)(2,1)S(1)} %get-tuple-element.26), channel_id=1, source_target_pairs={{0,136},{8,128},{16,152},{24,144},{32,168},{40,160},{48,184},{56,1... | collective-permute-start | bytes 393224 | tf_op jit(solution)/shard_map/ppermute | solution.py:333
  45.0 5.9 %collective-permute-start.20 = (bf16[1,128,256]{2,1,0:T(8,128)(2,1)S(1)}, bf16[1,128,256]{2,1,0:T(8,128)(2,1)S(1)}, u32[]{:S(2)}, u32[]{:S(2)}) collective-permute-start(bf16[1,128,256]{2,1,0:T(8,128)(2,1)S(1)} %get-tuple-element.27), channel_id=1, source_target_pairs={{0,8},{8,0},{16,24},{24,16},{32,40},{40,32},{48,56},{56,48},{64,72... | collective-permute-start | bytes 196616 | tf_op jit(solution)/shard_map/ppermute | solution.py:333
  45.4 7.8 %collective-permute-start.21 = (bf16[1,128,256]{2,1,0:T(8,128)(2,1)S(1)}, bf16[1,128,256]{2,1,0:T(8,128)(2,1)S(1)}, u32[]{:S(2)}, u32[]{:S(2)}) collective-permute-start(bf16[1,128,256]{2,1,0:T(8,128)(2,1)S(1)} %get-tuple-element.28), channel_id=1, source_target_pairs={{0,128},{8,136},{16,144},{24,152},{32,160},{40,168},{48,176},{56,1... | collective-permute-start | bytes 196616 | tf_op jit(solution)/shard_map/ppermute | solution.py:333
  45.9 7.8 %collective-permute-start.22 = (bf16[1,128,256]{2,1,0:T(8,128)(2,1)S(1)}, bf16[1,128,256]{2,1,0:T(8,128)(2,1)S(1)}, u32[]{:S(2)}, u32[]{:S(2)}) collective-permute-start(bf16[1,128,256]{2,1,0:T(8,128)(2,1)S(1)} %get-tuple-element.29), channel_id=1, source_target_pairs={{0,136},{8,128},{16,152},{24,144},{32,168},{40,160},{48,184},{56,1... | collective-permute-start | bytes 196616 | tf_op jit(solution)/shard_map/ppermute | solution.py:333
  58.1 35.2 %copy-start.2 = (bf16[512,256]{1,0:T(8,128)(2,1)S(1)}, bf16[512,256]{1,0:T(8,128)(2,1)}, u32[]{:S(2)}) copy-start(bf16[512,256]{1,0:T(8,128)(2,1)} %ct_ref.1) | copy-start | bytes 786436
  58.1 35.1 %copy-start.3 = (bf16[256,256]{1,0:T(8,128)(2,1)S(1)}, bf16[256,256]{1,0:T(8,128)(2,1)}, u32[]{:S(2)}) copy-start(bf16[256,256]{1,0:T(8,128)(2,1)} %w_ref.1) | copy-start | bytes 393220
  58.2 35.1 %copy-start.7 = (f32[256]{0:T(256)S(1)}, f32[256]{0:T(256)}, u32[]{:S(2)}) copy-start(f32[256]{0:T(256)} %param.12) | copy-start | bytes 3076
  130.9 107.8 %all-to-all-start.2 = ((bf16[32,128,256]{2,1,0:T(8,128)(2,1)}), bf16[32,128,256]{2,1,0:T(8,128)(2,1)}, u32[]{:S(2)}, u32[]{:S(2)}) async-start(bf16[32,128,256]{2,1,0:T(8,128)(2,1)} %far_terms.1), calls=%async_computation.2 | async-start | bytes 4194304 | tf_op jit(solution)/shard_map/all_to_all | solution.py:364
  135.7 1.4 collective-permute-start.26
  135.9 100.9 %copy-start.1 = (bf16[16,128,128]{2,1,0:T(8,128)(2,1)S(1)}, bf16[16,128,128]{2,1,0:T(8,128)(2,1)}, u32[]{:S(2)}) copy-start(bf16[16,128,128]{2,1,0:T(8,128)(2,1)} %near_ref.1) | copy-start | bytes 1572868
  137.2 47.5 %collective-permute-start.27 = (bf16[128,256]{1,0:T(8,128)(2,1)S(1)}, bf16[128,256]{1,0:T(8,128)(2,1)S(1)}, u32[]{:S(2)}, u32[]{:S(2)}) collective-permute-start(bf16[128,256]{1,0:T(8,128)(2,1)S(1)} %get-tuple-element.35), channel_id=1, source_target_pairs={{0,16},{8,24},{16,0},{24,8},{32,48},{40,56},{48,32},{56,40},{64,80... | collective-permute-start | bytes 196616 | tf_op jit(solution)/shard_map/ppermute | solution.py:333
  184.7 5.9 %collective-permute-start.28 = (bf16[128,256]{1,0:T(8,128)(2,1)S(1)}, bf16[128,256]{1,0:T(8,128)(2,1)S(1)}, u32[]{:S(2)}, u32[]{:S(2)}) collective-permute-start(bf16[128,256]{1,0:T(8,128)(2,1)S(1)} %fusion), channel_id=1, source_target_pairs={{0,32},{8,40},{16,48},{24,56},{32,0},{40,8},{48,16},{56,24},{64,96... | collective-permute-start | bytes 196616 | tf_op jit(solution)/shard_map/ppermute | solution.py:333
  190.6 8.3 %collective-permute-start.29 = (bf16[128,256]{1,0:T(8,128)(2,1)S(1)}, bf16[128,256]{1,0:T(8,128)(2,1)S(1)}, u32[]{:S(2)}, u32[]{:S(2)}) collective-permute-start(bf16[128,256]{1,0:T(8,128)(2,1)S(1)} %fusion.4), channel_id=1, source_target_pairs={{0,64},{8,72},{16,80},{24,88},{32,96},{40,104},{48,112},{56,120},{... | collective-permute-start | bytes 196616 | tf_op jit(solution)/shard_map/ppermute | solution.py:333
  198.9 4.6 %collective-permute-start.30 = (bf16[128,256]{1,0:T(8,128)(2,1)S(1)}, bf16[128,256]{1,0:T(8,128)(2,1)S(1)}, u32[]{:S(2)}, u32[]{:S(2)}) collective-permute-start(bf16[128,256]{1,0:T(8,128)(2,1)S(1)} %fusion.1), channel_id=1, source_target_pairs={{0,1},{1,0},{2,3},{3,2},{4,5},{5,4},{6,7},{7,6},{8,9},{9,8},{10,11... | collective-permute-start | bytes 196616 | tf_op jit(solution)/shard_map/ppermute | solution.py:333
  203.6 5.9 %collective-permute-start.31 = (bf16[128,256]{1,0:T(8,128)(2,1)S(1)}, bf16[128,256]{1,0:T(8,128)(2,1)S(1)}, u32[]{:S(2)}, u32[]{:S(2)}) collective-permute-start(bf16[128,256]{1,0:T(8,128)(2,1)S(1)} %get-tuple-element.33), channel_id=1, source_target_pairs={{0,2},{1,3},{2,0},{3,1},{4,6},{5,7},{6,4},{7,5},{8,10},{9,11},{10,... | collective-permute-start | bytes 196616 | tf_op jit(solution)/shard_map/ppermute | solution.py:333
  209.5 4.4 %collective-permute-start.32 = (bf16[128,256]{1,0:T(8,128)(2,1)S(1)}, bf16[128,256]{1,0:T(8,128)(2,1)S(1)}, u32[]{:S(2)}, u32[]{:S(2)}) collective-permute-start(bf16[128,256]{1,0:T(8,128)(2,1)S(1)} %fusion.2), channel_id=1, source_target_pairs={{0,128},{8,136},{16,144},{24,152},{32,160},{40,168},{48,176},{56,1... | collective-permute-start | bytes 196616 | tf_op jit(solution)/shard_map/ppermute | solution.py:333
  213.8 5.9 %collective-permute-start.33 = (bf16[128,256]{1,0:T(8,128)(2,1)S(1)}, bf16[128,256]{1,0:T(8,128)(2,1)S(1)}, u32[]{:S(2)}, u32[]{:S(2)}) collective-permute-start(bf16[128,256]{1,0:T(8,128)(2,1)S(1)} %fusion.3), channel_id=1, source_target_pairs={{0,4},{1,5},{2,6},{3,7},{4,0},{5,1},{6,2},{7,3},{8,12},{9,13},{10,... | collective-permute-start | bytes 196616 | tf_op jit(solution)/shard_map/ppermute | solution.py:333
  219.7 16.3 %collective-permute-start.34 = (f32[128,256]{1,0:T(8,128)S(1)}, f32[128,256]{1,0:T(8,128)S(1)}, u32[]{:S(2)}, u32[]{:S(2)}) collective-permute-start(f32[128,256]{1,0:T(8,128)S(1)} %add_multiply_fusion), channel_id=1, source_target_pairs={{0,8},{8,0},{16,24},{24,16},{32,40},{40,32},{48,56},{56,48},{64,72... | collective-permute-start | bytes 393224 | tf_op jit(solution)/shard_map/ppermute | solution.py:333
  219.9 3.9 %collective-permute-start.23 = (s32[4,32]{1,0:T(4,128)S(1)}, s32[4,32]{1,0:T(4,128)S(1)}, u32[]{:S(2)}, u32[]{:S(2)}) collective-permute-start(s32[4,32]{1,0:T(4,128)S(1)} %pad_add_fusion.1), channel_id=1, source_target_pairs={{0,16},{8,24},{16,0},{24,8},{32,48},{40,56},{48,32},{56,40},{64,80... | collective-permute-start | bytes 1544 | tf_op jit(solution)/shard_map/ppermute | solution.py:333
  223.8 4.6 %collective-permute-start.24 = (s32[8,32]{1,0:T(8,128)S(1)}, s32[8,32]{1,0:T(8,128)S(1)}, u32[]{:S(2)}, u32[]{:S(2)}) collective-permute-start(s32[8,32]{1,0:T(8,128)S(1)} %concatenate.24), channel_id=1, source_target_pairs={{0,32},{8,40},{16,48},{24,56},{32,0},{40,8},{48,16},{56,24},{64,96... | collective-permute-start | bytes 3080 | tf_op jit(solution)/shard_map/ppermute | solution.py:333
  228.4 7.6 %collective-permute-start.25 = (s32[16,32]{1,0:T(8,128)S(1)}, s32[16,32]{1,0:T(8,128)S(1)}, u32[]{:S(2)}, u32[]{:S(2)}) collective-permute-start(s32[16,32]{1,0:T(8,128)S(1)} %concatenate.25), channel_id=1, source_target_pairs={{0,64},{8,72},{16,80},{24,88},{32,96},{40,104},{48,112},{56,120},{... | collective-permute-start | bytes 6152 | tf_op jit(solution)/shard_map/ppermute | solution.py:333

commit v4 on v3

--- a/solution.py
+++ b/solution.py
@@ -50,38 +50,26 @@
 STAGES = ((0, -1, 1), (-2, 2), (-3, 3), (4,))
 
 
-def anywhere():
-    return pl.BlockSpec(memory_space=pl.ANY)
-
-
 def pick_blocks(place, peer_cols, sources, offsets, z_count, tile):
     width = sources[0].shape[1]
     count = len(offsets)
     peers = peer_cols.shape[0]
 
     def kernel(place_ref, cols_ref, *refs):
-        src, out, sem = refs[:count], refs[count:-1], refs[-1]
+        src, out = refs[:count], refs[count:]
         rest, z, core = place_ref[0], place_ref[1], place_ref[2]
-        copies = []
         for q in range(peers):
             for n, offset in enumerate(offsets):
                 k = rest + lax.rem(z + offset + z_count, z_count) * 2 + core
                 at = pl.multiple_of(cols_ref[q, k] * tile, tile)
-                copy = pltpu.make_async_copy(
-                    src[n].at[pl.ds(at, tile), :], out[q].at[n], sem.at[q, n]
-                )
-                copy.start()
-                copies.append(copy)
-        for copy in copies:
-            copy.wait()
+                out[q][n] = src[n][pl.ds(at, tile), :]
 
     return pl.pallas_call(
         kernel,
         grid=(1,),
-        in_specs=[smem(), smem()] + [anywhere()] * count,
-        out_specs=[anywhere()] * peers,
+        in_specs=[smem(), smem()] + [whole(a.shape) for a in sources],
+        out_specs=[whole((count, tile, width))] * peers,
         out_shape=[jax.ShapeDtypeStruct((count, tile, width), BF16)] * peers,
-        scratch_shapes=[pltpu.SemaphoreType.DMA((peers, count))],
         compiler_params=params(),
         name="pick_blocks",
     )(place, peer_cols, *sources)
@@ -167,9 +155,8 @@
     peers, rows, width = parts.shape
     chunk = 256
 
-    def kernel(parts_ref, w_ref, b_ref, ct_ref, hid_ref, grads_ref, wt_ref, rows_ref, sem):
+    def kernel(parts_ref, w_ref, b_ref, ct_ref, hid_ref, grads_ref, wt_ref):
         step = pl.program_id(0)
-        last = rows // chunk - 1
         total = parts_ref[0].astype(F32)
         for j in range(1, peers):
             total = total + parts_ref[j].astype(F32)
@@ -182,14 +169,7 @@
         grad_rows = lax.dot_general(
             grad_pre, w, (((1,), (1,)), ((), ())), preferred_element_type=F32
         ).astype(BF16)
-        at = pl.ds(pl.multiple_of(step * chunk, chunk), chunk)
-        rows_ref[at, :] = grad_rows
-        copies = [
-            pltpu.make_async_copy(rows_ref.at[at, :], grads_ref.at[j, at, :], sem.at[step, j])
-            for j in range(peers)
-        ]
-        for copy in copies:
-            copy.start()
+        grads_ref[...] = grad_rows
         term = transposed_dot(summed, grad_pre)
 
         @pl.when(step == 0)
@@ -199,15 +179,6 @@
         @pl.when(step != 0)
         def _():
             wt_ref[...] += term
-
-        @pl.when(step == last)
-        def _():
-            for i in range(last + 1):
-                part = pl.ds(i * chunk, chunk)
-                for j in range(peers):
-                    pltpu.make_async_copy(
-                        rows_ref.at[part, :], grads_ref.at[j, part, :], sem.at[i, j]
-                    ).wait()
 
     return pl.pallas_call(
         kernel,
@@ -220,28 +191,47 @@
         ],
         out_specs=[
             stepped((chunk, width)),
-            hbm(),
+            stepped((chunk, width)),
             whole((width, width)),
         ],
         out_shape=[
             jax.ShapeDtypeStruct((rows, width), BF16),
-            pltpu.HBM((peers, rows, width), BF16),
+            jax.ShapeDtypeStruct((rows, width), BF16),
             jax.ShapeDtypeStruct((width, width), F32),
         ],
-        scratch_shapes=[
-            pltpu.VMEM((rows, width), BF16),
-            pltpu.SemaphoreType.DMA((rows // chunk, peers)),
-        ],
         compiler_params=params(),
         name="dense_stage",
     )(parts, weight, bias, cotangent)
 
 
-def far_terms(far_rows, group_grad, far_tiles, tile):
+def lay_out(owner_ref, shards, group_ref):
+    size = sum(ref.shape[0] for ref in shards[0])
+    for n, refs in enumerate(shards):
+        start = owner_ref[n] * size
+        for ref in refs:
+            rows = ref.shape[0]
+            group_ref[pl.ds(pl.multiple_of(start, rows), rows), :] = ref[...]
+            start = start + rows
+
+
+def in_pairs(refs, layout):
+    taken, out = 0, []
+    for count in layout:
+        out.append(refs[taken : taken + count])
+        taken += count
+    return out
+
+
+def far_terms(far_rows, owners, shards, far_tiles, tile):
     dom_count = far_tiles.shape[0]
-    width = group_grad.shape[1]
-
-    def kernel(frow_ref, grad_ref, far_ref, out_ref, terms_ref, sem):
+    flat = [a for shard in shards for a in shard]
+    layout = [len(shard) for shard in shards]
+    width = flat[0].shape[1]
+    group_rows = sum(a.shape[0] for a in flat)
+
+    def kernel(frow_ref, owner_ref, *refs):
+        far_ref, out_ref, terms_ref, grad_ref, sem = refs[len(flat) :]
+        lay_out(owner_ref, in_pairs(refs, layout), grad_ref)
         copies = []
         for k in range(dom_count):
             row = frow_ref[k]
@@ -257,23 +247,29 @@
     return pl.pallas_call(
         kernel,
         grid=(1,),
-        in_specs=[smem(), whole(group_grad.shape), whole(far_tiles.shape)],
+        in_specs=[smem(), smem()] + [whole(a.shape) for a in flat] + [whole(far_tiles.shape)],
         out_specs=hbm(),
         out_shape=pltpu.HBM((dom_count, tile, width), BF16),
         scratch_shapes=[
             pltpu.VMEM((dom_count, tile, width), BF16),
+            pltpu.VMEM((group_rows, width), BF16),
             pltpu.SemaphoreType.DMA((dom_count,)),
         ],
         compiler_params=params(),
         name="far_terms",
-    )(far_rows, group_grad, far_tiles)
-
-
-def near_terms(near_rows, near_cols, group_grad, near_tiles, rows_dev):
+    )(far_rows, owners, *flat, far_tiles)
+
+
+def near_terms(near_rows, near_cols, owners, shards, near_tiles, rows_dev):
     near_count, tile, _ = near_tiles.shape
-    width = group_grad.shape[1]
-
-    def kernel(nrow_ref, ncol_ref, grad_ref, near_ref, out_ref):
+    flat = [a for shard in shards for a in shard]
+    layout = [len(shard) for shard in shards]
+    width = flat[0].shape[1]
+    group_rows = sum(a.shape[0] for a in flat)
+
+    def kernel(nrow_ref, ncol_ref, owner_ref, *refs):
+        near_ref, out_ref, grad_ref = refs[len(flat) :]
+        lay_out(owner_ref, in_pairs(refs, layout), grad_ref)
         out_ref[...] = jnp.zeros_like(out_ref)
         for q in range(near_count):
             src = pl.ds(pl.multiple_of(nrow_ref[q] * tile, tile), tile)
@@ -283,54 +279,65 @@
     return pl.pallas_call(
         kernel,
         grid=(1,),
-        in_specs=[smem(), smem(), whole(group_grad.shape), whole(near_tiles.shape)],
+        in_specs=[smem()] * 3 + [whole(a.shape) for a in flat] + [whole(near_tiles.shape)],
         out_specs=whole((rows_dev, width)),
         out_shape=pltpu.HBM((rows_dev, width), F32),
+        scratch_shapes=[pltpu.VMEM((group_rows, width), BF16)],
         compiler_params=params(),
         name="near_terms",
-    )(near_rows, near_cols, group_grad, near_tiles)
+    )(near_rows, near_cols, owners, *flat, near_tiles)
 
 
 def place_terms(me, group_cols, masks, arrived, local):
-    dom_count, tile, _ = arrived.shape
-
-    def kernel(me_ref, cols_ref, in_hbm_ref, local_hbm, out_ref, in_ref, local_ref, sem, in_sem):
+    _, tile, _ = arrived.shape
+
+    def kernel(me_ref, cols_ref, in_ref, local_hbm, out_ref, local_ref, sem):
         fetch = pltpu.make_async_copy(local_hbm, local_ref, sem)
         fetch.start()
         here = me_ref[0]
-        copies = []
+        out_ref[...] = jnp.zeros_like(out_ref)
         for n, mask in enumerate(masks):
-            d = lax.bitwise_xor(here, mask)
-            copy = pltpu.make_async_copy(in_hbm_ref.at[d], in_ref.at[n], in_sem.at[n])
-            copy.start()
-            copies.append(copy)
-        out_ref[...] = jnp.zeros_like(out_ref)
-        for n in range(dom_count):
-            copies[n].wait()
             at = pl.ds(pl.multiple_of(cols_ref[n, here] * tile, tile), tile)
-            out_ref[at, :] += in_ref[n].astype(F32)
+            out_ref[at, :] += in_ref[lax.bitwise_xor(here, mask)].astype(F32)
         fetch.wait()
         out_ref[...] += local_ref[...]
 
     return pl.pallas_call(
         kernel,
         grid=(1,),
-        in_specs=[smem(), smem(), hbm(), hbm()],
+        in_specs=[smem(), smem(), whole(arrived.shape), hbm()],
         out_specs=whole(local.shape),
         out_shape=jax.ShapeDtypeStruct(local.shape, F32),
-        scratch_shapes=[
-            pltpu.VMEM(arrived.shape, BF16),
-            pltpu.VMEM(local.shape, F32),
-            pltpu.SemaphoreType.DMA,
-            pltpu.SemaphoreType.DMA((dom_count,)),
-        ],
+        scratch_shapes=[pltpu.VMEM(local.shape, F32), pltpu.SemaphoreType.DMA],
         compiler_params=params(),
         name="place_terms",
-    )(me, group_cols, in_hbm(arrived), in_hbm(local))
+    )(me, group_cols, pltpu.with_memory_space_constraint(arrived, pltpu.VMEM), in_hbm(local))
 
 
 def swap(values, axis, count, bit):
     return lax.ppermute(values, axis, [(i, i ^ bit) for i in range(count)])
+
+
+def gather_group(own, repl_count):
+    x_count = repl_count // 2
+    half = own.shape[0] // 2
+
+    def along_x(values, shift):
+        pairs = [
+            (i, i // x_count * x_count + (i + shift) % x_count) for i in range(repl_count)
+        ]
+        return lax.ppermute(values, "repl", pairs)
+
+    low, high = along_x(own, 1), along_x(own, -1)
+    mate = swap(own, "repl", repl_count, x_count)
+    far = (along_x(low[:half], 1), along_x(high[half:], -1))
+    mate_low, mate_high = along_x(mate, 1), along_x(mate, -1)
+    mate_far = (along_x(mate_low[:half], 1), along_x(mate_high[half:], -1))
+    shards = ((own,), (low,), (high,), far, (mate,), (mate_low,), (mate_high,), mate_far)
+    here = lax.axis_index("repl")
+    x, line = here % x_count, here // x_count * x_count
+    owners = [start + (x + d) % x_count for start in (line, x_count - line) for d in (0, -1, 1, 2)]
+    return shards, jnp.stack(owners)
 
 
 def meet(values, axis, count, bit):
@@ -344,16 +351,16 @@
     kept = lax.dynamic_slice_in_dim(values, core * half, half, 0)
     sent = lax.dynamic_slice_in_dim(values, (1 - core) * half, half, 0)
     values = kept + swap(sent, "dom", dom_count, 1)
-    bit = 2
-    while bit < dom_count // 2:
+    bit = dom_count // 4
+    while bit > 1:
         values = meet(values, "dom", dom_count, bit)
-        bit *= 2
+        bit //= 2
     bit = 1
     while bit < repl_count // 2:
-        values = meet(values, "repl", repl_count, bit)
+        values = values + swap(values, "repl", repl_count, bit)
         bit *= 2
-    values = meet(values, "dom", dom_count, dom_count // 2)
-    values = meet(values, "repl", repl_count, repl_count // 2) * scale
+    values = values + swap(values, "dom", dom_count, dom_count // 2)
+    values = (values + swap(values, "repl", repl_count, repl_count // 2)) * scale
     other = swap(values, "dom", dom_count, 1)
     first = jnp.where(core == 0, values, other)
     second = jnp.where(core == 0, other, values)
@@ -438,14 +445,14 @@
     parts = exchange(partial.reshape(repl_count, rows_dev, width), "repl")
     hidden, grads, weight_term = dense_stage(parts, weight, bias_vector.reshape(1, width), cotangent)
 
-    group_grad = exchange(grads, "repl").reshape(blocks_dom * tile, width)
-    terms = far_terms(frow, group_grad, tiles, tile)
+    shards, owners = gather_group(grads, repl_count)
+    terms = far_terms(frow, owners, shards, tiles, tile)
     far_back = exchange(terms, "dom")
 
     node_total = rows_dev * dom_count * repl_count
     weight_grad = total_over_all(weight_term, 1.0 / math.sqrt(node_total), dom_count, repl_count)
 
-    local = near_terms(nrow, ncol, group_grad, near_tiles, rows_dev)
+    local = near_terms(nrow, ncol, owners, shards, near_tiles, rows_dev)
     grad_features = place_terms(here.reshape(1), group_cols, known, far_back, local)
     return (hidden, grad_features, weight_grad)
 

time: 244 us -> 256 us (1.049)
  blocking collectives: 67.5 us -> 35.5 us
  waiting for transfers between devices: 100 us -> 117 us
  local copies, waits for them, and re-layouts: 0.9 us -> 17.3 us
  starting transfers between devices: 50.5 us -> 61.7 us
  Pallas kernels: 19.8 us -> 15.6 us
    all_to_all x2 -> x1, blocking collectives: 67.5 us -> 35.5 us  [exchange(): return lax.all_to_all(values, axes, 0, 0, tiled=True)]
    ppermute x27 -> x28, waiting for transfers between devices: 88.2 us -> 102 us  [swap(): return lax.ppermute(values, axis, [(i, i ^ bit) for i in range(count)])]
    ppermute x0 -> x8, starting transfers between devices: none -> 10.1 us  [along_x(): return lax.ppermute(values, 'repl', pairs)]
    unnamed x19 -> x65, local copies, waits for them, and re-layouts: 0.06 us -> 7.66 us
    ppermute x0 -> x8, waiting for transfers between devices: none -> 5.44 us  [along_x(): return lax.ppermute(values, 'repl', pairs)]
    concatenate x3, local copies, waits for them, and re-layouts: 0.07 us -> 5.15 us  [on_device(): group_cols = jnp.concatenate([group_cols, other], axis=0)]
    pallas_call x7, Pallas kernels: 12.6 us -> 9.51 us  [the longest x1 2.7 us: place_terms(): pl.pallas_call(kernel, grid=(1,), in_specs=[smem(), smem(), whole(arrived...]
    ppermute x8, waiting for transfers between devices: 12.2 us -> 9.61 us  [along_z(): return lax.ppermute(values, 'dom', pairs)]
  transfers between devices with their start and end apart: 36 -> 45, of which waited for: 22 -> 26; matrix products, arithmetic and copies ran while one was open for 1% -> 5% of each run, Pallas kernels for 3% -> 2%
where the time goes in v4:
time: 256 us; the launch traced here: 254 us
  waiting for transfers between devices  117 us (46%)
  starting transfers between devices  61.7 us (24%)
  blocking collectives  35.5 us (14%)
  local copies, waits for them, and re-layouts  17.3 us (7%)
  Pallas kernels  15.6 us (6%)
  other arithmetic  4.85 us (2%)
    ppermute x28, waiting for transfers between devices, swap(): return lax.ppermute(values, axis, [(i, i ^ bit) for i in range(count)])  102 us
    all_to_all x1, blocking collectives, exchange(): return lax.all_to_all(values, axes, 0, 0, tiled=True)  35.5 us
    ppermute x28, starting transfers between devices, swap(): return lax.ppermute(values, axis, [(i, i ^ bit) for i in range(count)])  29.9 us
    ppermute x8, starting transfers between devices, along_z(): return lax.ppermute(values, 'dom', pairs)  15.9 us
    ppermute x8, starting transfers between devices, along_x(): return lax.ppermute(values, 'repl', pairs)  10.1 us
    ppermute x8, waiting for transfers between devices, along_z(): return lax.ppermute(values, 'dom', pairs)  9.61 us
    unnamed x65, local copies, waits for them, and re-layouts  7.66 us
    all_to_all x1, starting transfers between devices, exchange(): return lax.all_to_all(values, axes, 0, 0, tiled=True)  5.75 us
  transfers between devices with their start and end apart: 45, of which 26 were waited for; matrix products, arithmetic and copies ran while one was open for 5% of the time, Pallas kernels for 2%

profile of v4, /device:TPU:2, one launch (start us, length us, event | category | flops | bytes accessed | tf_op | source)
XLA Modules:
  0.0 253.5 jit_solution(2229374603134230747)
XLA Ops:
  0.7 1.2 convert_element_type.25.refs_0_
  1.8 2.0 collective-permute-start
  3.8 4.0 %collective-permute-start.1 = (bf16[512,256]{1,0:T(8,128)(2,1)S(1)}, bf16[512,256]{1,0:T(8,128)(2,1)S(1)}, u32[]{:S(2)}, u32[]{:S(2)}) collective-permute-start(bf16[512,256]{1,0:T(8,128)(2,1)S(1)} %convert_element_type.25.refs_0_), channel_id=1, source_target_pairs={{0,112},{8,120},{16,0},{24,8},{32,16},{40,24},{48,32},{56,40},{64,... | collective-permute-start | bytes 786440 | tf_op jit(solution)/shard_map/ppermute | solution.py:407
  7.9 6.2 %collective-permute-done.refs_1_ = bf16[512,256]{1,0:T(8,128)(2,1)S(1)} collective-permute-done((bf16[512,256]{1,0:T(8,128)(2,1)S(1)}, bf16[512,256]{1,0:T(8,128)(2,1)S(1)}, u32[]{:S(2)}, u32[]{:S(2)}) %collective-permute-start) | collective-permute-done | bytes 262176 | tf_op jit(solution)/shard_map/ppermute | solution.py:407
  14.1 3.2 %collective-permute-start.3 = (bf16[512,256]{1,0:T(8,128)(2,1)S(1)}, bf16[512,256]{1,0:T(8,128)(2,1)S(1)}, u32[]{:S(2)}, u32[]{:S(2)}) collective-permute-start(bf16[512,256]{1,0:T(8,128)(2,1)S(1)} %collective-permute-done.1.refs_2_), channel_id=1, source_target_pairs={{0,112},{8,120},{16,0},{24,8},{32,16},{40,24},{48,32},{56,40},{64,... | collective-permute-start | bytes 786440 | tf_op jit(solution)/shard_map/ppermute | solution.py:407
  18.0 1.6 collective-permute-start.9
  19.9 1.7 collective-permute-done.9
  21.6 1.0 collective-permute-done.10
  22.8 3.2 %collective-permute-start.5 = (bf16[512,256]{1,0:T(8,128)(2,1)S(1)}, bf16[512,256]{1,0:T(8,128)(2,1)S(1)}, u32[]{:S(2)}, u32[]{:S(2)}) collective-permute-start(bf16[512,256]{1,0:T(8,128)(2,1)S(1)} %collective-permute-done.3.refs_1_.refs_4_), channel_id=1, source_target_pairs={{0,112},{8,120},{16,0},{24,8},{32,16},{40,24},{48,32},{56,40},{64,... | collective-permute-start | bytes 786440 | tf_op jit(solution)/shard_map/ppermute | solution.py:407
  26.7 1.7 collective-permute-start.12
  29.2 3.2 %collective-permute-done.4.refs_0_.refs_5_ = bf16[512,256]{1,0:T(8,128)(2,1)S(1)} collective-permute-done((bf16[512,256]{1,0:T(8,128)(2,1)S(1)}, bf16[512,256]{1,0:T(8,128)(2,1)S(1)}, u32[]{:S(2)}, u32[]{:S(2)}) %collective-permute-start.4) | collective-permute-done | bytes 262176 | tf_op jit(solution)/shard_map/ppermute | solution.py:407
  32.5 3.3 %collective-permute-start.7 = (bf16[256,256]{1,0:T(8,128)(2,1)S(1)}, bf16[256,256]{1,0:T(8,128)(2,1)S(1)}, u32[]{:S(2)}, u32[]{:S(2)}) collective-permute-start(bf16[256,256]{1,0:T(8,128)(2,1)S(1)} %slice.42), channel_id=1, source_target_pairs={{0,112},{8,120},{16,0},{24,8},{32,16},{40,24},{48,32},{56,40},{64,... | collective-permute-start | bytes 393224 | tf_op jit(solution)/shard_map/ppermute | solution.py:407
  36.5 0.8 collective-permute-start.15
  37.7 1.9 collective-permute-start.16
  39.6 1.0 collective-permute-start.18
  40.6 1.2 collective-permute-start.19
  43.0 0.8 collective-permute-done.16.refs_13_
  43.7 1.6 collective-permute-start.21
  45.3 1.6 collective-permute-start.22
  47.1 1.5 collective-permute-done.18.refs_15_
  48.6 0.8 collective-permute-done.19.refs_16_
  49.4 3.1 %collective-permute-done.21.refs_18_ = bf16[1,128,256]{2,1,0:T(8,128)(2,1)S(1)} collective-permute-done((bf16[1,128,256]{2,1,0:T(8,128)(2,1)S(1)}, bf16[1,128,256]{2,1,0:T(8,128)(2,1)S(1)}, u32[]{:S(2)}, u32[]{:S(2)}) %collective-permute-start.21) | collective-permute-done | bytes 65568 | tf_op jit(solution)/shard_map/ppermute | solution.py:318
  52.5 4.3 %aggregate.1 = bf16[4096,256]{1,0:T(8,128)(2,1)} custom-call(s32[3]{0:T(128)S(1)} %pad_add_fusion.2.place_ref, s32[32]{0:T(128)S(1)} %bitcast.29, s32[32]{0:T(128)S(1)} %bitcast.25, s32[16]{0:T(128)S(1)} %convert_reduce_fusion.nrow_ref, s32[16]{0:T(128)S(1)} %bitcast.31, bf16[512,256]{1,0:T(8,128)(2,1)S(1)} %convert_element_type.25.refs_0_, ...), custom_call_target="tpu_custom_call" | custom-call | tf_op jit(solution)/shard_map/aggregate/pallas_call | solution.py:136
  56.9 35.5 %all_to_all.10.parts_ref = bf16[8,512,256]{2,1,0:T(8,128)(2,1)S(1)} all-to-all(bf16[8,512,256]{2,1,0:T(8,128)(2,1)} %bitcast.34), channel_id=1, replica_groups=mesh['dom'=32,'repl'=8] {'repl'}, dimensions={0} | all-to-all | bytes 4194304 | tf_op jit(solution)/shard_map/all_to_all | solution.py:371
  92.4 1.8 dense_stage.1
  94.7 2.0 collective-permute-start.27
  96.8 6.2 %collective-permute-done.30.refs_5_ = bf16[512,256]{1,0:T(8,128)(2,1)S(1)} collective-permute-done((bf16[512,256]{1,0:T(8,128)(2,1)S(1)}, bf16[512,256]{1,0:T(8,128)(2,1)S(1)}, u32[]{:S(2)}, u32[]{:S(2)}) %collective-permute-start.30) | collective-permute-done | bytes 262176 | tf_op jit(solution)/shard_map/ppermute | solution.py:318
  103.4 1.6 collective-permute-start.32
  106.2 2.6 %collective-permute-start.29 = (bf16[256,256]{1,0:T(8,128)(2,1)}, bf16[256,256]{1,0:T(8,128)(2,1)S(1)}, u32[]{:S(2)}, u32[]{:S(2)}) collective-permute-start(bf16[256,256]{1,0:T(8,128)(2,1)} %slice.44), channel_id=1, source_target_pairs={{0,3},{1,0},{2,1},{3,2},{4,7},{5,4},{6,5},{7,6},{8,11},{9,8},{10,9... | collective-permute-start | bytes 393224 | tf_op jit(solution)/shard_map/ppermute | solution.py:329
  108.8 2.7 %collective-permute-done.31.refs_6_ = bf16[512,256]{1,0:T(8,128)(2,1)S(1)} collective-permute-done((bf16[512,256]{1,0:T(8,128)(2,1)S(1)}, bf16[512,256]{1,0:T(8,128)(2,1)S(1)}, u32[]{:S(2)}, u32[]{:S(2)}) %collective-permute-start.31) | collective-permute-done | bytes 262176 | tf_op jit(solution)/shard_map/ppermute | solution.py:329
  113.0 2.8 %collective-permute-start.34 = (bf16[256,256]{1,0:T(8,128)(2,1)}, bf16[256,256]{1,0:T(8,128)(2,1)S(1)}, u32[]{:S(2)}, u32[]{:S(2)}) collective-permute-start(bf16[256,256]{1,0:T(8,128)(2,1)} %slice.46), channel_id=1, source_target_pairs={{0,3},{1,0},{2,1},{3,2},{4,7},{5,4},{6,5},{7,6},{8,11},{9,8},{10,9... | collective-permute-start | bytes 393224 | tf_op jit(solution)/shard_map/ppermute | solution.py:329
  116.0 2.3 collective-permute-done.33.refs_8_
  118.7 2.5 far_terms.1
  121.2 5.8 %all-to-all-start.1 = ((bf16[32,128,256]{2,1,0:T(8,128)(2,1)}), bf16[32,128,256]{2,1,0:T(8,128)(2,1)S(1)}, u32[]{:S(2)}, u32[]{:S(2)}) async-start(bf16[32,128,256]{2,1,0:T(8,128)(2,1)} %far_terms.1), calls=%async_computation.1 | async-start | bytes 4194304 | tf_op jit(solution)/shard_map/all_to_all | solution.py:371
  127.0 1.6 constant_dynamic-slice_fusion
  128.9 1.4 collective-permute-done.35
  130.3 1.0 fusion.2
  131.3 5.8 %collective-permute-start.36 = (bf16[128,256]{1,0:T(8,128)(2,1)S(1)}, bf16[128,256]{1,0:T(8,128)(2,1)S(1)}, u32[]{:S(2)}, u32[]{:S(2)}) collective-permute-start(bf16[128,256]{1,0:T(8,128)(2,1)S(1)} %get-tuple-element.33), channel_id=1, source_target_pairs={{0,64},{8,72},{16,80},{24,88},{32,96},{40,104},{48,112},{56,120},{... | collective-permute-start | bytes 196616 | tf_op jit(solution)/shard_map/ppermute | solution.py:318
  137.1 44.4 %collective-permute-done.36 = bf16[128,256]{1,0:T(8,128)(2,1)S(1)} collective-permute-done((bf16[128,256]{1,0:T(8,128)(2,1)S(1)}, bf16[128,256]{1,0:T(8,128)(2,1)S(1)}, u32[]{:S(2)}, u32[]{:S(2)}) %collective-permute-start.36) | collective-permute-done | bytes 65568 | tf_op jit(solution)/shard_map/ppermute | solution.py:318
  181.6 6.0 %collective-permute-done.37 = bf16[128,256]{1,0:T(8,128)(2,1)S(1)} collective-permute-done((bf16[128,256]{1,0:T(8,128)(2,1)S(1)}, bf16[128,256]{1,0:T(8,128)(2,1)S(1)}, u32[]{:S(2)}, u32[]{:S(2)}) %collective-permute-start.37) | collective-permute-done | bytes 65568 | tf_op jit(solution)/shard_map/ppermute | solution.py:318
  187.7 4.3 %collective-permute-done.38 = bf16[128,256]{1,0:T(8,128)(2,1)S(1)} collective-permute-done((bf16[128,256]{1,0:T(8,128)(2,1)S(1)}, bf16[128,256]{1,0:T(8,128)(2,1)S(1)}, u32[]{:S(2)}, u32[]{:S(2)}) %collective-permute-start.38) | collective-permute-done | bytes 65568 | tf_op jit(solution)/shard_map/ppermute | solution.py:318
  192.0 3.3 %collective-permute-start.39 = (f32[128,256]{1,0:T(8,128)S(1)}, f32[128,256]{1,0:T(8,128)S(1)}, u32[]{:S(2)}, u32[]{:S(2)}) collective-permute-start(f32[128,256]{1,0:T(8,128)S(1)} %convert_add_fusion), channel_id=1, source_target_pairs={{0,1},{1,0},{2,3},{3,2},{4,5},{5,4},{6,7},{7,6},{8,9},{9,8},{10,11... | collective-permute-start | bytes 393224 | tf_op jit(solution)/shard_map/ppermute | solution.py:318
  195.3 2.9 %collective-permute-done.39 = f32[128,256]{1,0:T(8,128)S(1)} collective-permute-done((f32[128,256]{1,0:T(8,128)S(1)}, f32[128,256]{1,0:T(8,128)S(1)}, u32[]{:S(2)}, u32[]{:S(2)}) %collective-permute-start.39) | collective-permute-done | bytes 131104 | tf_op jit(solution)/shard_map/ppermute | solution.py:318
  198.3 4.5 %collective-permute-start.40 = (f32[128,256]{1,0:T(8,128)S(1)}, f32[128,256]{1,0:T(8,128)S(1)}, u32[]{:S(2)}, u32[]{:S(2)}) collective-permute-start(f32[128,256]{1,0:T(8,128)S(1)} %add.120), channel_id=1, source_target_pairs={{0,2},{1,3},{2,0},{3,1},{4,6},{5,7},{6,4},{7,5},{8,10},{9,11},{10,... | collective-permute-start | bytes 393224 | tf_op jit(solution)/shard_map/ppermute | solution.py:318
  202.8 2.9 %collective-permute-done.40 = f32[128,256]{1,0:T(8,128)S(1)} collective-permute-done((f32[128,256]{1,0:T(8,128)S(1)}, f32[128,256]{1,0:T(8,128)S(1)}, u32[]{:S(2)}, u32[]{:S(2)}) %collective-permute-start.40) | collective-permute-done | bytes 131104 | tf_op jit(solution)/shard_map/ppermute | solution.py:318
  205.8 5.0 %collective-permute-done.41 = f32[128,256]{1,0:T(8,128)S(1)} collective-permute-done((f32[128,256]{1,0:T(8,128)S(1)}, f32[128,256]{1,0:T(8,128)S(1)}, u32[]{:S(2)}, u32[]{:S(2)}) %collective-permute-start.41) | collective-permute-done | bytes 131104 | tf_op jit(solution)/shard_map/ppermute | solution.py:318
  210.8 2.2 collective-permute-start.42
  213.0 4.4 %collective-permute-done.42 = f32[128,256]{1,0:T(8,128)S(1)} collective-permute-done((f32[128,256]{1,0:T(8,128)S(1)}, f32[128,256]{1,0:T(8,128)S(1)}, u32[]{:S(2)}, u32[]{:S(2)}) %collective-permute-start.42) | collective-permute-done | bytes 131104 | tf_op jit(solution)/shard_map/ppermute | solution.py:318
  218.5 3.2 %collective-permute-done.23 = s32[4,32]{1,0:T(4,128)S(1)} collective-permute-done((s32[4,32]{1,0:T(4,128)S(1)}, s32[4,32]{1,0:T(4,128)S(1)}, u32[]{:S(2)}, u32[]{:S(2)}) %collective-permute-start.23) | collective-permute-done | bytes 544 | tf_op jit(solution)/shard_map/ppermute | solution.py:318
  221.7 1.2 concatenate.24
  222.9 4.7 %collective-permute-done.24 = s32[8,32]{1,0:T(8,128)S(1)} collective-permute-done((s32[8,32]{1,0:T(8,128)}, s32[8,32]{1,0:T(8,128)S(1)}, u32[]{:S(2)}, u32[]{:S(2)}) %collective-permute-start.24) | collective-permute-done | bytes 1056 | tf_op jit(solution)/shard_map/ppermute | solution.py:318
  227.6 1.9 concatenate.25
  229.5 0.8 collective-permute-start.25
  230.3 7.1 %collective-permute-done.25 = s32[16,32]{1,0:T(8,128)} collective-permute-done((s32[16,32]{1,0:T(8,128)}, s32[16,32]{1,0:T(8,128)}, u32[]{:S(2)}, u32[]{:S(2)}) %collective-permute-start.25) | collective-permute-done | bytes 2080 | tf_op jit(solution)/shard_map/ppermute | solution.py:318
  237.4 2.1 concatenate.26.cols_ref
  239.5 0.9 copy-done.3
  240.4 0.9 copy-done.5
  241.4 0.9 copy-done.7
  242.3 0.9 copy-done.9
  243.2 0.9 copy-done.11
  244.1 0.9 copy-done.13
  247.0 1.9 near_terms.1.local_hbm
  249.0 1.0 broadcast_select_fusion.1
  250.7 2.7 %place_terms.1 = f32[512,256]{1,0:T(8,128)} custom-call(s32[1]{0:T(128)} %bitcast.10.me_ref, s32[32,32]{1,0:T(8,128)S(1)} %concatenate.26.cols_ref, bf16[32,128,256]{2,1,0:T(8,128)(2,1)S(1)} %all-to-all-done.1.in_ref, f32[512,256]{1,0:T(8,128)} %near_terms.1.local_hbm), custom_call_target="tpu_custom_call" | custom-call | tf_op jit(solution)/shard_map/place_terms/pallas_call | solution.py:305
  (133 shorter events, 14.1 us)
Async XLA Ops:
  0.6 51.9 %copy-start.17 = (s32[1,32,1]{1,2,0:T(1,128)S(1)}, s32[1,32,1]{1,2,0:T(1,128)}, u32[]{:S(2)}) copy-start(s32[1,32,1]{1,2,0:T(1,128)} %param.19) | copy-start | bytes 388
  0.6 35.2 %copy-start.31 = (s32[1,33]{1,0:T(1,128)S(1)}, s32[1,33]{1,0:T(1,128)}, u32[]{:S(2)}) copy-start(s32[1,33]{1,0:T(1,128)} %param.15) | copy-start | bytes 400
  0.7 51.9 %copy-start.20 = (s32[1,32,1]{1,2,0:T(1,128)S(1)}, s32[1,32,1]{1,2,0:T(1,128)}, u32[]{:S(2)}) copy-start(s32[1,32,1]{1,2,0:T(1,128)} %param.18) | copy-start | bytes 388
  0.7 51.8 %copy-start.21 = (s32[1,16]{1,0:T(1,128)S(1)}, s32[1,16]{1,0:T(1,128)}, u32[]{:S(2)}) copy-start(s32[1,16]{1,0:T(1,128)} %param.16) | copy-start | bytes 196
  0.7 51.8 %copy-start = (bf16[1,32,1,128,128]{4,3,2,1,0:T(8,128)(2,1)S(1)}, bf16[1,32,1,128,128]{4,3,2,1,0:T(8,128)(2,1)}, u32[]{:S(2)}) copy-start(bf16[1,32,1,128,128]{4,3,2,1,0:T(8,128)(2,1)} %param.17) | copy-start | bytes 3145732
  1.8 12.2 %collective-permute-start = (bf16[512,256]{1,0:T(8,128)(2,1)S(1)}, bf16[512,256]{1,0:T(8,128)(2,1)S(1)}, u32[]{:S(2)}, u32[]{:S(2)}) collective-permute-start(bf16[512,256]{1,0:T(8,128)(2,1)S(1)} %convert_element_type.25.refs_0_), channel_id=1, source_target_pairs={{0,16},{8,24},{16,32},{24,40},{32,48},{40,56},{48,64},{56,72},{64,... | collective-permute-start | bytes 786440 | tf_op jit(solution)/shard_map/ppermute | solution.py:407
  3.8 10.2 %collective-permute-start.1 = (bf16[512,256]{1,0:T(8,128)(2,1)S(1)}, bf16[512,256]{1,0:T(8,128)(2,1)S(1)}, u32[]{:S(2)}, u32[]{:S(2)}) collective-permute-start(bf16[512,256]{1,0:T(8,128)(2,1)S(1)} %convert_element_type.25.refs_0_), channel_id=1, source_target_pairs={{0,112},{8,120},{16,0},{24,8},{32,16},{40,24},{48,32},{56,40},{64,... | collective-permute-start | bytes 786440 | tf_op jit(solution)/shard_map/ppermute | solution.py:407
  14.1 8.7 %collective-permute-start.2 = (bf16[512,256]{1,0:T(8,128)(2,1)S(1)}, bf16[512,256]{1,0:T(8,128)(2,1)S(1)}, u32[]{:S(2)}, u32[]{:S(2)}) collective-permute-start(bf16[512,256]{1,0:T(8,128)(2,1)S(1)} %collective-permute-done.refs_1_), channel_id=1, source_target_pairs={{0,16},{8,24},{16,32},{24,40},{32,48},{40,56},{48,64},{56,72},{64,... | collective-permute-start | bytes 786440 | tf_op jit(solution)/shard_map/ppermute | solution.py:407
  14.1 8.7 %collective-permute-start.3 = (bf16[512,256]{1,0:T(8,128)(2,1)S(1)}, bf16[512,256]{1,0:T(8,128)(2,1)S(1)}, u32[]{:S(2)}, u32[]{:S(2)}) collective-permute-start(bf16[512,256]{1,0:T(8,128)(2,1)S(1)} %collective-permute-done.1.refs_2_), channel_id=1, source_target_pairs={{0,112},{8,120},{16,0},{24,8},{32,16},{40,24},{48,32},{56,40},{64,... | collective-permute-start | bytes 786440 | tf_op jit(solution)/shard_map/ppermute | solution.py:407
  18.0 1.9 collective-permute-start.8
  18.0 3.6 %collective-permute-start.9 = (s32[8,32]{1,0:T(8,128)S(1)}, s32[8,32]{1,0:T(8,128)S(1)}, u32[]{:S(2)}, u32[]{:S(2)}) collective-permute-start(s32[8,32]{1,0:T(8,128)S(1)} %broadcast_in_dim.2), channel_id=1, source_target_pairs={{0,128},{8,136},{16,144},{24,152},{32,160},{40,168},{48,176},{56,1... | collective-permute-start | bytes 3080 | tf_op jit(solution)/shard_map/ppermute | solution.py:318
  19.6 3.0 %collective-permute-start.10 = (s32[8,32]{1,0:T(8,128)S(1)}, s32[8,32]{1,0:T(8,128)S(1)}, u32[]{:S(2)}, u32[]{:S(2)}) collective-permute-start(s32[8,32]{1,0:T(8,128)S(1)} %broadcast_in_dim.2), channel_id=1, source_target_pairs={{0,136},{8,128},{16,152},{24,144},{32,168},{40,160},{48,184},{56,1... | collective-permute-start | bytes 3080 | tf_op jit(solution)/shard_map/ppermute | solution.py:318
  19.9 207.7 %copy-start.28 = (s32[1,32]{1,0:T(1,128)}, s32[1,32]{1,0:T(1,128)S(1)}, u32[]{:S(2)}) copy-start(s32[1,32]{1,0:T(1,128)S(1)} %slice.34) | copy-start | bytes 388
  21.6 200.1 %copy-start.29 = (s32[1,32]{1,0:T(1,128)}, s32[1,32]{1,0:T(1,128)S(1)}, u32[]{:S(2)}) copy-start(s32[1,32]{1,0:T(1,128)S(1)} %slice.35) | copy-start | bytes 388
  22.6 195.4 %copy-start.30 = (s32[1,32]{1,0:T(1,128)}, s32[1,32]{1,0:T(1,128)S(1)}, u32[]{:S(2)}) copy-start(s32[1,32]{1,0:T(1,128)S(1)} %slice.36) | copy-start | bytes 388
  22.8 9.6 %collective-permute-start.4 = (bf16[512,256]{1,0:T(8,128)(2,1)S(1)}, bf16[512,256]{1,0:T(8,128)(2,1)S(1)}, u32[]{:S(2)}, u32[]{:S(2)}) collective-permute-start(bf16[512,256]{1,0:T(8,128)(2,1)S(1)} %collective-permute-done.2.refs_0_.refs_3_), channel_id=1, source_target_pairs={{0,16},{8,24},{16,32},{24,40},{32,48},{40,56},{48,64},{56,72},{64,... | collective-permute-start | bytes 786440 | tf_op jit(solution)/shard_map/ppermute | solution.py:407
  22.8 9.6 %collective-permute-start.5 = (bf16[512,256]{1,0:T(8,128)(2,1)S(1)}, bf16[512,256]{1,0:T(8,128)(2,1)S(1)}, u32[]{:S(2)}, u32[]{:S(2)}) collective-permute-start(bf16[512,256]{1,0:T(8,128)(2,1)S(1)} %collective-permute-done.3.refs_1_.refs_4_), channel_id=1, source_target_pairs={{0,112},{8,120},{16,0},{24,8},{32,16},{40,24},{48,32},{56,40},{64,... | collective-permute-start | bytes 786440 | tf_op jit(solution)/shard_map/ppermute | solution.py:407
  26.6 5.9 %collective-permute-start.11 = (bf16[3,128,256]{2,1,0:T(8,128)(2,1)S(1)}, bf16[3,128,256]{2,1,0:T(8,128)(2,1)S(1)}, u32[]{:S(2)}, u32[]{:S(2)}) collective-permute-start(bf16[3,128,256]{2,1,0:T(8,128)(2,1)S(1)} %get-tuple-element.18), channel_id=1, source_target_pairs={{0,8},{8,0},{16,24},{24,16},{32,40},{40,32},{48,56},{56,48},{64,72... | collective-permute-start | bytes 589832 | tf_op jit(solution)/shard_map/ppermute | solution.py:318
  26.7 9.8 %collective-permute-start.12 = (bf16[3,128,256]{2,1,0:T(8,128)(2,1)S(1)}, bf16[3,128,256]{2,1,0:T(8,128)(2,1)S(1)}, u32[]{:S(2)}, u32[]{:S(2)}) collective-permute-start(bf16[3,128,256]{2,1,0:T(8,128)(2,1)S(1)} %get-tuple-element.19), channel_id=1, source_target_pairs={{0,128},{8,136},{16,144},{24,152},{32,160},{40,168},{48,176},{56,1... | collective-permute-start | bytes 589832 | tf_op jit(solution)/shard_map/ppermute | solution.py:318
  28.4 9.3 %collective-permute-start.13 = (bf16[3,128,256]{2,1,0:T(8,128)(2,1)S(1)}, bf16[3,128,256]{2,1,0:T(8,128)(2,1)S(1)}, u32[]{:S(2)}, u32[]{:S(2)}) collective-permute-start(bf16[3,128,256]{2,1,0:T(8,128)(2,1)S(1)} %get-tuple-element.20), channel_id=1, source_target_pairs={{0,136},{8,128},{16,152},{24,144},{32,168},{40,160},{48,184},{56,1... | collective-permute-start | bytes 589832 | tf_op jit(solution)/shard_map/ppermute | solution.py:318
  32.4 7.2 %collective-permute-start.14 = (bf16[2,128,256]{2,1,0:T(8,128)(2,1)S(1)}, bf16[2,128,256]{2,1,0:T(8,128)(2,1)S(1)}, u32[]{:S(2)}, u32[]{:S(2)}) collective-permute-start(bf16[2,128,256]{2,1,0:T(8,128)(2,1)S(1)} %get-tuple-element.21), channel_id=1, source_target_pairs={{0,8},{8,0},{16,24},{24,16},{32,40},{40,32},{48,56},{56,48},{64,72... | collective-permute-start | bytes 393224 | tf_op jit(solution)/shard_map/ppermute | solution.py:318
  32.4 7.2 %collective-permute-start.6 = (bf16[256,256]{1,0:T(8,128)(2,1)S(1)}, bf16[256,256]{1,0:T(8,128)(2,1)S(1)}, u32[]{:S(2)}, u32[]{:S(2)}) collective-permute-start(bf16[256,256]{1,0:T(8,128)(2,1)S(1)} %slice.41), channel_id=1, source_target_pairs={{0,16},{8,24},{16,32},{24,40},{32,48},{40,56},{48,64},{56,72},{64,... | collective-permute-start | bytes 393224 | tf_op jit(solution)/shard_map/ppermute | solution.py:407
  32.5 8.1 %collective-permute-start.7 = (bf16[256,256]{1,0:T(8,128)(2,1)S(1)}, bf16[256,256]{1,0:T(8,128)(2,1)S(1)}, u32[]{:S(2)}, u32[]{:S(2)}) collective-permute-start(bf16[256,256]{1,0:T(8,128)(2,1)S(1)} %slice.42), channel_id=1, source_target_pairs={{0,112},{8,120},{16,0},{24,8},{32,16},{40,24},{48,32},{56,40},{64,... | collective-permute-start | bytes 393224 | tf_op jit(solution)/shard_map/ppermute | solution.py:407
  36.5 6.5 %collective-permute-start.15 = (bf16[2,128,256]{2,1,0:T(8,128)(2,1)S(1)}, bf16[2,128,256]{2,1,0:T(8,128)(2,1)S(1)}, u32[]{:S(2)}, u32[]{:S(2)}) collective-permute-start(bf16[2,128,256]{2,1,0:T(8,128)(2,1)S(1)} %get-tuple-element.22), channel_id=1, source_target_pairs={{0,128},{8,136},{16,144},{24,152},{32,160},{40,168},{48,176},{56,1... | collective-permute-start | bytes 393224 | tf_op jit(solution)/shard_map/ppermute | solution.py:318
  37.7 6.0 %collective-permute-start.16 = (bf16[2,128,256]{2,1,0:T(8,128)(2,1)S(1)}, bf16[2,128,256]{2,1,0:T(8,128)(2,1)S(1)}, u32[]{:S(2)}, u32[]{:S(2)}) collective-permute-start(bf16[2,128,256]{2,1,0:T(8,128)(2,1)S(1)} %get-tuple-element.23), channel_id=1, source_target_pairs={{0,136},{8,128},{16,152},{24,144},{32,168},{40,160},{48,184},{56,1... | collective-permute-start | bytes 393224 | tf_op jit(solution)/shard_map/ppermute | solution.py:318
  39.6 5.7 %collective-permute-start.17 = (bf16[2,128,256]{2,1,0:T(8,128)(2,1)S(1)}, bf16[2,128,256]{2,1,0:T(8,128)(2,1)S(1)}, u32[]{:S(2)}, u32[]{:S(2)}) collective-permute-start(bf16[2,128,256]{2,1,0:T(8,128)(2,1)S(1)} %get-tuple-element.24), channel_id=1, source_target_pairs={{0,8},{8,0},{16,24},{24,16},{32,40},{40,32},{48,56},{56,48},{64,72... | collective-permute-start | bytes 393224 | tf_op jit(solution)/shard_map/ppermute | solution.py:318
  39.6 9.0 %collective-permute-start.18 = (bf16[2,128,256]{2,1,0:T(8,128)(2,1)S(1)}, bf16[2,128,256]{2,1,0:T(8,128)(2,1)S(1)}, u32[]{:S(2)}, u32[]{:S(2)}) collective-permute-start(bf16[2,128,256]{2,1,0:T(8,128)(2,1)S(1)} %get-tuple-element.25), channel_id=1, source_target_pairs={{0,128},{8,136},{16,144},{24,152},{32,160},{40,168},{48,176},{56,1... | collective-permute-start | bytes 393224 | tf_op jit(solution)/shard_map/ppermute | solution.py:318
  40.6 8.8 %collective-permute-start.19 = (bf16[2,128,256]{2,1,0:T(8,128)(2,1)S(1)}, bf16[2,128,256]{2,1,0:T(8,128)(2,1)S(1)}, u32[]{:S(2)}, u32[]{:S(2)}) collective-permute-start(bf16[2,128,256]{2,1,0:T(8,128)(2,1)S(1)} %get-tuple-element.26), channel_id=1, source_target_pairs={{0,136},{8,128},{16,152},{24,144},{32,168},{40,160},{48,184},{56,1... | collective-permute-start | bytes 393224 | tf_op jit(solution)/shard_map/ppermute | solution.py:318
  43.0 6.4 %collective-permute-start.20 = (bf16[1,128,256]{2,1,0:T(8,128)(2,1)S(1)}, bf16[1,128,256]{2,1,0:T(8,128)(2,1)S(1)}, u32[]{:S(2)}, u32[]{:S(2)}) collective-permute-start(bf16[1,128,256]{2,1,0:T(8,128)(2,1)S(1)} %get-tuple-element.27), channel_id=1, source_target_pairs={{0,8},{8,0},{16,24},{24,16},{32,40},{40,32},{48,56},{56,48},{64,72... | collective-permute-start | bytes 196616 | tf_op jit(solution)/shard_map/ppermute | solution.py:318
  43.7 8.7 %collective-permute-start.21 = (bf16[1,128,256]{2,1,0:T(8,128)(2,1)S(1)}, bf16[1,128,256]{2,1,0:T(8,128)(2,1)S(1)}, u32[]{:S(2)}, u32[]{:S(2)}) collective-permute-start(bf16[1,128,256]{2,1,0:T(8,128)(2,1)S(1)} %get-tuple-element.28), channel_id=1, source_target_pairs={{0,128},{8,136},{16,144},{24,152},{32,160},{40,168},{48,176},{56,1... | collective-permute-start | bytes 196616 | tf_op jit(solution)/shard_map/ppermute | solution.py:318
  45.3 7.2 %collective-permute-start.22 = (bf16[1,128,256]{2,1,0:T(8,128)(2,1)S(1)}, bf16[1,128,256]{2,1,0:T(8,128)(2,1)S(1)}, u32[]{:S(2)}, u32[]{:S(2)}) collective-permute-start(bf16[1,128,256]{2,1,0:T(8,128)(2,1)S(1)} %get-tuple-element.29), channel_id=1, source_target_pairs={{0,136},{8,128},{16,152},{24,144},{32,168},{40,160},{48,184},{56,1... | collective-permute-start | bytes 196616 | tf_op jit(solution)/shard_map/ppermute | solution.py:318
  47.1 9.8 %copy-start.23 = (s32[16]{0:T(128)}, s32[16]{0:T(128)S(1)}, u32[]{:S(2)}) copy-start(s32[16]{0:T(128)S(1)} %convert_reduce_fusion.nrow_ref) | copy-start | bytes 196
  56.9 35.5 %copy-start.14 = (bf16[512,256]{1,0:T(8,128)(2,1)S(1)}, bf16[512,256]{1,0:T(8,128)(2,1)}, u32[]{:S(2)}) copy-start(bf16[512,256]{1,0:T(8,128)(2,1)} %ct_ref.1) | copy-start | bytes 786436
  56.9 35.5 %copy-start.16 = (bf16[256,256]{1,0:T(8,128)(2,1)S(1)}, bf16[256,256]{1,0:T(8,128)(2,1)}, u32[]{:S(2)}) copy-start(bf16[256,256]{1,0:T(8,128)(2,1)} %w_ref.1) | copy-start | bytes 393220
  56.9 35.5 %copy-start.25 = (f32[256]{0:T(256)S(1)}, f32[256]{0:T(256)}, u32[]{:S(2)}) copy-start(f32[256]{0:T(256)} %param.12) | copy-start | bytes 3076
  94.2 18.2 %copy-start.15 = (f32[256,256]{1,0:T(8,128)}, f32[256,256]{1,0:T(8,128)S(1)}, u32[]{:S(2)}) copy-start(f32[256,256]{1,0:T(8,128)S(1)} %get-tuple-element.32) | copy-start | bytes 786436
  94.2 27.0 %copy-start.4 = (bf16[512,256]{1,0:T(8,128)(2,1)}, bf16[512,256]{1,0:T(8,128)(2,1)S(1)}, u32[]{:S(2)}) copy-start(bf16[512,256]{1,0:T(8,128)(2,1)S(1)} %get-tuple-element.31.refs_0_) | copy-start | bytes 786436
  94.2 8.8 %collective-permute-start.30 = (bf16[512,256]{1,0:T(8,128)(2,1)S(1)}, bf16[512,256]{1,0:T(8,128)(2,1)S(1)}, u32[]{:S(2)}, u32[]{:S(2)}) collective-permute-start(bf16[512,256]{1,0:T(8,128)(2,1)S(1)} %get-tuple-element.31.refs_0_), channel_id=1, source_target_pairs={{0,4},{1,5},{2,6},{3,7},{4,0},{5,1},{6,2},{7,3},{8,12},{9,13},{10,... | collective-permute-start | bytes 786440 | tf_op jit(solution)/shard_map/ppermute | solution.py:318
  94.7 10.3 %collective-permute-start.26 = (bf16[512,256]{1,0:T(8,128)(2,1)S(1)}, bf16[512,256]{1,0:T(8,128)(2,1)S(1)}, u32[]{:S(2)}, u32[]{:S(2)}) collective-permute-start(bf16[512,256]{1,0:T(8,128)(2,1)S(1)} %get-tuple-element.31.refs_0_), channel_id=1, source_target_pairs={{0,1},{1,2},{2,3},{3,0},{4,5},{5,6},{6,7},{7,4},{8,9},{9,10},{10,1... | collective-permute-start | bytes 786440 | tf_op jit(solution)/shard_map/ppermute | solution.py:329
  94.7 10.8 %collective-permute-start.27 = (bf16[512,256]{1,0:T(8,128)(2,1)S(1)}, bf16[512,256]{1,0:T(8,128)(2,1)S(1)}, u32[]{:S(2)}, u32[]{:S(2)}) collective-permute-start(bf16[512,256]{1,0:T(8,128)(2,1)S(1)} %get-tuple-element.31.refs_0_), channel_id=1, source_target_pairs={{0,3},{1,0},{2,1},{3,2},{4,7},{5,4},{6,5},{7,6},{8,11},{9,8},{10,9... | collective-permute-start | bytes 786440 | tf_op jit(solution)/shard_map/ppermute | solution.py:329
  103.0 18.2 %copy-start.6 = (bf16[512,256]{1,0:T(8,128)(2,1)}, bf16[512,256]{1,0:T(8,128)(2,1)S(1)}, u32[]{:S(2)}) copy-start(bf16[512,256]{1,0:T(8,128)(2,1)S(1)} %collective-permute-done.30.refs_5_) | copy-start | bytes 786436
  103.0 8.5 %collective-permute-start.31 = (bf16[512,256]{1,0:T(8,128)(2,1)S(1)}, bf16[512,256]{1,0:T(8,128)(2,1)S(1)}, u32[]{:S(2)}, u32[]{:S(2)}) collective-permute-start(bf16[512,256]{1,0:T(8,128)(2,1)S(1)} %collective-permute-done.30.refs_5_), channel_id=1, source_target_pairs={{0,1},{1,2},{2,3},{3,0},{4,5},{5,6},{6,7},{7,4},{8,9},{9,10},{10,1... | collective-permute-start | bytes 786440 | tf_op jit(solution)/shard_map/ppermute | solution.py:329
  103.4 9.0 %collective-permute-start.32 = (bf16[512,256]{1,0:T(8,128)(2,1)S(1)}, bf16[512,256]{1,0:T(8,128)(2,1)S(1)}, u32[]{:S(2)}, u32[]{:S(2)}) collective-permute-start(bf16[512,256]{1,0:T(8,128)(2,1)S(1)} %collective-permute-done.30.refs_5_), channel_id=1, source_target_pairs={{0,3},{1,0},{2,1},{3,2},{4,7},{5,4},{6,5},{7,6},{8,11},{9,8},{10,9... | collective-permute-start | bytes 786440 | tf_op jit(solution)/shard_map/ppermute | solution.py:329
  105.0 10.9 %collective-permute-start.28 = (bf16[256,256]{1,0:T(8,128)(2,1)S(1)}, bf16[256,256]{1,0:T(8,128)(2,1)S(1)}, u32[]{:S(2)}, u32[]{:S(2)}) collective-permute-start(bf16[256,256]{1,0:T(8,128)(2,1)S(1)} %slice.43), channel_id=1, source_target_pairs={{0,1},{1,2},{2,3},{3,0},{4,5},{5,6},{6,7},{7,4},{8,9},{9,10},{10,1... | collective-permute-start | bytes 393224 | tf_op jit(solution)/shard_map/ppermute | solution.py:329
  106.2 9.8 %collective-permute-start.29 = (bf16[256,256]{1,0:T(8,128)(2,1)}, bf16[256,256]{1,0:T(8,128)(2,1)S(1)}, u32[]{:S(2)}, u32[]{:S(2)}) collective-permute-start(bf16[256,256]{1,0:T(8,128)(2,1)} %slice.44), channel_id=1, source_target_pairs={{0,3},{1,0},{2,1},{3,2},{4,7},{5,4},{6,5},{7,6},{8,11},{9,8},{10,9... | collective-permute-start | bytes 393224 | tf_op jit(solution)/shard_map/ppermute | solution.py:329
  112.2 6.1 %collective-permute-start.33 = (bf16[256,256]{1,0:T(8,128)(2,1)}, bf16[256,256]{1,0:T(8,128)(2,1)S(1)}, u32[]{:S(2)}, u32[]{:S(2)}) collective-permute-start(bf16[256,256]{1,0:T(8,128)(2,1)} %slice.45), channel_id=1, source_target_pairs={{0,1},{1,2},{2,3},{3,0},{4,5},{5,6},{6,7},{7,4},{8,9},{9,10},{10,1... | collective-permute-start | bytes 393224 | tf_op jit(solution)/shard_map/ppermute | solution.py:329
  112.3 8.8 %copy-start.2 = (bf16[512,256]{1,0:T(8,128)(2,1)}, bf16[512,256]{1,0:T(8,128)(2,1)S(1)}, u32[]{:S(2)}) copy-start(bf16[512,256]{1,0:T(8,128)(2,1)S(1)} %collective-permute-done.32.refs_7_) | copy-start | bytes 786436
  113.0 5.6 %collective-permute-start.34 = (bf16[256,256]{1,0:T(8,128)(2,1)}, bf16[256,256]{1,0:T(8,128)(2,1)S(1)}, u32[]{:S(2)}, u32[]{:S(2)}) collective-permute-start(bf16[256,256]{1,0:T(8,128)(2,1)} %slice.46), channel_id=1, source_target_pairs={{0,3},{1,0},{2,1},{3,2},{4,7},{5,4},{6,5},{7,6},{8,11},{9,8},{10,9... | collective-permute-start | bytes 393224 | tf_op jit(solution)/shard_map/ppermute | solution.py:329
  115.9 5.3 %copy-start.18 = (s32[8]{0:T(128)}, s32[8]{0:T(128)S(1)}, u32[]{:S(2)}) copy-start(s32[8]{0:T(128)S(1)} %stack.55.owner_ref) | copy-start | bytes 100
  121.2 129.4 %all-to-all-start.1 = ((bf16[32,128,256]{2,1,0:T(8,128)(2,1)}), bf16[32,128,256]{2,1,0:T(8,128)(2,1)S(1)}, u32[]{:S(2)}, u32[]{:S(2)}) async-start(bf16[32,128,256]{2,1,0:T(8,128)(2,1)} %far_terms.1), calls=%async_computation.1 | async-start | bytes 4194304 | tf_op jit(solution)/shard_map/all_to_all | solution.py:371
  127.0 112.5 %copy-start.1 = (bf16[16,128,128]{2,1,0:T(8,128)(2,1)S(1)}, bf16[16,128,128]{2,1,0:T(8,128)(2,1)}, u32[]{:S(2)}) copy-start(bf16[16,128,128]{2,1,0:T(8,128)(2,1)} %refs_10_.1) | copy-start | bytes 1572868
  128.6 1.7 collective-permute-start.35
  131.3 50.2 %collective-permute-start.36 = (bf16[128,256]{1,0:T(8,128)(2,1)S(1)}, bf16[128,256]{1,0:T(8,128)(2,1)S(1)}, u32[]{:S(2)}, u32[]{:S(2)}) collective-permute-start(bf16[128,256]{1,0:T(8,128)(2,1)S(1)} %get-tuple-element.33), channel_id=1, source_target_pairs={{0,64},{8,72},{16,80},{24,88},{32,96},{40,104},{48,112},{56,120},{... | collective-permute-start | bytes 196616 | tf_op jit(solution)/shard_map/ppermute | solution.py:318
  181.5 6.1 %collective-permute-start.37 = (bf16[128,256]{1,0:T(8,128)(2,1)S(1)}, bf16[128,256]{1,0:T(8,128)(2,1)S(1)}, u32[]{:S(2)}, u32[]{:S(2)}) collective-permute-start(bf16[128,256]{1,0:T(8,128)(2,1)S(1)} %fusion), channel_id=1, source_target_pairs={{0,32},{8,40},{16,48},{24,56},{32,0},{40,8},{48,16},{56,24},{64,96... | collective-permute-start | bytes 196616 | tf_op jit(solution)/shard_map/ppermute | solution.py:318
  187.6 4.4 %collective-permute-start.38 = (bf16[128,256]{1,0:T(8,128)(2,1)S(1)}, bf16[128,256]{1,0:T(8,128)(2,1)S(1)}, u32[]{:S(2)}, u32[]{:S(2)}) collective-permute-start(bf16[128,256]{1,0:T(8,128)(2,1)S(1)} %fusion.1), channel_id=1, source_target_pairs={{0,16},{8,24},{16,0},{24,8},{32,48},{40,56},{48,32},{56,40},{64,80... | collective-permute-start | bytes 196616 | tf_op jit(solution)/shard_map/ppermute | solution.py:318
  192.0 6.2 %collective-permute-start.39 = (f32[128,256]{1,0:T(8,128)S(1)}, f32[128,256]{1,0:T(8,128)S(1)}, u32[]{:S(2)}, u32[]{:S(2)}) collective-permute-start(f32[128,256]{1,0:T(8,128)S(1)} %convert_add_fusion), channel_id=1, source_target_pairs={{0,1},{1,0},{2,3},{3,2},{4,5},{5,4},{6,7},{7,6},{8,9},{9,8},{10,11... | collective-permute-start | bytes 393224 | tf_op jit(solution)/shard_map/ppermute | solution.py:318
  198.3 7.4 %collective-permute-start.40 = (f32[128,256]{1,0:T(8,128)S(1)}, f32[128,256]{1,0:T(8,128)S(1)}, u32[]{:S(2)}, u32[]{:S(2)}) collective-permute-start(f32[128,256]{1,0:T(8,128)S(1)} %add.120), channel_id=1, source_target_pairs={{0,2},{1,3},{2,0},{3,1},{4,6},{5,7},{6,4},{7,5},{8,10},{9,11},{10,... | collective-permute-start | bytes 393224 | tf_op jit(solution)/shard_map/ppermute | solution.py:318
  205.7 5.1 %collective-permute-start.41 = (f32[128,256]{1,0:T(8,128)S(1)}, f32[128,256]{1,0:T(8,128)S(1)}, u32[]{:S(2)}, u32[]{:S(2)}) collective-permute-start(f32[128,256]{1,0:T(8,128)S(1)} %add.121), channel_id=1, source_target_pairs={{0,128},{8,136},{16,144},{24,152},{32,160},{40,168},{48,176},{56,1... | collective-permute-start | bytes 393224 | tf_op jit(solution)/shard_map/ppermute | solution.py:318
  210.8 6.6 %collective-permute-start.42 = (f32[128,256]{1,0:T(8,128)S(1)}, f32[128,256]{1,0:T(8,128)S(1)}, u32[]{:S(2)}, u32[]{:S(2)}) collective-permute-start(f32[128,256]{1,0:T(8,128)S(1)} %add.122), channel_id=1, source_target_pairs={{0,4},{1,5},{2,6},{3,7},{4,0},{5,1},{6,2},{7,3},{8,12},{9,13},{10,... | collective-permute-start | bytes 393224 | tf_op jit(solution)/shard_map/ppermute | solution.py:318
  218.0 30.9 %collective-permute-start.43 = (f32[128,256]{1,0:T(8,128)}, f32[128,256]{1,0:T(8,128)}, u32[]{:S(2)}, u32[]{:S(2)}) collective-permute-start(f32[128,256]{1,0:T(8,128)} %add_multiply_fusion), channel_id=1, source_target_pairs={{0,8},{8,0},{16,24},{24,16},{32,40},{40,32},{48,56},{56,48},{64,72... | collective-permute-start | bytes 393224 | tf_op jit(solution)/shard_map/ppermute | solution.py:318
  218.0 3.7 %collective-permute-start.23 = (s32[4,32]{1,0:T(4,128)S(1)}, s32[4,32]{1,0:T(4,128)S(1)}, u32[]{:S(2)}, u32[]{:S(2)}) collective-permute-start(s32[4,32]{1,0:T(4,128)S(1)} %pad_add_fusion.1), channel_id=1, source_target_pairs={{0,16},{8,24},{16,0},{24,8},{32,48},{40,56},{48,32},{56,40},{64,80... | collective-permute-start | bytes 1544 | tf_op jit(solution)/shard_map/ppermute | solution.py:318
  221.7 8.6 %copy-start.26 = (s32[4,32]{1,0:T(4,128)}, s32[4,32]{1,0:T(4,128)S(1)}, u32[]{:S(2)}) copy-start(s32[4,32]{1,0:T(4,128)S(1)} %collective-permute-done.23) | copy-start | bytes 1540
  222.9 4.7 %collective-permute-start.24 = (s32[8,32]{1,0:T(8,128)}, s32[8,32]{1,0:T(8,128)S(1)}, u32[]{:S(2)}, u32[]{:S(2)}) collective-permute-start(s32[8,32]{1,0:T(8,128)} %concatenate.24), channel_id=1, source_target_pairs={{0,32},{8,40},{16,48},{24,56},{32,0},{40,8},{48,16},{56,24},{64,96... | collective-permute-start | bytes 3080 | tf_op jit(solution)/shard_map/ppermute | solution.py:318
  229.5 7.9 %collective-permute-start.25 = (s32[16,32]{1,0:T(8,128)}, s32[16,32]{1,0:T(8,128)}, u32[]{:S(2)}, u32[]{:S(2)}) collective-permute-start(s32[16,32]{1,0:T(8,128)} %concatenate.25), channel_id=1, source_target_pairs={{0,64},{8,72},{16,80},{24,88},{32,96},{40,104},{48,112},{56,120},{... | collective-permute-start | bytes 6152 | tf_op jit(solution)/shard_map/ppermute | solution.py:318
  (13 other events, 20.9 us)
